TPU v7x, 32 devices: a whole 2x2x4 slice. The times are simulated.
32 devices in a mesh: dp: 8 (over y, x, core), tensor: 4 (over z).
Axes of the slice: x: 2, y: 2, z: 4, core: 2. Of those that a mesh axis runs over, the one named last changes fastest.
Arguments:
- inputs: bfloat16 [2, 8, 512, 1024], P(None, 'dp', 'tensor'), may hold values from -6 to 6
- lengths: int32 [2, 8], P(None, 'dp'), may hold values from 1 to 512, 2560 in all within a row
- cotangent: bfloat16 [2, 8, 512, 1024], P(None, 'dp', 'tensor'), may hold values from -6 to 6
- first_expand: bfloat16 [1024, 4096], P('dp', 'tensor'), may hold values from -0.1875 to 0.1875
- first_reduce: bfloat16 [1024, 4096], P('dp', 'tensor'), may hold values from -0.09375 to 0.09375
- heads_project: bfloat16 [1024, 3, 1024], P('dp', None, 'tensor'), may hold values from -0.1875 to 0.1875
- heads_merge: bfloat16 [1024, 1024], P('dp', 'tensor'), may hold values from -0.75 to 0.75
- filter_expand: bfloat16 [1024, 2, 1024], P('dp', None, 'tensor'), may hold values from -0.1875 to 0.1875
- filter_reduce: bfloat16 [1024, 1024], P('dp', 'tensor'), may hold values from -0.1875 to 0.1875
- second_expand: bfloat16 [1024, 4096], P('dp', 'tensor'), may hold values from -0.1875 to 0.1875
- second_reduce: bfloat16 [1024, 4096], P('dp', 'tensor'), may hold values from -0.09375 to 0.09375
- norm_gains: bfloat16 [6, 1024], replicated, may hold values from 0.25 to 1.75
- biases: bfloat16 [19, 1024], replicated, may hold values from -3 to 3
- kernel: bfloat16 [31, 1024], replicated, may hold values from -1 to 1
- distance_table: bfloat16 [73, 64], replicated, may hold values from -6 to 6
Outputs:
- outputs: bfloat16 [2, 8, 512, 1024], P(None, 'dp', 'tensor')
- input_grad: float32 [2, 8, 512, 1024], P(None, 'dp', 'tensor')
- first_expand_grad: float32 [1024, 4096], P('dp', 'tensor')
- first_reduce_grad: float32 [1024, 4096], P('dp', 'tensor')
- heads_project_grad: float32 [1024, 3, 1024], P('dp', None, 'tensor')
- heads_merge_grad: float32 [1024, 1024], P('dp', 'tensor')
- filter_expand_grad: float32 [1024, 2, 1024], P('dp', None, 'tensor')
- filter_reduce_grad: float32 [1024, 1024], P('dp', 'tensor')
- second_expand_grad: float32 [1024, 4096], P('dp', 'tensor')
- second_reduce_grad: float32 [1024, 4096], P('dp', 'tensor')
- norm_gains_grad: float32 [6, 1024], replicated
- biases_grad: float32 [19, 1024], replicated
- kernel_grad: float32 [31, 1024], replicated
- distance_table_grad: float32 [73, 64], replicated
Inputs may be any that keep to these rules, and one draw needn't show every extreme that they name: In each micro-batch the clip lengths sum to 2560, and some clip has 512 live tokens.
All inputs are finite; a program needn't handle non-finite values. No bound on the sum of `lengths` on one device may be relied on, other than what follows from the above.
Results may differ from a plain program's by a relative error of at most 0.025.
Values may be sent and summed in bfloat16 or wider, within the bound.
No kernel may reach another device: no remote copies, remote signals or barrier semaphores. Data moves between devices by JAX's collectives and lax.ppermute only.
A program may use at most 256 MiB of HBM per device.

v0:
```python
import jax
import jax.numpy as jnp
from jax import lax
from jax.sharding import PartitionSpec as P

D = 1024
HD = 64
FF = 4096
LEFT = 64
RIGHT = 8


EPSILON = 1e-05
MASKED = -1e30
WIDE_TYPE = jnp.float32
NARROW_TYPE = jnp.bfloat16
HIGHEST = lax.Precision.HIGHEST


def contract_rows(left_side, right_side):
    return lax.dot_general(
        left_side, right_side, (((0,), (0,)), ((), ())), preferred_element_type=WIDE_TYPE
    )


def contract_last(left_side, right_side):
    return lax.dot_general(
        left_side, right_side, (((1,), (1,)), ((), ())), preferred_element_type=WIDE_TYPE
    )


def swish_slope(pre_act):
    logistic = jax.nn.sigmoid(pre_act)
    return logistic * (1.0 + pre_act * (1.0 - logistic))


def row_norm(stream, gain_row, bias_row):
    center = stream - jnp.mean(stream, axis=-1, keepdims=True)
    inv_std = lax.rsqrt(jnp.mean(center * center, axis=-1, keepdims=True) + EPSILON)
    unit_rows = center * inv_std
    return (unit_rows * gain_row + bias_row, unit_rows, inv_std)


def row_norm_back(grad_out, unit_rows, inv_std, gain_row):
    scaled = grad_out * gain_row
    grad_in = inv_std * (
        scaled
        - jnp.mean(scaled, axis=-1, keepdims=True)
        - unit_rows * jnp.mean(scaled * unit_rows, axis=-1, keepdims=True)
    )
    return (grad_in, jnp.sum(grad_out * unit_rows, axis=0), jnp.sum(grad_out, axis=0))


def own_part(row_values, member, part_size):
    return lax.dynamic_slice_in_dim(row_values, member * part_size, part_size, 0)


def placed(piece_rows, member, full_size, along_axis):
    full_shape = list(piece_rows.shape)
    full_shape[along_axis] = full_size
    empty = jnp.zeros(tuple(full_shape), WIDE_TYPE)
    return lax.dynamic_update_slice_in_dim(
        empty, piece_rows, member * piece_rows.shape[along_axis], along_axis
    )


def split_heads(rows_in):
    return rows_in.reshape(rows_in.shape[0], -1, HD)


def spread_rows(rows_low):
    return lax.all_gather(rows_low, "tensor", axis=0, tiled=True)


def collect_rows(partial_value):
    return lax.psum_scatter(
        partial_value.astype(jnp.bfloat16), "tensor", scatter_dimension=0, tiled=True
    ).astype(jnp.float32)


def spread_grads(rows_low):
    return lax.all_gather(rows_low, "tensor", axis=0, tiled=True)


def collect_grads(partial_value):
    return lax.psum_scatter(
        partial_value.astype(jnp.bfloat16), "tensor", scatter_dimension=0, tiled=True
    ).astype(jnp.float32)


def fetch_layer(shards):
    return (
        lax.all_gather(shards[0], "dp", axis=0, tiled=True),
        lax.all_gather(shards[1], "dp", axis=0, tiled=True),
        lax.all_gather(shards[2], "dp", axis=0, tiled=True),
        lax.all_gather(shards[3], "dp", axis=0, tiled=True),
        lax.all_gather(shards[4], "dp", axis=0, tiled=True),
        lax.all_gather(shards[5], "dp", axis=0, tiled=True),
        lax.all_gather(shards[6], "dp", axis=0, tiled=True),
        lax.all_gather(shards[7], "dp", axis=0, tiled=True),
    )


def reduce_layer(grads):
    return (
        lax.psum_scatter(grads[0], "dp", scatter_dimension=0, tiled=True),
        lax.psum_scatter(grads[1], "dp", scatter_dimension=0, tiled=True),
        lax.psum_scatter(grads[2], "dp", scatter_dimension=0, tiled=True),
        lax.psum_scatter(grads[3], "dp", scatter_dimension=0, tiled=True),
        lax.psum_scatter(grads[4], "dp", scatter_dimension=0, tiled=True),
        lax.psum_scatter(grads[5], "dp", scatter_dimension=0, tiled=True),
        lax.psum_scatter(grads[6], "dp", scatter_dimension=0, tiled=True),
        lax.psum_scatter(grads[7], "dp", scatter_dimension=0, tiled=True),
    )


def feed_forward(stream, gain_row, bias_row, weights, hidden_bias, out_bias):
    expand, shrink = weights
    normed, unit_rows, inv_std = row_norm(stream, gain_row, bias_row)
    spread = spread_rows(normed.astype(NARROW_TYPE))
    hidden = jnp.dot(spread, expand, preferred_element_type=WIDE_TYPE) + hidden_bias
    active = (hidden * jax.nn.sigmoid(hidden)).astype(NARROW_TYPE)
    branch = collect_rows(contract_last(active, shrink))
    return (stream + 0.5 * (branch + out_bias), (unit_rows, inv_std, spread, hidden))


def feed_backward(grad_stream, stored, gain_row, weights):
    unit_rows, inv_std, spread, hidden = stored
    expand, shrink = weights
    branch_grad = 0.5 * grad_stream
    out_bias_grad = jnp.sum(branch_grad, axis=0)
    gathered = spread_grads(branch_grad.astype(NARROW_TYPE))
    active = (hidden * jax.nn.sigmoid(hidden)).astype(NARROW_TYPE)
    shrink_grad = contract_rows(gathered, active)
    hidden_grad = (
        jnp.dot(gathered, shrink, preferred_element_type=WIDE_TYPE) * swish_slope(hidden)
    ).astype(NARROW_TYPE)
    expand_grad = contract_rows(spread, hidden_grad)
    hidden_bias_grad = jnp.sum(hidden_grad, axis=0, dtype=WIDE_TYPE)
    normed_grad = collect_grads(contract_last(hidden_grad, expand))
    stream_grad, gain_grad, bias_grad = row_norm_back(normed_grad, unit_rows, inv_std, gain_row)
    return (
        grad_stream + stream_grad,
        (expand_grad, shrink_grad),
        gain_grad,
        bias_grad,
        hidden_bias_grad,
        out_bias_grad,
    )


def relative_band(near_scores):
    head_count = near_scores.shape[0]
    row_count = near_scores.shape[1]
    left_fill = jnp.broadcast_to(
        near_scores[:, :, :1], (head_count, row_count, row_count - 1 - LEFT)
    )
    right_fill = jnp.broadcast_to(
        near_scores[:, :, -1:], (head_count, row_count, row_count - 1 - RIGHT)
    )
    closing = jnp.zeros((head_count, row_count, 1), WIDE_TYPE)
    full_rows = jnp.concatenate([left_fill, near_scores, right_fill, closing], axis=2)
    flat_rows = full_rows.reshape(head_count, 2 * row_count * row_count)
    shifted = lax.slice_in_dim(
        flat_rows, row_count - 1, row_count - 1 + row_count * (2 * row_count - 1), axis=1
    )
    return shifted.reshape(head_count, row_count, 2 * row_count - 1)[:, :, :row_count]


def relative_back(scaled_grad):
    head_count = scaled_grad.shape[0]
    row_count = scaled_grad.shape[1]
    widened = jnp.pad(scaled_grad, ((0, 0), (0, 0), (0, row_count - 1)))
    flat_rows = widened.reshape(head_count, row_count * (2 * row_count - 1))
    flat_rows = jnp.pad(flat_rows, ((0, 0), (row_count - 1, 1)))
    diagonals = flat_rows.reshape(head_count, row_count, 2 * row_count)[:, :, : 2 * row_count - 1]
    left_end = row_count - 1 - LEFT
    right_start = row_count - 1 + RIGHT
    far_left = jnp.sum(diagonals[:, :, : left_end + 1], axis=2)
    far_right = jnp.sum(diagonals[:, :, right_start:], axis=2)
    return jnp.concatenate(
        [far_left[..., None], diagonals[:, :, left_end + 1 : right_start], far_right[..., None]],
        axis=2,
    )


def raw_scores(queries, key_rows, distance, key_live):
    query_heads = split_heads(queries)
    near_scores = jnp.einsum(
        "qhe,be->hqb", query_heads.astype(WIDE_TYPE), distance, precision=HIGHEST
    )
    relative = relative_band(near_scores)
    products = jnp.einsum(
        "qhe,khe->hqk", query_heads, split_heads(key_rows), preferred_element_type=WIDE_TYPE
    )
    scores = (products + relative) * HD ** (-0.5)
    return jnp.where(key_live[None, None, :], scores, MASKED)


def attention_forward(
    stream, gain_row, bias_row, weights, query_bias, value_bias, merge_bias, distance, key_live
):
    project, merge = weights
    normed, unit_rows, inv_std = row_norm(stream, gain_row, bias_row)
    spread = spread_rows(normed.astype(NARROW_TYPE))
    projected = jnp.einsum("nd,dke->nke", spread, project, preferred_element_type=WIDE_TYPE)
    queries = (projected[:, 0] + query_bias).astype(NARROW_TYPE)
    key_rows = projected[:, 1].astype(NARROW_TYPE)
    values = (projected[:, 2] + value_bias).astype(NARROW_TYPE)
    scores = raw_scores(queries, key_rows, distance, key_live)
    row_max = jnp.max(scores, axis=-1, keepdims=True)
    log_total = row_max + jnp.log(jnp.sum(jnp.exp(scores - row_max), axis=-1, keepdims=True))
    chances = jnp.exp(scores - log_total).astype(NARROW_TYPE)
    merged = jnp.einsum(
        "hqk,khe->qhe", chances, split_heads(values), preferred_element_type=WIDE_TYPE
    )
    merged = merged.reshape(merged.shape[0], -1).astype(NARROW_TYPE)
    branch = collect_rows(contract_last(merged, merge))
    stored = (unit_rows, inv_std, spread, queries, key_rows, values, merged, log_total)
    return (stream + branch + merge_bias, stored)


def attention_backward(grad_stream, stored, gain_row, weights, distance, key_live):
    unit_rows, inv_std, spread, queries, key_rows, values, merged, log_total = stored
    project, merge = weights
    row_count = spread.shape[0]
    merge_bias_grad = jnp.sum(grad_stream, axis=0)
    gathered = spread_grads(grad_stream.astype(NARROW_TYPE))
    merge_grad = contract_rows(gathered, merged)
    merged_grad = jnp.dot(gathered, merge, preferred_element_type=WIDE_TYPE).astype(NARROW_TYPE)
    scores = raw_scores(queries, key_rows, distance, key_live)
    chances = jnp.exp(scores - log_total)
    heads_grad = split_heads(merged_grad)
    chance_grad = jnp.einsum(
        "qhe,khe->hqk", heads_grad, split_heads(values), preferred_element_type=WIDE_TYPE
    )
    score_grad = (
        chances * (chance_grad - jnp.sum(chance_grad * chances, axis=-1, keepdims=True))
    ).astype(NARROW_TYPE)
    value_grad = jnp.einsum(
        "hqk,qhe->khe", chances.astype(NARROW_TYPE), heads_grad, preferred_element_type=WIDE_TYPE
    )
    score_scale = HD ** (-0.5)
    query_grad = (
        jnp.einsum(
            "hqk,khe->qhe", score_grad, split_heads(key_rows), preferred_element_type=WIDE_TYPE
        )
        * score_scale
    )
    key_grad = (
        jnp.einsum(
            "hqk,qhe->khe", score_grad, split_heads(queries), preferred_element_type=WIDE_TYPE
        )
        * score_scale
    )
    near_grad = relative_back(score_grad.astype(WIDE_TYPE) * score_scale)
    query_grad = query_grad + jnp.einsum("hqb,be->qhe", near_grad, distance, precision=HIGHEST)
    distance_grad = jnp.einsum(
        "hqb,qhe->be", near_grad, split_heads(queries).astype(WIDE_TYPE), precision=HIGHEST
    )
    projected_grad = jnp.stack(
        [
            query_grad.reshape(row_count, -1),
            key_grad.reshape(row_count, -1),
            value_grad.reshape(row_count, -1),
        ],
        axis=1,
    ).astype(NARROW_TYPE)
    project_grad = jnp.einsum(
        "nd,nke->dke", spread, projected_grad, preferred_element_type=WIDE_TYPE
    )
    normed_grad = collect_grads(
        jnp.einsum("nke,dke->nd", projected_grad, project, preferred_element_type=WIDE_TYPE)
    )
    stream_grad, gain_grad, bias_grad = row_norm_back(normed_grad, unit_rows, inv_std, gain_row)
    query_bias_grad = jnp.sum(projected_grad[:, 0], axis=0, dtype=WIDE_TYPE)
    value_bias_grad = jnp.sum(projected_grad[:, 2], axis=0, dtype=WIDE_TYPE)
    return (
        grad_stream + stream_grad,
        (project_grad, merge_grad),
        gain_grad,
        bias_grad,
        query_bias_grad,
        value_bias_grad,
        merge_bias_grad,
        distance_grad,
    )


def causal_mix(signal, kernel_rows):
    tap_count = kernel_rows.shape[0]
    row_count = signal.shape[0]
    padded = jnp.pad(signal, ((tap_count - 1, 0), (0, 0)))
    mixed_rows = jnp.zeros_like(signal)
    for tap_index in range(tap_count):
        mixed_rows = mixed_rows + kernel_rows[tap_index] * padded[tap_index : tap_index + row_count]
    return mixed_rows


def causal_back(mixed_grad, signal, kernel_rows):
    tap_count = kernel_rows.shape[0]
    row_count = signal.shape[0]
    padded = jnp.pad(signal, ((tap_count - 1, 0), (0, 0)))
    padded_grad = jnp.pad(mixed_grad, ((0, tap_count - 1), (0, 0)))
    signal_grad = jnp.zeros_like(signal)
    kernel_terms = []
    for tap_index in range(tap_count):
        begin = tap_count - 1 - tap_index
        signal_grad = signal_grad + kernel_rows[tap_index] * padded_grad[begin : begin + row_count]
        kernel_terms.append(jnp.sum(padded[tap_index : tap_index + row_count] * mixed_grad, axis=0))
    return (signal_grad, jnp.stack(kernel_terms))


def filter_forward(
    stream, gain_row, bias_row, weights, kernel_rows, depth_gain, depth_bias, model_width
):
    expand, shrink = weights
    normed, unit_rows, inv_std = row_norm(stream, gain_row, bias_row)
    spread = spread_rows(normed.astype(NARROW_TYPE))
    projected = jnp.einsum("nd,dke->nke", spread, expand, preferred_element_type=WIDE_TYPE)
    gated_rows = projected[:, 0] * jax.nn.sigmoid(projected[:, 1])
    mixed_rows = causal_mix(gated_rows, kernel_rows)
    moments = lax.psum(
        (jnp.sum(mixed_rows, axis=1), jnp.sum(mixed_rows * mixed_rows, axis=1)), "tensor"
    )
    mean_row = moments[0] / model_width
    channel_std = lax.rsqrt(moments[1] / model_width - mean_row * mean_row + EPSILON)[:, None]
    channel_unit = (mixed_rows - mean_row[:, None]) * channel_std
    normed_mix = channel_unit * depth_gain + depth_bias
    active = (normed_mix * jax.nn.sigmoid(normed_mix)).astype(NARROW_TYPE)
    branch = collect_rows(contract_last(active, shrink))
    return (
        stream + branch,
        (unit_rows, inv_std, spread, projected, gated_rows, channel_unit, channel_std),
    )


def filter_backward(
    grad_stream, stored, gain_row, weights, kernel_rows, depth_gain, depth_bias, model_width
):
    unit_rows, inv_std, spread, projected, gated_rows, channel_unit, channel_std = stored
    expand, shrink = weights
    gathered = spread_grads(grad_stream.astype(NARROW_TYPE))
    normed_mix = channel_unit * depth_gain + depth_bias
    active = (normed_mix * jax.nn.sigmoid(normed_mix)).astype(NARROW_TYPE)
    shrink_grad = contract_rows(gathered, active)
    mix_grad = jnp.dot(gathered, shrink, preferred_element_type=WIDE_TYPE) * swish_slope(normed_mix)
    depth_gain_grad = jnp.sum(mix_grad * channel_unit, axis=0)
    depth_bias_grad = jnp.sum(mix_grad, axis=0)
    scaled = mix_grad * depth_gain
    moments = lax.psum((jnp.sum(scaled, axis=1), jnp.sum(scaled * channel_unit, axis=1)), "tensor")
    mixed_grad = channel_std * (
        scaled
        - moments[0][:, None] / model_width
        - channel_unit * moments[1][:, None] / model_width
    )
    gated_grad, kernel_grad = causal_back(mixed_grad, gated_rows, kernel_rows)
    logistic = jax.nn.sigmoid(projected[:, 1])
    projected_grad = jnp.stack(
        [gated_grad * logistic, gated_grad * projected[:, 0] * logistic * (1.0 - logistic)], axis=1
    ).astype(NARROW_TYPE)
    expand_grad = jnp.einsum(
        "nd,nke->dke", spread, projected_grad, preferred_element_type=WIDE_TYPE
    )
    normed_grad = collect_grads(
        jnp.einsum("nke,dke->nd", projected_grad, expand, preferred_element_type=WIDE_TYPE)
    )
    stream_grad, gain_grad, bias_grad = row_norm_back(normed_grad, unit_rows, inv_std, gain_row)
    return (
        grad_stream + stream_grad,
        (expand_grad, shrink_grad),
        gain_grad,
        bias_grad,
        depth_gain_grad,
        depth_bias_grad,
        kernel_grad,
    )


def on_device(
    inputs,
    lengths,
    cotangent,
    first_expand,
    first_reduce,
    heads_project,
    heads_merge,
    filter_expand,
    filter_reduce,
    second_expand,
    second_reduce,
    norm_gains,
    biases,
    kernel,
    distance_table,
):
    batches = inputs.shape[0]
    rows_here = inputs.shape[2]
    model_width = inputs.shape[3]
    member = lax.axis_index("tensor")
    length_full = rows_here * lax.axis_size("tensor")
    hidden_here = first_expand.shape[1]
    heads_width = heads_project.shape[2]
    channels = filter_expand.shape[2]
    stride = FF // D
    shards = (
        first_expand,
        first_reduce,
        heads_project,
        heads_merge,
        filter_expand,
        filter_reduce,
        second_expand,
        second_reduce,
    )
    gain_all = norm_gains.astype(WIDE_TYPE)
    bias_all = biases.astype(WIDE_TYPE)
    kernel_here = lax.dynamic_slice_in_dim(kernel.astype(WIDE_TYPE), member * channels, channels, 1)
    distance = distance_table.astype(WIDE_TYPE)
    first_hidden = own_part(bias_all[11 : 11 + stride].reshape(-1), member, hidden_here)
    second_hidden = own_part(
        bias_all[11 + stride : 11 + 2 * stride].reshape(-1), member, hidden_here
    )
    query_bias = own_part(bias_all[6], member, heads_width)
    value_bias = own_part(bias_all[7], member, heads_width)
    depth_gain = own_part(gain_all[3], member, channels)
    depth_bias = own_part(bias_all[3], member, channels)
    positions = jnp.arange(length_full)
    row_ids = member * rows_here + jnp.arange(rows_here)
    weight_totals = None
    gain_total = jnp.zeros(gain_all.shape, WIDE_TYPE)
    bias_total = jnp.zeros(bias_all.shape, WIDE_TYPE)
    kernel_total = jnp.zeros(kernel_here.shape, WIDE_TYPE)
    distance_total = jnp.zeros(distance.shape, WIDE_TYPE)
    output_list = []
    input_list = []
    for batch_index in range(batches):
        stream_zero = inputs[batch_index, 0].astype(WIDE_TYPE)
        clip_length = lengths[batch_index, 0]
        row_live = (row_ids < clip_length).astype(WIDE_TYPE)[:, None]
        key_live = positions < clip_length
        layer_full = fetch_layer(shards)
        stream_one, stored_one = feed_forward(
            stream_zero,
            gain_all[0],
            bias_all[0],
            (layer_full[0], layer_full[1]),
            first_hidden,
            bias_all[9],
        )
        stream_two, stored_two = attention_forward(
            stream_one,
            gain_all[1],
            bias_all[1],
            (layer_full[2], layer_full[3]),
            query_bias,
            value_bias,
            bias_all[8],
            distance,
            key_live,
        )
        stream_three, stored_three = filter_forward(
            stream_two,
            gain_all[2],
            bias_all[2],
            (layer_full[4], layer_full[5]),
            kernel_here,
            depth_gain,
            depth_bias,
            model_width,
        )
        stream_four, stored_four = feed_forward(
            stream_three,
            gain_all[4],
            bias_all[4],
            (layer_full[6], layer_full[7]),
            second_hidden,
            bias_all[10],
        )
        final_normed, final_unit, final_std = row_norm(stream_four, gain_all[5], bias_all[5])
        output_list.append((final_normed * row_live).astype(NARROW_TYPE))
        grad_four, final_gain_grad, final_bias_grad = row_norm_back(
            cotangent[batch_index, 0].astype(WIDE_TYPE) * row_live,
            final_unit,
            final_std,
            gain_all[5],
        )
        (
            grad_three,
            second_grads,
            second_gain_grad,
            second_bias_grad,
            second_hidden_grad,
            second_out_grad,
        ) = feed_backward(grad_four, stored_four, gain_all[4], (layer_full[6], layer_full[7]))
        (
            grad_two,
            filter_grads,
            filter_gain_grad,
            filter_bias_grad,
            depth_gain_grad,
            depth_bias_grad,
            kernel_grad,
        ) = filter_backward(
            grad_three,
            stored_three,
            gain_all[2],
            (layer_full[4], layer_full[5]),
            kernel_here,
            depth_gain,
            depth_bias,
            model_width,
        )
        (
            grad_one,
            mixer_grads,
            mixer_gain_grad,
            mixer_bias_grad,
            query_bias_grad,
            value_bias_grad,
            merge_bias_grad,
            distance_grad,
        ) = attention_backward(
            grad_two, stored_two, gain_all[1], (layer_full[2], layer_full[3]), distance, key_live
        )
        (
            grad_zero,
            first_grads,
            first_gain_grad,
            first_bias_grad,
            first_hidden_grad,
            first_out_grad,
        ) = feed_backward(grad_one, stored_one, gain_all[0], (layer_full[0], layer_full[1]))
        input_list.append(grad_zero)
        batch_grads = (
            first_grads[0],
            first_grads[1],
            mixer_grads[0],
            mixer_grads[1],
            filter_grads[0],
            filter_grads[1],
            second_grads[0],
            second_grads[1],
        )
        if weight_totals is None:
            weight_totals = tuple(batch_grads)
        else:
            weight_totals = tuple((total + term for total, term in zip(weight_totals, batch_grads)))
        gain_rows = jnp.stack(
            [
                first_gain_grad,
                mixer_gain_grad,
                filter_gain_grad,
                placed(depth_gain_grad, member, model_width, 0),
                second_gain_grad,
                final_gain_grad,
            ]
        )
        bias_rows = jnp.stack(
            [
                first_bias_grad,
                mixer_bias_grad,
                filter_bias_grad,
                placed(depth_bias_grad, member, model_width, 0),
                second_bias_grad,
                final_bias_grad,
                placed(query_bias_grad, member, model_width, 0),
                placed(value_bias_grad, member, model_width, 0),
                merge_bias_grad,
                first_out_grad,
                second_out_grad,
            ]
        )
        hidden_rows = jnp.concatenate(
            [
                placed(first_hidden_grad, member, hidden_here * lax.axis_size("tensor"), 0).reshape(
                    stride, model_width
                ),
                placed(
                    second_hidden_grad, member, hidden_here * lax.axis_size("tensor"), 0
                ).reshape(stride, model_width),
            ]
        )
        gain_total = gain_total + gain_rows
        bias_total = bias_total + jnp.concatenate([bias_rows, hidden_rows])
        kernel_total = kernel_total + kernel_grad
        distance_total = distance_total + distance_grad
    weight_totals = reduce_layer(weight_totals)
    kernel_full = placed(kernel_total, member, model_width, 1)
    gain_sum, bias_sum, kernel_sum, distance_sum = lax.psum(
        (gain_total, bias_total, kernel_full, distance_total), ("dp", "tensor")
    )
    outputs = jnp.stack(output_list)[:, None]
    input_grad = jnp.stack(input_list)[:, None]
    return (
        outputs,
        input_grad,
        weight_totals[0],
        weight_totals[1],
        weight_totals[2],
        weight_totals[3],
        weight_totals[4],
        weight_totals[5],
        weight_totals[6],
        weight_totals[7],
        gain_sum,
        bias_sum,
        kernel_sum,
        distance_sum,
    )


def solution(mesh):
    in_specs = (
        P(None, "dp", "tensor", None),
        P(None, "dp"),
        P(None, "dp", "tensor", None),
        P("dp", "tensor"),
        P("dp", "tensor"),
        P("dp", None, "tensor"),
        P("dp", "tensor"),
        P("dp", None, "tensor"),
        P("dp", "tensor"),
        P("dp", "tensor"),
        P("dp", "tensor"),
        P(),
        P(),
        P(),
        P(),
    )
    out_specs = (
        P(None, "dp", "tensor", None),
        P(None, "dp", "tensor", None),
        P("dp", "tensor"),
        P("dp", "tensor"),
        P("dp", None, "tensor"),
        P("dp", "tensor"),
        P("dp", None, "tensor"),
        P("dp", "tensor"),
        P("dp", "tensor"),
        P("dp", "tensor"),
        P(),
        P(),
        P(),
        P(),
    )
    return jax.shard_map(
        on_device, mesh=mesh, in_specs=in_specs, out_specs=out_specs, check_vma=False
    )
```

profile of v0, /device:TPU:0, one launch (start us, length us, event | category | flops | bytes accessed | tf_op | source)
XLA Modules:
  0.0 1912.5 jit_solution(7910292420422372367)
XLA Ops:
  16.9 28.6 %all-gather.23.cloned.1.call-done = bf16[512,1024]{1,0:T(8,128)(2,1)} async-done(((bf16[128,1024]{1,0:T(8,128)(2,1)}), bf16[512,1024]{1,0:T(8,128)(2,1)}) %all-gather.23.cloned.1.call-update) | async-done | bytes 1048592 | tf_op jit(solution)/shard_map/all_gather | solution.py:72
  45.5 29.3 %all-gather.25.cloned.1.call-done = bf16[1024,1024]{1,0:T(8,128)(2,1)} async-done(((bf16[128,1024]{1,0:T(8,128)(2,1)}), bf16[1024,1024]{1,0:T(8,128)(2,1)}) %all-gather.25.cloned.1.call-update) | async-done | bytes 2097168 | tf_op jit(solution)/shard_map/all_gather | solution.py:93
  109.2 25.4 %all-gather.43.cloned.1.call-done = bf16[512,1024]{1,0:T(8,128)(2,1)} async-done(((bf16[128,1024]{1,0:T(8,128)(2,1)}), bf16[512,1024]{1,0:T(8,128)(2,1)}) %all-gather.43.cloned.1.call-update) | async-done | bytes 1048592 | tf_op jit(solution)/shard_map/all_gather | solution.py:72
  164.0 28.0 %reduce-scatter.33.cloned.1.call-done = bf16[128,1024]{1,0:T(8,128)(2,1)} async-done(((bf16[512,1024]{1,0:T(8,128)(2,1)}), bf16[128,1024]{1,0:T(8,128)(2,1)}) %reduce-scatter.33.cloned.1.call-update) | async-done | bytes 262160 | tf_op jit(solution)/shard_map/reduce_scatter | solution.py:76
  220.0 30.1 %all-gather.29.cloned.1.call-done = bf16[512,1024]{1,0:T(8,128)(2,1)} async-done(((bf16[128,1024]{1,0:T(8,128)(2,1)}), bf16[512,1024]{1,0:T(8,128)(2,1)}) %all-gather.29.cloned.1.call-update) | async-done | bytes 1048592 | tf_op jit(solution)/shard_map/all_gather | solution.py:72
  419.2 26.0 %reduce-scatter.35.cloned.1.call-done = bf16[128,1024]{1,0:T(8,128)(2,1)} async-done(((bf16[512,1024]{1,0:T(8,128)(2,1)}), bf16[128,1024]{1,0:T(8,128)(2,1)}) %reduce-scatter.35.cloned.1.call-update) | async-done | bytes 262160 | tf_op jit(solution)/shard_map/reduce_scatter | solution.py:76
  470.2 30.1 %all-gather.47.cloned.1.call-done = bf16[512,1024]{1,0:T(8,128)(2,1)} async-done(((bf16[128,1024]{1,0:T(8,128)(2,1)}), bf16[512,1024]{1,0:T(8,128)(2,1)}) %all-gather.47.cloned.1.call-update) | async-done | bytes 1048592 | tf_op jit(solution)/shard_map/all_gather | solution.py:72
  503.7 26.0 %all-gather.33.cloned.1.call-done = bf16[512,1024]{1,0:T(8,128)(2,1)} async-done(((bf16[128,1024]{1,0:T(8,128)(2,1)}), bf16[512,1024]{1,0:T(8,128)(2,1)}) %all-gather.33.cloned.1.call-update) | async-done | bytes 1048592 | tf_op jit(solution)/shard_map/all_gather | solution.py:72
  581.4 26.3 %reduce-scatter.37.cloned.1.call-done = bf16[128,1024]{1,0:T(8,128)(2,1)} async-done(((bf16[512,1024]{1,0:T(8,128)(2,1)}), bf16[128,1024]{1,0:T(8,128)(2,1)}) %reduce-scatter.37.cloned.1.call-update) | async-done | bytes 262160 | tf_op jit(solution)/shard_map/reduce_scatter | solution.py:76
  636.0 30.0 %all-gather.49.cloned.1.call-done = bf16[512,1024]{1,0:T(8,128)(2,1)} async-done(((bf16[128,1024]{1,0:T(8,128)(2,1)}), bf16[512,1024]{1,0:T(8,128)(2,1)}) %all-gather.49.cloned.1.call-update) | async-done | bytes 1048592 | tf_op jit(solution)/shard_map/all_gather | solution.py:72
  754.2 28.8 %reduce-scatter.31.cloned.1.call-done = bf16[128,1024]{1,0:T(8,128)(2,1)} async-done(((bf16[512,1024]{1,0:T(8,128)(2,1)}), bf16[128,1024]{1,0:T(8,128)(2,1)}) %reduce-scatter.31.cloned.1.call-update) | async-done | bytes 262160 | tf_op jit(solution)/shard_map/reduce_scatter | solution.py:76
  908.9 25.9 %all-gather.61.cloned.1.call-done = bf16[512,1024]{1,0:T(8,128)(2,1)} async-done(((bf16[128,1024]{1,0:T(8,128)(2,1)}), bf16[512,1024]{1,0:T(8,128)(2,1)}) %all-gather.61.cloned.1.call-update) | async-done | bytes 1048592 | tf_op jit(solution)/shard_map/all_gather | solution.py:82
  937.5 26.9 %all-gather.53.cloned.1.call-done = bf16[512,1024]{1,0:T(8,128)(2,1)} async-done(((bf16[128,1024]{1,0:T(8,128)(2,1)}), bf16[512,1024]{1,0:T(8,128)(2,1)}) %all-gather.53.cloned.1.call-update) | async-done | bytes 1048592 | tf_op jit(solution)/shard_map/all_gather | solution.py:82
  1016.2 26.2 %reduce-scatter.51.cloned.1.call-done = bf16[128,1024]{1,0:T(8,128)(2,1)} async-done(((bf16[512,1024]{1,0:T(8,128)(2,1)}), bf16[128,1024]{1,0:T(8,128)(2,1)}) %reduce-scatter.51.cloned.1.call-update) | async-done | bytes 262160 | tf_op jit(solution)/shard_map/reduce_scatter | solution.py:86
  1230.8 26.7 %reduce-scatter.45.cloned.1.call-done = bf16[128,1024]{1,0:T(8,128)(2,1)} async-done(((bf16[512,1024]{1,0:T(8,128)(2,1)}), bf16[128,1024]{1,0:T(8,128)(2,1)}) %reduce-scatter.45.cloned.1.call-update) | async-done | bytes 262160 | tf_op jit(solution)/shard_map/reduce_scatter | solution.py:86
  1264.1 25.7 %all-gather.57.cloned.1.call-done = bf16[512,1024]{1,0:T(8,128)(2,1)} async-done(((bf16[128,1024]{1,0:T(8,128)(2,1)}), bf16[512,1024]{1,0:T(8,128)(2,1)}) %all-gather.57.cloned.1.call-update) | async-done | bytes 1048592 | tf_op jit(solution)/shard_map/all_gather | solution.py:82
  1424.1 40.3 %all-reduce.8 = (f32[6,1024]{1,0:T(8,128)}, f32[73,64]{0,1:T(8,128)}) all-reduce(f32[6,1024]{1,0:T(8,128)S(1)} %add.1189, f32[73,64]{0,1:T(8,128)S(1)} %fusion.10), channel_id=1, replica_groups=mesh['dp'=8,'tensor'=4] {'dp','tensor'}, use_global_device_ids=true, to_apply=%region_102.103 | all-reduce | flops 10816 | bytes 86528 | tf_op jit(solution)/shard_map/psum | solution.py:590
  1467.0 48.7 %reduce-scatter.71.cloned.1.call-done = f32[128,1024]{1,0:T(8,128)} async-done(((f32[1024,1024]{1,0:T(8,128)}), f32[128,1024]{1,0:T(8,128)}) %reduce-scatter.71.cloned.1.call-update) | async-done | bytes 524304 | tf_op jit(solution)/shard_map/reduce_scatter | solution.py:113
  1515.7 55.3 %reduce-scatter.69.cloned.1.call-done = f32[128,1024]{1,0:T(8,128)} async-done(((f32[1024,1024]{1,0:T(8,128)}), f32[128,1024]{1,0:T(8,128)}) %reduce-scatter.69.cloned.1.call-update) | async-done | bytes 524304 | tf_op jit(solution)/shard_map/reduce_scatter | solution.py:112
  1571.0 40.0 %reduce-scatter.63.cloned.1.call-done = f32[128,256]{1,0:T(8,128)} async-done(((f32[1024,256]{1,0:T(8,128)}), f32[128,256]{1,0:T(8,128)}) %reduce-scatter.63.cloned.1.call-update) | async-done | bytes 131088 | tf_op jit(solution)/shard_map/reduce_scatter | solution.py:109
  1611.0 50.6 %reduce-scatter.61.cloned.1.call-done = f32[128,3,256]{2,0,1:T(8,128)} async-done(((f32[1024,3,256]{2,0,1:T(8,128)}), f32[128,3,256]{2,0,1:T(8,128)}) %reduce-scatter.61.cloned.1.call-update) | async-done | bytes 393232 | tf_op jit(solution)/shard_map/reduce_scatter | solution.py:108
  1661.6 129.7 %all-reduce.14.cloned.1.call-done = (f32[19,1024]{1,0:T(8,128)}, f32[31,1024]{1,0:T(8,128)}) async-done(((f32[19,1024]{1,0:T(8,128)}, f32[31,1024]{1,0:T(8,128)}), (f32[19,1024]{1,0:T(8,128)}, f32[31,1024]{1,0:T(8,128)})) %all-reduce.14.cloned.1.call-update) | async-done | bytes 204816 | tf_op jit(solution)/shard_map/psum | solution.py:590
  1791.3 55.9 %reduce-scatter.59.cloned.1.call-done = f32[128,1024]{1,0:T(8,128)} async-done(((f32[1024,1024]{1,0:T(8,128)}), f32[128,1024]{1,0:T(8,128)}) %reduce-scatter.59.cloned.1.call-update) | async-done | bytes 524304 | tf_op jit(solution)/shard_map/reduce_scatter | solution.py:107
  1847.2 55.5 %reduce-scatter.57.cloned.1.call-done = f32[128,1024]{1,0:T(8,128)} async-done(((f32[1024,1024]{1,0:T(8,128)}), f32[128,1024]{1,0:T(8,128)}) %reduce-scatter.57.cloned.1.call-update) | async-done | bytes 524304 | tf_op jit(solution)/shard_map/reduce_scatter | solution.py:106
  (936 shorter events, 978.4 us)
Async XLA Ops:
  15.4 89.2 %all-gather.27.cloned.1.call-start = ((), (), s32[]{:S(2)}) async-start(), calls=%async_computation.26 | async-start | bytes 2359296 | tf_op jit(solution)/shard_map/all_gather | solution.py:94
  16.2 118.4 %all-gather.43.cloned.1.call-start = ((), (), s32[]{:S(2)}) async-start(), calls=%async_computation.38 | async-start | bytes 1310720 | tf_op jit(solution)/shard_map/all_gather | solution.py:72
  16.8 147.2 %reduce-scatter.25.cloned.1.call-start = ((), (), s32[]{:S(2)}) async-start(), calls=%async_computation.27 | async-start | bytes 1310720 | tf_op jit(solution)/shard_map/reduce_scatter | solution.py:76
  144.0 106.1 %all-gather.29.cloned.1.call-start = ((), (), s32[]{:S(2)}) async-start(), calls=%async_computation.28 | async-start | bytes 1310720 | tf_op jit(solution)/shard_map/all_gather | solution.py:72
  196.8 222.5 %reduce-scatter.27.cloned.1.call-start = ((), (), s32[]{:S(2)}) async-start(), calls=%async_computation.30 | async-start | bytes 1310720 | tf_op jit(solution)/shard_map/reduce_scatter | solution.py:76
  361.1 84.1 %reduce-scatter.35.cloned.1.call-start = ((), (), s32[]{:S(2)}) async-start(), calls=%async_computation.41 | async-start | bytes 1310720 | tf_op jit(solution)/shard_map/reduce_scatter | solution.py:76
  448.7 130.9 %reduce-scatter.29.cloned.1.call-start = ((), (), s32[]{:S(2)}) async-start(), calls=%async_computation.33 | async-start | bytes 1310720 | tf_op jit(solution)/shard_map/reduce_scatter | solution.py:76
  558.2 107.8 %all-gather.49.cloned.1.call-start = ((), (), s32[]{:S(2)}) async-start(), calls=%async_computation.44 | async-start | bytes 1310720 | tf_op jit(solution)/shard_map/all_gather | solution.py:72
  612.2 113.0 %all-gather.37.cloned.1.call-start = ((), (), s32[]{:S(2)}) async-start(), calls=%async_computation.34 | async-start | bytes 1310720 | tf_op jit(solution)/shard_map/all_gather | solution.py:72
  612.8 141.4 %reduce-scatter.39.cloned.1.call-start = ((), (), s32[]{:S(2)}) async-start(), calls=%async_computation.45 | async-start | bytes 1310720 | tf_op jit(solution)/shard_map/reduce_scatter | solution.py:76
  732.3 84.1 %all-gather.51.cloned.1.call-start = ((), (), s32[]{:S(2)}) async-start(), calls=%async_computation.46 | async-start | bytes 1310720 | tf_op jit(solution)/shard_map/all_gather | solution.py:82
  908.9 105.5 %reduce-scatter.43.cloned.1.call-start = ((), (), s32[]{:S(2)}) async-start(), calls=%async_computation.49 | async-start | bytes 1310720 | tf_op jit(solution)/shard_map/reduce_scatter | solution.py:86
  1048.2 182.6 %reduce-scatter.53.cloned.1.call-start = ((), (), s32[]{:S(2)}) async-start(), calls=%async_computation.59 | async-start | bytes 1310720 | tf_op jit(solution)/shard_map/reduce_scatter | solution.py:86
  1168.4 89.2 %reduce-scatter.45.cloned.1.call-start = ((), (), s32[]{:S(2)}) async-start(), calls=%async_computation.51 | async-start | bytes 1310720 | tf_op jit(solution)/shard_map/reduce_scatter | solution.py:86
  1263.9 117.0 %reduce-scatter.47.cloned.1.call-start = ((), (), s32[]{:S(2)}) async-start(), calls=%async_computation.53 | async-start | bytes 1310720 | tf_op jit(solution)/shard_map/reduce_scatter | solution.py:86
  1329.0 90.8 %reduce-scatter.65.cloned.1.call-start = ((), (), s32[]{:S(2)}) async-start(), calls=%async_computation.66 | async-start | bytes 2359296 | tf_op jit(solution)/shard_map/reduce_scatter | solution.py:110
  1333.4 133.6 %reduce-scatter.67.cloned.1.call-start = ((), (), s32[]{:S(2)}) async-start(), calls=%async_computation.67 | async-start | bytes 1179648 | tf_op jit(solution)/shard_map/reduce_scatter | solution.py:111
  1338.1 177.6 %reduce-scatter.71.cloned.1.call-start = ((), (), s32[]{:S(2)}) async-start(), calls=%async_computation.69 | async-start | bytes 4718592 | tf_op jit(solution)/shard_map/reduce_scatter | solution.py:113
  1345.3 225.7 %reduce-scatter.69.cloned.1.call-start = ((), (), s32[]{:S(2)}) async-start(), calls=%async_computation.68 | async-start | bytes 4718592 | tf_op jit(solution)/shard_map/reduce_scatter | solution.py:112
  1352.5 258.5 %reduce-scatter.63.cloned.1.call-start = ((), (), s32[]{:S(2)}) async-start(), calls=%async_computation.65 | async-start | bytes 1179648 | tf_op jit(solution)/shard_map/reduce_scatter | solution.py:109
  1356.3 305.3 %reduce-scatter.61.cloned.1.call-start = ((), (), s32[]{:S(2)}) async-start(), calls=%async_computation.64 | async-start | bytes 3538944 | tf_op jit(solution)/shard_map/reduce_scatter | solution.py:108
  1361.9 429.3 %all-reduce.14.cloned.1.call-start = ((), (), s32[]{:S(2)}) async-start(), calls=%async_computation.70 | async-start | bytes 458752 | tf_op jit(solution)/shard_map/psum | solution.py:590
  1383.9 463.3 %reduce-scatter.59.cloned.1.call-start = ((), (), s32[]{:S(2)}) async-start(), calls=%async_computation.63 | async-start | bytes 4718592 | tf_op jit(solution)/shard_map/reduce_scatter | solution.py:107
  1390.6 512.1 %reduce-scatter.57.cloned.1.call-start = ((), (), s32[]{:S(2)}) async-start(), calls=%async_computation.62 | async-start | bytes 4718592 | tf_op jit(solution)/shard_map/reduce_scatter | solution.py:106
  (285 other events, 5898.6 us)
Sparse Core Ops, SparseCore 0:
  14.8 30.6 all-gather.22
  47.4 27.3 all-gather.24
  76.7 27.8 all-gather.26
  106.6 27.9 all-gather.42
  222.1 27.9 all-gather.28
  252.2 27.4 all-gather.44
  472.3 27.9 all-gather.46
  502.3 27.4 all-gather.32
  638.0 27.9 all-gather.48
  667.9 27.3 all-gather.40
  697.3 27.9 all-gather.36
  817.8 27.4 all-gather.58
  937.0 27.4 all-gather.52
  1074.4 27.4 all-gather.62
  1291.8 27.4 all-gather.64
  1380.0 39.8 reduce-scatter.64
  1424.0 36.0 reduce-scatter.66
  1464.4 51.2 reduce-scatter.70
  1519.6 51.2 reduce-scatter.68
  1574.9 36.0 reduce-scatter.62
  1615.3 46.2 reduce-scatter.60
  1667.6 123.5 all-reduce.13
  1795.0 52.1 reduce-scatter.58
  1851.4 51.3 reduce-scatter.56
  (23 shorter events, 598.0 us)
where the time goes:
time: 1920 us; the launch traced here: 1910 us
  waiting for transfers between devices  1280 us (67%)
  local copies, waits for them, and re-layouts  244 us (13%)
  matrix products  173 us (9%)
  other arithmetic  110 us (6%)
  blocking collectives  84 us (4%)
    all_gather x8, waiting for transfers between devices, spread_rows(): return lax.all_gather(rows_low, 'tensor', axis=0, tiled=True)  221 us
    all_gather x8, waiting for transfers between devices, spread_grads(): return lax.all_gather(rows_low, 'tensor', axis=0, tiled=True)  190 us
    reduce_scatter x8, waiting for transfers between devices, collect_rows(): lax.psum_scatter(partial_value.astype(jnp.bfloat16), 'tensor', scatter_di...  171 us
    psum x1, waiting for transfers between devices, on_device(): lax.psum((gain_total, bias_total, kernel_full, distance_total), ('dp', 't...  130 us
    reduce_scatter x8, waiting for transfers between devices, collect_grads(): lax.psum_scatter(partial_value.astype(jnp.bfloat16), 'tensor', scatter_di...  114 us
    unnamed x546, local copies, waits for them, and re-layouts  91.6 us
    reduce_scatter x1, waiting for transfers between devices, reduce_layer(): lax.psum_scatter(grads[1], 'dp', scatter_dimension=0, tiled=True)  55.9 us
    reduce_scatter x1, waiting for transfers between devices, reduce_layer(): lax.psum_scatter(grads[0], 'dp', scatter_dimension=0, tiled=True)  55.5 us
  transfers between devices with their start and end apart: 47, of which 42 were waited for; matrix products, arithmetic and copies ran while one was open for 16% of the time, Pallas kernels for 0%

commit v1 on v0

v1 whole, which is shorter than its diff:
```python
import functools

import jax
import jax.numpy as jnp
from jax import lax
from jax.experimental import pallas as pl
from jax.experimental.pallas import tpu as pltpu
from jax.sharding import Mesh
from jax.sharding import PartitionSpec as P

HD = 64
LEFT = 64
RIGHT = 8
EPSILON = 1e-05
MASKED = -1e30
WIDE = jnp.float32
NARROW = jnp.bfloat16
CHUNK = 64
QROWS = 128
NEAR = 128
VMEM_BYTES = 48 * 1024 * 1024
PLANE_BLOCKS = 4
LANES = 128
COST_PART = 0.0005
PAD = 32


def sds(shape, dtype):
    return jax.ShapeDtypeStruct(shape, dtype)


def params(parallel=1):
    return pltpu.CompilerParams(
        dimension_semantics=("arbitrary",) * parallel, vmem_limit_bytes=VMEM_BYTES
    )


def cost(flops, moved, exps=0):
    return pl.CostEstimate(
        flops=int(flops * COST_PART), bytes_accessed=int(moved * COST_PART), transcendentals=0
    )


def whole(shape):
    return pl.BlockSpec(shape, lambda *_: (0,) * len(shape))


def rel_cols(p, r, width):
    return pl.ds(pl.multiple_of(jnp.bitwise_xor(p, r) * width, width), width)


def weight_specs(w, cols, col_block):
    if len(w) == PLANE_BLOCKS:
        shape = (1, 1, w[0].shape[2], cols)
        return [
            pl.BlockSpec(shape, functools.partial(lambda r, t, p: (t, r, 0, col_block), r))
            for r in range(PLANE_BLOCKS)
        ]
    shape = (1, w[0].shape[1], cols)
    return [
        pl.BlockSpec(shape, lambda t, p: (t, 0, col_block)),
        pl.BlockSpec(shape, lambda t, p: (t, 0, col_block)),
        pl.BlockSpec(shape, lambda t, p: (t, 0, col_block)),
        pl.BlockSpec(shape, lambda t, p: (jnp.minimum(t, 1), 0, col_block)),
        pl.BlockSpec(shape, lambda t, p: (jnp.maximum(t - 2, 0), 0, col_block)),
    ]


def weight_blocks(w_refs, t):
    if len(w_refs) == PLANE_BLOCKS:
        return [ref[0, 0] for ref in w_refs]
    own, wx, wy, da, db = w_refs
    return own[0], wx[0], wy[0], jnp.where(t < 2, da[0], db[0])


def sigmoid(v):
    return 1.0 / (1.0 + jnp.exp(-v))


def norm_stats(v):
    mean = jnp.mean(v, axis=-1, keepdims=True)
    center = v - mean
    inv_std = lax.rsqrt(jnp.mean(center * center, axis=-1, keepdims=True) + EPSILON)
    return center * inv_std, inv_std


def expand_body(kind, merged, scale, nw, p_ref, *refs):
    refs = list(refs)
    x_ref = refs.pop(0)
    if merged:
        pa_ref, pb_ref, ob_ref = refs[:3]
        refs = refs[3:]
    g_ref, b_ref = refs[:2]
    w_refs = refs[2 : 2 + nw]
    refs = refs[2 + nw :]
    if kind != "conv":
        hb_ref = refs.pop(0)
    if merged:
        xn_ref = refs.pop(0)
    a_ref = refs.pop(0)
    outs = refs
    t = pl.program_id(0)
    p = p_ref[0]
    width = x_ref.shape[1] // PLANE_BLOCKS

    @pl.when(t == 0)
    def _():
        def step(i, carry):
            rows = pl.ds(pl.multiple_of(i * CHUNK, CHUNK), CHUNK)
            v = x_ref[rows, :]
            if merged:
                branch = pa_ref[rows, :].astype(WIDE) + pb_ref[rows, :].astype(WIDE)
                v = v + scale * (branch + ob_ref[...])
                xn_ref[rows, :] = v
            unit, _ = norm_stats(v)
            a_ref[rows, :] = (unit * g_ref[...] + b_ref[...]).astype(NARROW)
            return carry

        lax.fori_loop(0, x_ref.shape[0] // CHUNK, step, 0)

    acc = None
    for r, w in enumerate(weight_blocks(w_refs, t)):
        term = jnp.dot(a_ref[:, rel_cols(p, r, width)], w, preferred_element_type=WIDE)
        acc = term if acc is None else acc + term
    if kind == "ff":
        u = acc + hb_ref[...]
        outs[0][...] = u
        outs[1][...] = (u * sigmoid(u)).astype(NARROW)
    elif kind == "qkv":
        outs[0][...] = (acc + hb_ref[...]).astype(NARROW)
    else:
        half = acc.shape[1] // 2
        gate = sigmoid(acc[:, half:])
        outs[0][...] = gate
        outs[1][...] = acc[:, :half] * gate


def norm_expand(kind, x, merge, scale, gain, bias, w, cols, col_block, p, hidden_bias):
    rows, width = x.shape
    merged = merge is not None
    ins = [x]
    specs = [whole((rows, width))]
    if merged:
        ins += list(merge)
        specs += [whole((rows, width)), whole((rows, width)), whole((1, width))]
    ins += [gain, bias, *w]
    specs += [whole((1, width)), whole((1, width)), *weight_specs(w, cols, col_block)]
    if kind != "conv":
        ins.append(hidden_bias)
        specs.append(pl.BlockSpec((1, cols), lambda t, p: (0, t)))
    shapes, out_specs = [], []
    if merged:
        shapes.append(sds((rows, width), WIDE))
        out_specs.append(whole((rows, width)))
    shapes.append(sds((rows, width), NARROW))
    out_specs.append(whole((rows, width)))
    if kind == "ff":
        outs = [(cols, WIDE), (cols, NARROW)]
    elif kind == "qkv":
        outs = [(cols, NARROW)]
    else:
        outs = [(cols // 2, WIDE), (cols // 2, WIDE)]
    for out_cols, dtype in outs:
        shapes.append(sds((rows, 4 * out_cols), dtype))
        out_specs.append(pl.BlockSpec((rows, out_cols), lambda t, p: (0, t)))
    return pl.pallas_call(
        functools.partial(expand_body, kind, merged, scale, len(w)),
        grid_spec=pltpu.PrefetchScalarGridSpec(
            num_scalar_prefetch=1, grid=(4,), in_specs=specs, out_specs=out_specs
        ),
        out_shape=shapes,
        compiler_params=params(),
        cost_estimate=cost(2 * rows * width * 4 * cols, 8 * width * cols + 12 * rows * width),
        name="norm_expand_" + kind,
    )(p, *ins)


def reduce_body(nw, p_ref, s_ref, *refs):
    w_refs = refs[:nw]
    out_ref, acc_ref = refs[nw:]
    t = pl.program_id(0)
    p = p_ref[0]
    width = out_ref.shape[1] // PLANE_BLOCKS
    s = s_ref[...]

    @pl.when(t == 0)
    def _():
        acc_ref[...] = jnp.zeros_like(acc_ref)

    for r, w in enumerate(weight_blocks(w_refs, t)):
        cols = rel_cols(p, r, width)
        acc_ref[:, cols] += lax.dot_general(
            s, w, (((1,), (1,)), ((), ())), preferred_element_type=WIDE
        )

    @pl.when(t == 3)
    def _():
        out_ref[...] = acc_ref[...].astype(NARROW)


def reduce_mm(s, w, cols, col_block, p, width):
    rows = s.shape[0]
    return pl.pallas_call(
        functools.partial(reduce_body, len(w)),
        grid_spec=pltpu.PrefetchScalarGridSpec(
            num_scalar_prefetch=1,
            grid=(4,),
            in_specs=[
                pl.BlockSpec((rows, cols), lambda t, p: (0, t)),
                *weight_specs(w, cols, col_block),
            ],
            out_specs=whole((rows, width)),
            scratch_shapes=[pltpu.VMEM((rows, width), WIDE)],
        ),
        out_shape=sds((rows, width), NARROW),
        compiler_params=params(),
        cost_estimate=cost(2 * rows * width * 4 * cols, 8 * width * cols + 2 * rows * width),
        name="reduce_mm",
    )(p, s, *w)


def back_body(kind, nw, p_ref, g_ref, *refs):
    w_refs = refs[:nw]
    rest = refs[nw:]
    t = pl.program_id(0)
    p = p_ref[0]
    width = g_ref.shape[1] // PLANE_BLOCKS
    acc = None
    for r, w in enumerate(weight_blocks(w_refs, t)):
        term = jnp.dot(g_ref[:, rel_cols(p, r, width)], w, preferred_element_type=WIDE)
        acc = term if acc is None else acc + term
    if kind == "ff":
        u_ref, gu_ref, gc_ref = rest
        u = u_ref[...]
        logistic = sigmoid(u)
        gu = acc * (logistic * (1.0 + u * (1.0 - logistic)))
        gu_ref[...] = gu.astype(NARROW)
        gc_ref[...] = jnp.sum(gu, axis=0, keepdims=True)
    else:
        (out_ref,) = rest
        out_ref[...] = acc.astype(out_ref.dtype)


def back_expand(kind, g, w, cols, col_block, p, u=None):
    rows, width = g.shape
    ins = [g, *w]
    block = pl.BlockSpec((rows, cols), lambda t, p: (0, t))
    specs = [whole((rows, width)), *weight_specs(w, cols, col_block)]
    if kind == "ff":
        ins.append(u)
        specs.append(block)
        shapes = [sds((rows, 4 * cols), NARROW), sds((1, 4 * cols), WIDE)]
        out_specs = [block, pl.BlockSpec((1, cols), lambda t, p: (0, t))]
    else:
        shapes = sds((rows, 4 * cols), NARROW if kind == "low" else WIDE)
        out_specs = block
    return pl.pallas_call(
        functools.partial(back_body, kind, len(w)),
        grid_spec=pltpu.PrefetchScalarGridSpec(
            num_scalar_prefetch=1, grid=(4,), in_specs=specs, out_specs=out_specs
        ),
        out_shape=shapes,
        compiler_params=params(),
        cost_estimate=cost(2 * rows * width * 4 * cols, 8 * width * cols + 12 * rows * cols),
        name="back_expand_" + kind,
    )(p, *ins)


def wgrad_body(count, p_ref, *refs):
    x_refs = refs[:count]
    s_refs = refs[count : 2 * count]
    own_ref, sx_ref, kx_ref, sy_ref, ky_ref = refs[2 * count :]
    t = pl.program_id(0)
    p = p_ref[0]

    def grad(r, put):
        start = 0
        for x_ref, s_ref in zip(x_refs, s_refs):
            width = x_ref.shape[1] // PLANE_BLOCKS
            cols = s_ref.shape[1]
            term = lax.dot_general(
                x_ref[:, rel_cols(p, r, width)],
                s_ref[...],
                (((0,), (0,)), ((), ())),
                preferred_element_type=WIDE,
            ).astype(NARROW)
            put(start, cols, term)
            start += cols

    def put_own(start, cols, term):
        own_ref[0, :, start : start + cols] = term

    grad(0, put_own)

    @pl.when(t < 2)
    def _():
        def put_x(start, cols, term):
            sx_ref[0, 0, :, start : start + cols] = term

        def put_d(start, cols, term):
            sx_ref[1, 0, :, start : start + cols] = term

        def put_y(start, cols, term):
            ky_ref[0, :, start : start + cols] = term

        grad(1, put_x)
        grad(3, put_d)
        grad(2, put_y)

    @pl.when(t >= 2)
    def _():
        def put_y(start, cols, term):
            sy_ref[0, 0, :, start : start + cols] = term

        def put_d(start, cols, term):
            sy_ref[1, 0, :, start : start + cols] = term

        def put_x(start, cols, term):
            kx_ref[0, :, start : start + cols] = term

        grad(2, put_y)
        grad(3, put_d)
        grad(1, put_x)


def wgrad(xs, ss, p):
    rows, width = xs[0].shape
    wrows = width // PLANE_BLOCKS
    widths = [s.shape[1] // 4 for s in ss]
    cols = sum(widths)
    first = lambda t: jnp.minimum(t, 1)
    last = lambda t: jnp.maximum(t - 2, 0)
    return pl.pallas_call(
        functools.partial(wgrad_body, len(xs)),
        grid_spec=pltpu.PrefetchScalarGridSpec(
            num_scalar_prefetch=1,
            grid=(4,),
            in_specs=[whole((rows, width)) for _ in xs]
            + [pl.BlockSpec((rows, c), lambda t, p: (0, t)) for c in widths],
            out_specs=[
                pl.BlockSpec((1, wrows, cols), lambda t, p: (t, 0, 0)),
                pl.BlockSpec((2, 1, wrows, cols), lambda t, p: (0, first(t), 0, 0)),
                pl.BlockSpec((1, wrows, cols), lambda t, p: (last(t), 0, 0)),
                pl.BlockSpec((2, 1, wrows, cols), lambda t, p: (0, last(t), 0, 0)),
                pl.BlockSpec((1, wrows, cols), lambda t, p: (first(t), 0, 0)),
            ],
        ),
        out_shape=[
            sds((4, wrows, cols), NARROW),
            sds((2, 2, wrows, cols), NARROW),
            sds((2, wrows, cols), NARROW),
            sds((2, 2, wrows, cols), NARROW),
            sds((2, wrows, cols), NARROW),
        ],
        compiler_params=params(),
        cost_estimate=cost(2 * rows * width * 4 * cols, 8 * width * cols + 4 * rows * width),
        name="wgrad",
    )(p, *xs, *ss)


def wgrad_flat_body(p_ref, x_ref, s_ref, out_ref):
    p = p_ref[0]
    width = x_ref.shape[1] // PLANE_BLOCKS
    for r in range(PLANE_BLOCKS):
        out_ref[0, r] = lax.dot_general(
            x_ref[:, rel_cols(p, r, width)],
            s_ref[...],
            (((0,), (0,)), ((), ())),
            preferred_element_type=WIDE,
        ).astype(NARROW)


def wgrad_flat(x, s, p):
    rows, width = x.shape
    wrows = width // PLANE_BLOCKS
    cols = s.shape[1] // 4
    return pl.pallas_call(
        wgrad_flat_body,
        grid_spec=pltpu.PrefetchScalarGridSpec(
            num_scalar_prefetch=1,
            grid=(4,),
            in_specs=[whole((rows, width)), pl.BlockSpec((rows, cols), lambda t, p: (0, t))],
            out_specs=pl.BlockSpec((1, PLANE_BLOCKS, wrows, cols), lambda t, p: (t, 0, 0, 0)),
        ),
        out_shape=sds((4, PLANE_BLOCKS, wrows, cols), NARROW),
        compiler_params=params(),
        cost_estimate=cost(2 * rows * width * 4 * cols, 8 * width * cols + 4 * rows * width),
        name="wgrad_flat",
    )(p, x, s)


def combine_body(own_ref, rx_ref, ry_ref, fx_ref, fy_ref, out_ref):
    t = pl.program_id(0)
    near = jnp.where(t < 2, rx_ref[0, 0], ry_ref[0, 0])
    far = jnp.where(t < 2, fx_ref[0], fy_ref[0])
    total = own_ref[0].astype(WIDE) + near.astype(WIDE) + far.astype(WIDE)
    out_ref[0] = total.astype(NARROW)


def combine(own, rx, ry, fx, fy):
    rows, cols = own.shape[1:]
    first = lambda t: jnp.minimum(t, 1)
    last = lambda t: jnp.maximum(t - 2, 0)
    return pl.pallas_call(
        combine_body,
        grid=(4,),
        in_specs=[
            pl.BlockSpec((1, rows, cols), lambda t: (t, 0, 0)),
            pl.BlockSpec((1, 1, rows, cols), lambda t: (0, first(t), 0, 0)),
            pl.BlockSpec((1, 1, rows, cols), lambda t: (0, last(t), 0, 0)),
            pl.BlockSpec((1, rows, cols), lambda t: (first(t), 0, 0)),
            pl.BlockSpec((1, rows, cols), lambda t: (last(t), 0, 0)),
        ],
        out_specs=pl.BlockSpec((1, rows, cols), lambda t: (t, 0, 0)),
        out_shape=sds(own.shape, NARROW),
        compiler_params=params(),
        cost_estimate=cost(8 * rows * cols, 32 * rows * cols),
        name="combine",
    )(own, rx, ry, fx, fy)


def norm_back_body(scale, x_ref, gx_ref, pa_ref, pb_ref, g_ref, out_ref, low_ref, sums_ref):
    @pl.when(pl.program_id(0) == 0)
    def _():
        sums_ref[...] = jnp.zeros_like(sums_ref)

    unit, inv_std = norm_stats(x_ref[...])
    grad = pa_ref[...].astype(WIDE) + pb_ref[...].astype(WIDE)
    scaled = grad * g_ref[...]
    gx = gx_ref[...] + inv_std * (
        scaled
        - jnp.mean(scaled, axis=-1, keepdims=True)
        - unit * jnp.mean(scaled * unit, axis=-1, keepdims=True)
    )
    out_ref[...] = gx
    branch = scale * gx
    low_ref[...] = branch.astype(NARROW)
    sums_ref[0:1, :] += jnp.sum(grad * unit, axis=0, keepdims=True)
    sums_ref[1:2, :] += jnp.sum(grad, axis=0, keepdims=True)
    sums_ref[2:3, :] += jnp.sum(branch, axis=0, keepdims=True)


def norm_back(scale, x, gx, pa, pb, gain):
    rows, width = x.shape
    block = pl.BlockSpec((CHUNK, width), lambda i: (i, 0))
    return pl.pallas_call(
        functools.partial(norm_back_body, scale),
        grid=(rows // CHUNK,),
        in_specs=[block, block, block, block, whole((1, width))],
        out_specs=[block, block, whole((8, width))],
        out_shape=[sds((rows, width), WIDE), sds((rows, width), NARROW), sds((8, width), WIDE)],
        compiler_params=params(),
        cost_estimate=cost(20 * rows * width, 18 * rows * width),
        name="norm_back",
    )(x, gx, pa, pb, gain)


def final_body(
    x_ref, pa_ref, pb_ref, ob_ref, cot_ref, live_ref, g_ref, b_ref, y_ref, gx_ref, low_ref, sums_ref
):
    @pl.when(pl.program_id(0) == 0)
    def _():
        sums_ref[...] = jnp.zeros_like(sums_ref)

    branch = pa_ref[...].astype(WIDE) + pb_ref[...].astype(WIDE)
    v = x_ref[...] + 0.5 * (branch + ob_ref[...])
    unit, inv_std = norm_stats(v)
    live = live_ref[...]
    y_ref[...] = ((unit * g_ref[...] + b_ref[...]) * live).astype(NARROW)
    grad = cot_ref[...].astype(WIDE) * live
    scaled = grad * g_ref[...]
    gx = inv_std * (
        scaled
        - jnp.mean(scaled, axis=-1, keepdims=True)
        - unit * jnp.mean(scaled * unit, axis=-1, keepdims=True)
    )
    gx_ref[...] = gx
    half = 0.5 * gx
    low_ref[...] = half.astype(NARROW)
    sums_ref[0:1, :] += jnp.sum(grad * unit, axis=0, keepdims=True)
    sums_ref[1:2, :] += jnp.sum(grad, axis=0, keepdims=True)
    sums_ref[2:3, :] += jnp.sum(half, axis=0, keepdims=True)


def final_norm(x, pa, pb, ob, cot, live, gain, bias):
    rows, width = x.shape
    block = pl.BlockSpec((CHUNK, width), lambda i: (i, 0))
    row = whole((1, width))
    return pl.pallas_call(
        final_body,
        grid=(rows // CHUNK,),
        in_specs=[
            block, block, block, row, block,
            pl.BlockSpec((CHUNK, 1), lambda i: (i, 0)), row, row,
        ],
        out_specs=[block, block, block, whole((8, width))],
        out_shape=[
            sds((rows, width), NARROW),
            sds((rows, width), WIDE),
            sds((rows, width), NARROW),
            sds((8, width), WIDE),
        ],
        compiler_params=params(),
        cost_estimate=cost(24 * rows * width, 18 * rows * width),
        name="final_norm",
    )(x, pa, pb, ob, cot, live, gain, bias)


def distances(i0, keys):
    rows = lax.broadcasted_iota(jnp.int32, (QROWS, keys), 0) + i0
    cols = lax.broadcasted_iota(jnp.int32, (QROWS, keys), 1)
    return cols - rows, cols


def attend_body(len_ref, qkv_ref, table_ref, o_ref, p_out_ref):
    keys = qkv_ref.shape[0]
    width = qkv_ref.shape[1] // 3
    length = len_ref[0]
    table = table_ref[...]

    key_live = lax.broadcasted_iota(jnp.int32, (QROWS, keys), 1) < length
    for n in range(keys // QROWS):
        i0 = n * QROWS
        rows = slice(i0, i0 + QROWS)
        begin = max(0, i0 - QROWS)
        end = min(keys, i0 + 2 * QROWS)
        span = end - begin
        apart = distances(i0 - begin, span)[0]
        far_left = apart <= -LEFT
        far_right = apart >= RIGHT
        for e in range(width // HD):
            q = qkv_ref[rows, e * HD : (e + 1) * HD]
            k = qkv_ref[:, width + e * HD : width + (e + 1) * HD]
            v = qkv_ref[:, 2 * width + e * HD : 2 * width + (e + 1) * HD]
            near = lax.dot_general(q, table, (((1,), (1,)), ((), ())), preferred_element_type=WIDE)
            left, right = near[:, 0:1], near[:, LEFT + RIGHT : LEFT + RIGHT + 1]
            band = jnp.concatenate([near, jnp.zeros((QROWS, span - NEAR), WIDE)], axis=1)
            band = pltpu.roll(band, (i0 - begin + span - LEFT) % span, 1, stride=1, stride_axis=0)
            pieces = [jnp.where(far_left, left, jnp.where(far_right, right, band))]
            if begin > 0:
                pieces.insert(0, jnp.broadcast_to(left, (QROWS, begin)))
            if end < keys:
                pieces.append(jnp.broadcast_to(right, (QROWS, keys - end)))
            rel = jnp.concatenate(pieces, axis=1) if len(pieces) > 1 else pieces[0]
            s = lax.dot_general(q, k, (((1,), (1,)), ((), ())), preferred_element_type=WIDE)
            s = jnp.where(key_live, (s + rel) * HD ** (-0.5), MASKED)
            top = jnp.max(s, axis=-1, keepdims=True)
            ex = jnp.exp(s - top)
            chance = (ex * (1.0 / row_sum(ex))).astype(NARROW)
            p_out_ref[e, rows, :] = chance
            o_ref[rows, e * HD : (e + 1) * HD] = jnp.dot(
                chance, v, preferred_element_type=WIDE
            ).astype(NARROW)


def attend(qkv, table, length):
    rows = qkv.shape[0]
    width = qkv.shape[1] // 12
    heads = width // HD
    return pl.pallas_call(
        attend_body,
        grid_spec=pltpu.PrefetchScalarGridSpec(
            num_scalar_prefetch=1,
            grid=(4,),
            in_specs=[
                pl.BlockSpec((rows, 3 * width), lambda t, n: (0, t)),
                whole(table.shape),
            ],
            out_specs=[
                pl.BlockSpec((rows, width), lambda t, n: (0, t)),
                pl.BlockSpec((heads, rows, rows), lambda t, n: (t, 0, 0)),
            ],
        ),
        out_shape=[sds((rows, 4 * width), NARROW), sds((4 * heads, rows, rows), NARROW)],
        compiler_params=params(),
        cost_estimate=cost(16 * heads * rows * rows * HD, 10 * heads * rows * rows, 4 * heads * rows * rows),
        name="attend",
    )(length, qkv, table)


def attend_back_body(qkv_ref, go_ref, p_ref, table_ref, out_ref, sums_ref, dist_ref, gk_ref, gv_ref):
    keys = qkv_ref.shape[0]
    width = qkv_ref.shape[1] // 3
    table = table_ref[...]
    scale = HD ** (-0.5)
    nt = (((1,), (1,)), ((), ()))
    flip = (
        lax.broadcasted_iota(jnp.int32, (QROWS, QROWS), 0)
        + lax.broadcasted_iota(jnp.int32, (QROWS, QROWS), 1)
        == QROWS - 1
    ).astype(NARROW)
    bucket = lax.broadcasted_iota(jnp.int32, (QROWS, NEAR), 1)
    first_row = table[0:1, :].astype(WIDE)
    last_row = table[LEFT + RIGHT : LEFT + RIGHT + 1, :].astype(WIDE)

    @pl.when(pl.program_id(0) == 0)
    def _():
        dist_ref[...] = jnp.zeros_like(dist_ref)

    q_turned = jnp.transpose(qkv_ref[:, :width])
    go_turned = jnp.transpose(go_ref[...])
    for n in range(keys // QROWS):
        i0 = n * QROWS
        rows = slice(i0, i0 + QROWS)
        begin = max(0, i0 - QROWS)
        end = min(keys, i0 + 2 * QROWS)
        span = end - begin
        apart = distances(i0 - begin, span)[0]
        far_left = apart <= -LEFT
        far_right = apart >= RIGHT
        key_of = lax.broadcasted_iota(jnp.int32, (QROWS, NEAR), 0) + bucket + (i0 - LEFT)
        inside = (bucket > 0) & (bucket < LEFT + RIGHT) & (key_of >= 0) & (key_of < keys)
        for e in range(width // HD):
            lanes = slice(e * HD, (e + 1) * HD)
            q = qkv_ref[rows, lanes]
            k = qkv_ref[:, width + e * HD : width + (e + 1) * HD]
            v = qkv_ref[:, 2 * width + e * HD : 2 * width + (e + 1) * HD]
            go = go_ref[rows, lanes]
            chance = p_ref[e, rows, :]
            wide = chance.astype(WIDE)
            gp = lax.dot_general(go, v, nt, preferred_element_type=WIDE)
            gs = (wide * (gp - jnp.sum(gp * wide, axis=-1, keepdims=True))).astype(NARROW)
            gsw = gs.astype(WIDE)
            window = gsw[:, begin:end]
            turned = jnp.dot(flip, gs[:, begin:end], preferred_element_type=WIDE)
            turned = pltpu.roll(
                turned, (LEFT + 1 - QROWS - (i0 - begin)) % span, 1, stride=1, stride_axis=0
            )[:, :NEAR]
            back = jnp.dot(flip, turned.astype(NARROW), preferred_element_type=WIDE)
            left_sum = row_sum(jnp.where(far_left, window, 0.0))
            right_sum = row_sum(jnp.where(far_right, window, 0.0))
            if begin > 0:
                left_sum += row_sum(gsw[:, :begin])
            if end < keys:
                right_sum += row_sum(gsw[:, end:])
            left_sum *= scale
            right_sum *= scale
            near = (jnp.where(inside, back, 0.0) * scale).astype(NARROW)
            gq = jnp.dot(gs, k, preferred_element_type=WIDE) * scale
            gq += jnp.dot(near, table, preferred_element_type=WIDE)
            gq += left_sum * first_row + right_sum * last_row
            out_ref[rows, lanes] = gq.astype(NARROW)
            q_part = q_turned[lanes, rows]
            qw = q.astype(WIDE)
            dist_ref[:HD, :] += jnp.dot(q_part, near, preferred_element_type=WIDE)
            dist_ref[HD : HD + 1, :HD] += jnp.sum(left_sum * qw, axis=0, keepdims=True)
            dist_ref[HD + 1 : HD + 2, :HD] += jnp.sum(right_sum * qw, axis=0, keepdims=True)
            gk = jnp.dot(q_part, gs, preferred_element_type=WIDE)
            gv = jnp.dot(go_turned[lanes, rows], chance, preferred_element_type=WIDE)
            if n == 0:
                gk_ref[lanes, :] = gk
                gv_ref[lanes, :] = gv
            else:
                gk_ref[lanes, :] += gk
                gv_ref[lanes, :] += gv

    out_ref[:, width : 2 * width] = jnp.transpose(gk_ref[...] * scale).astype(NARROW)
    out_ref[:, 2 * width :] = jnp.transpose(gv_ref[...]).astype(NARROW)
    sums_ref[...] = jnp.sum(out_ref[...].astype(WIDE), axis=0, keepdims=True)


def attend_back(qkv, go, chances, table):
    rows = qkv.shape[0]
    width = qkv.shape[1] // 12
    heads = width // HD
    return pl.pallas_call(
        attend_back_body,
        grid=(4,),
        in_specs=[
            pl.BlockSpec((rows, 3 * width), lambda t: (0, t)),
            pl.BlockSpec((rows, width), lambda t: (0, t)),
            pl.BlockSpec((heads, rows, rows), lambda t: (t, 0, 0)),
            whole(table.shape),
        ],
        out_specs=[
            pl.BlockSpec((rows, 3 * width), lambda t: (0, t)),
            pl.BlockSpec((1, 3 * width), lambda t: (0, t)),
            whole((HD + 8, NEAR)),
        ],
        out_shape=[
            sds((rows, 12 * width), NARROW),
            sds((1, 12 * width), WIDE),
            sds((HD + 8, NEAR), WIDE),
        ],
        scratch_shapes=[pltpu.VMEM((width, rows), WIDE), pltpu.VMEM((width, rows), WIDE)],
        compiler_params=params(),
        cost_estimate=cost(40 * heads * rows * rows * HD, 10 * heads * rows * rows),
        name="attend_back",
    )(qkv, go, chances, table)


def lane_pair(first, second, rows):
    lane = lax.broadcasted_iota(jnp.int32, (rows, LANES), 1)
    return jnp.where(lane == 0, first, jnp.where(lane == 1, second, 0.0))


def row_sum(v):
    return jnp.sum(v, axis=-1, keepdims=True)


def mix_body(taps_count, z_ref, taps_ref, y_ref, sums_ref, pad_ref):
    rows = z_ref.shape[0]

    @pl.when(pl.program_id(0) == 0)
    def _():
        sums_ref[...] = jnp.zeros_like(sums_ref)

    pad_ref[0:PAD, :] = jnp.zeros((PAD, pad_ref.shape[1]), WIDE)
    pad_ref[PAD:, :] = z_ref[...]
    for start in range(0, rows, CHUNK):
        total = None
        for i in range(taps_count):
            begin = start + PAD - taps_count + 1 + i
            term = taps_ref[i : i + 1, :] * pad_ref[begin : begin + CHUNK, :]
            total = term if total is None else total + term
        here = slice(start, start + CHUNK)
        y_ref[here, :] = total
        sums_ref[here, :] += lane_pair(row_sum(total), row_sum(total * total), CHUNK)


def causal_mix(z, taps, taps_count):
    rows, cols = z.shape
    block = pl.BlockSpec((rows, cols // 4), lambda t: (0, t))
    return pl.pallas_call(
        functools.partial(mix_body, taps_count),
        grid=(4,),
        in_specs=[block, pl.BlockSpec((taps.shape[0], cols // 4), lambda t: (0, t))],
        out_specs=[block, whole((rows, LANES))],
        out_shape=[sds((rows, cols), WIDE), sds((rows, LANES), WIDE)],
        scratch_shapes=[pltpu.VMEM((rows + PAD, cols // 4), WIDE)],
        compiler_params=params(),
        cost_estimate=cost(2 * taps_count * rows * cols, 8 * rows * cols),
        name="causal_mix",
    )(z, taps)


def depth_stats(sa_ref, sb_ref, here, width):
    sums = (sa_ref[here, :] + sb_ref[here, :]) * (1.0 / width)
    mean = sums[:, 0:1]
    return mean, lax.rsqrt(sums[:, 1:2] - mean * mean + EPSILON)


def filter_out_body(p_ref, y_ref, sa_ref, sb_ref, g_ref, b_ref, *refs):
    w_refs = refs[:5]
    out_ref, low_ref, acc_ref = refs[5:]
    t = pl.program_id(0)
    p = p_ref[0]
    width = out_ref.shape[1]
    mean, std = depth_stats(sa_ref, sb_ref, slice(None), width)
    yn = (y_ref[...] - mean) * std * g_ref[...] + b_ref[...]
    low = (yn * sigmoid(yn)).astype(NARROW)
    low_ref[...] = low

    @pl.when(t == 0)
    def _():
        acc_ref[...] = jnp.zeros_like(acc_ref)

    for r, w in enumerate(weight_blocks(w_refs, t)):
        cols = rel_cols(p, r, width // PLANE_BLOCKS)
        acc_ref[:, cols] += lax.dot_general(
            low, w, (((1,), (1,)), ((), ())), preferred_element_type=WIDE
        )

    @pl.when(t == 3)
    def _():
        out_ref[...] = acc_ref[...].astype(NARROW)


def filter_out(y, sums, gain, bias, w, cols, col_block, p, width):
    rows = y.shape[0]
    block = pl.BlockSpec((rows, cols), lambda t, p: (0, t))
    row = pl.BlockSpec((1, cols), lambda t, p: (0, t))
    return pl.pallas_call(
        filter_out_body,
        grid_spec=pltpu.PrefetchScalarGridSpec(
            num_scalar_prefetch=1,
            grid=(4,),
            in_specs=[
                block, whole((rows, LANES)), whole((rows, LANES)), row, row,
                *weight_specs(w, cols, col_block),
            ],
            out_specs=[whole((rows, width)), block],
            scratch_shapes=[pltpu.VMEM((rows, width), WIDE)],
        ),
        out_shape=[sds((rows, width), NARROW), sds(y.shape, NARROW)],
        compiler_params=params(),
        cost_estimate=cost(2 * rows * width * 4 * cols, 8 * width * cols + 6 * rows * width),
        name="filter_out",
    )(p, y, *sums, gain, bias, *w)


def filter_in_body(p_ref, grad_ref, y_ref, sa_ref, sb_ref, g_ref, b_ref, *refs):
    w_refs = refs[:5]
    gyn_ref, cols_ref, rows_ref = refs[5:]
    t = pl.program_id(0)
    p = p_ref[0]
    width = grad_ref.shape[1]
    acc = None
    for r, w in enumerate(weight_blocks(w_refs, t)):
        cols = rel_cols(p, r, width // PLANE_BLOCKS)
        term = jnp.dot(grad_ref[:, cols], w, preferred_element_type=WIDE)
        acc = term if acc is None else acc + term
    mean, std = depth_stats(sa_ref, sb_ref, slice(None), width)
    unit = (y_ref[...] - mean) * std
    yn = unit * g_ref[...] + b_ref[...]
    logistic = sigmoid(yn)
    gyn = acc * (logistic * (1.0 + yn * (1.0 - logistic)))
    gyn_ref[...] = gyn
    cols_ref[0:1, :] = jnp.sum(gyn * unit, axis=0, keepdims=True)
    cols_ref[1:2, :] = jnp.sum(gyn, axis=0, keepdims=True)
    scaled = gyn * g_ref[...]
    pair = lane_pair(row_sum(scaled), row_sum(scaled * unit), gyn.shape[0])

    @pl.when(t == 0)
    def _():
        rows_ref[...] = pair

    @pl.when(t > 0)
    def _():
        rows_ref[...] += pair


def filter_in(grad, y, sums, gain, bias, w, cols, col_block, p):
    rows, width = grad.shape
    block = pl.BlockSpec((rows, cols), lambda t, p: (0, t))
    row = pl.BlockSpec((1, cols), lambda t, p: (0, t))
    return pl.pallas_call(
        filter_in_body,
        grid_spec=pltpu.PrefetchScalarGridSpec(
            num_scalar_prefetch=1,
            grid=(4,),
            in_specs=[
                whole((rows, width)), block, whole((rows, LANES)), whole((rows, LANES)), row, row,
                *weight_specs(w, cols, col_block),
            ],
            out_specs=[
                block,
                pl.BlockSpec((8, cols), lambda t, p: (0, t)),
                whole((rows, LANES)),
            ],
        ),
        out_shape=[sds(y.shape, WIDE), sds((8, 4 * cols), WIDE), sds((rows, LANES), WIDE)],
        compiler_params=params(),
        cost_estimate=cost(2 * rows * width * 4 * cols, 8 * width * cols + 6 * rows * width),
        name="filter_in",
    )(p, grad, y, *sums, gain, bias, *w)


def mix_back_body(
    taps_count, width, gyn_ref, y_ref, sa_ref, sb_ref, ra_ref, rb_ref, g_ref, z_ref, gate_ref,
    taps_ref, out_ref, grad_ref, gpad_ref, zpad_ref,
):
    rows, cols = z_ref.shape
    zpad_ref[0:PAD, :] = jnp.zeros((PAD, cols), WIDE)
    zpad_ref[PAD:, :] = z_ref[...]
    gpad_ref[rows:, :] = jnp.zeros((PAD, cols), WIDE)
    mean, std = depth_stats(sa_ref, sb_ref, slice(None), width)
    pair = (ra_ref[...] + rb_ref[...]) * (1.0 / width)
    unit = (y_ref[...] - mean) * std
    gpad_ref[0:rows, :] = std * (gyn_ref[...] * g_ref[...] - pair[:, 0:1] - unit * pair[:, 1:2])
    sums = [None] * taps_count
    for start in range(0, rows, CHUNK):
        here = slice(start, start + CHUNK)
        gy = gpad_ref[here, :]
        total = None
        for i in range(taps_count):
            begin = start + taps_count - 1 - i
            term = taps_ref[i : i + 1, :] * gpad_ref[begin : begin + CHUNK, :]
            total = term if total is None else total + term
        for i in range(taps_count):
            begin = start + PAD - taps_count + 1 + i
            part = zpad_ref[begin : begin + CHUNK, :] * gy
            part = jnp.sum(part.reshape(CHUNK // 8, 8, cols), axis=0)
            sums[i] = part if sums[i] is None else sums[i] + part
        gate = gate_ref[here, :]
        first = total * gate
        out_ref[here, :cols] = first.astype(NARROW)
        out_ref[here, cols:] = (total * z_ref[here, :] * (1.0 - gate)).astype(NARROW)
    for i in range(taps_count):
        grad_ref[i : i + 1, :] = jnp.sum(sums[i], axis=0, keepdims=True)


def mix_back(gyn, y, sums, pairs, gain, z, gate, taps, taps_count, width):
    rows, cols = z.shape
    n = cols // 4
    block = pl.BlockSpec((rows, n), lambda t: (0, t))
    row = pl.BlockSpec((1, n), lambda t: (0, t))
    lanes = whole((rows, LANES))
    tap_block = pl.BlockSpec((taps.shape[0], n), lambda t: (0, t))
    return pl.pallas_call(
        functools.partial(mix_back_body, taps_count, width),
        grid=(4,),
        in_specs=[block, block, lanes, lanes, lanes, lanes, row, block, block, tap_block],
        out_specs=[pl.BlockSpec((rows, 2 * n), lambda t: (0, t)), tap_block],
        out_shape=[sds((rows, 2 * cols), NARROW), sds(taps.shape, WIDE)],
        scratch_shapes=[pltpu.VMEM((rows + PAD, n), WIDE), pltpu.VMEM((rows + PAD, n), WIDE)],
        compiler_params=params(),
        cost_estimate=cost(4 * taps_count * rows * cols, 20 * rows * cols),
        name="mix_back",
    )(gyn, y, *sums, *pairs, gain, z, gate, taps)


def halve_body(groups, core_ref, *refs):
    count = sum(len(g) for g in groups)
    ins = list(refs[:count])
    keeps = refs[count : count + len(groups)]
    sends = refs[count + len(groups) :]
    low = core_ref[0] == 0
    for group, keep, send in zip(groups, keeps, sends):
        start = 0
        for n in group:
            ref = ins.pop(0)
            left, right = ref[:, :n], ref[:, n:]
            keep[:, start : start + n] = jnp.where(low, left, right)
            send[:, start : start + n] = jnp.where(low, right, left)
            start += n


def halve(groups, core):
    rows = groups[0][0].shape[0]
    halves = tuple(tuple(w.shape[1] // 2 for w in g) for g in groups)
    flat = [w for g in groups for w in g]
    shapes = [sds((rows, sum(h)), NARROW) for h in halves] * 2
    out = pl.pallas_call(
        functools.partial(halve_body, halves),
        grid_spec=pltpu.PrefetchScalarGridSpec(
            num_scalar_prefetch=1,
            grid=(1,),
            in_specs=[whole(w.shape) for w in flat],
            out_specs=[whole(s.shape) for s in shapes],
        ),
        out_shape=shapes,
        compiler_params=params(),
        cost_estimate=cost(0, 4 * sum(w.size for w in flat)),
        name="halve",
    )(core, *flat)
    return out[: len(groups)], out[len(groups) :]


def join_body(core_ref, keep_ref, came_ref, out_ref):
    low = core_ref[0] == 0
    rows = keep_ref.shape[0]
    keep, came = keep_ref[...], came_ref[...]
    out_ref[:rows, :] = jnp.where(low, keep, came)
    out_ref[rows:, :] = jnp.where(low, came, keep)


def join(keep, came, core):
    rows, cols = keep.shape
    return pl.pallas_call(
        join_body,
        grid_spec=pltpu.PrefetchScalarGridSpec(
            num_scalar_prefetch=1,
            grid=(1,),
            in_specs=[whole((rows, cols)), whole((rows, cols))],
            out_specs=whole((2 * rows, cols)),
        ),
        out_shape=sds((2 * rows, cols), keep.dtype),
        compiler_params=params(),
        cost_estimate=cost(0, 8 * rows * cols),
        name="join",
    )(core, keep, came)


def pack_body(lead, plan, core_ref, *refs):
    out_ref = refs[-1]
    low = core_ref[0] == 0
    out_ref[...] = jnp.zeros_like(out_ref)
    for ref, items in zip(refs[:-1], plan):
        for kind, src, dst in items:
            if kind == "once":
                v = ref[src : src + 1, :]
                out_ref[dst : dst + 1, :] = jnp.where(low, v, 0.0)
            elif kind == "all":
                out_ref[dst : dst + 8, :] = ref[...]
            elif kind == "taps":
                n = ref.shape[1] // 4
                for t in range(4):
                    v = ref[: src, t * n : (t + 1) * n]
                    out_ref[dst : dst + src, 2 * t * n : (2 * t + 1) * n] = jnp.where(low, v, 0.0)
                    out_ref[dst : dst + src, (2 * t + 1) * n : (2 * t + 2) * n] = jnp.where(low, 0.0, v)
            elif kind == "hidden":
                n = ref.shape[1] // 4
                for t in range(4):
                    v = ref[0:1, t * n : (t + 1) * n]
                    out_ref[dst + t : dst + t + 1, :n] = jnp.where(low, v, 0.0)
                    out_ref[dst + t : dst + t + 1, n:] = jnp.where(low, 0.0, v)
            else:
                row, first, step, n = src
                for t in range(4):
                    begin = t * step + first
                    v = ref[row : row + 1, begin : begin + n]
                    out_ref[dst : dst + 1, 2 * t * n : (2 * t + 1) * n] = jnp.where(low, v, 0.0)
                    out_ref[dst : dst + 1, (2 * t + 1) * n : (2 * t + 2) * n] = jnp.where(low, 0.0, v)


def pack(rows, width, core, sources):
    arrays = [a for a, _ in sources]
    plan = tuple(tuple(items) for _, items in sources)
    return pl.pallas_call(
        functools.partial(pack_body, rows, plan),
        grid_spec=pltpu.PrefetchScalarGridSpec(
            num_scalar_prefetch=1,
            grid=(1,),
            in_specs=[whole(a.shape) for a in arrays],
            out_specs=whole((rows, width)),
        ),
        out_shape=sds((rows, width), WIDE),
        compiler_params=params(),
        cost_estimate=cost(0, 8 * rows * width),
        name="pack",
    )(core, *arrays)


def on_device(planes, inputs, lengths, cotangent, *weights_and_rest):
    shards = weights_and_rest[:8]
    norm_gains, biases, kernel, distance_table = weights_and_rest[8:]
    batches, _, rows_here, width = inputs.shape
    parts = 4
    core = lax.axis_index("pair")
    plane = lax.axis_index("plane")
    part = lax.axis_index("tensor")
    quick = planes == PLANE_BLOCKS
    place = plane if quick else plane * 0
    p = place.astype(jnp.int32).reshape(1)

    def other_core(v):
        return lax.ppermute(v, "pair", [(0, 1), (1, 0)])

    def step_x(v):
        return lax.ppermute(v, "plane", [(i, i ^ 1) for i in range(planes)])

    def step_y(v):
        return lax.ppermute(v, "plane", [(i, i ^ 2) for i in range(planes)])

    def over_planes(v):
        if quick:
            return v + step_x(v) + step_y(v) + lax.ppermute(v, "plane", [(i, i ^ 3) for i in range(4)])
        bit = 1
        while bit < planes:
            v = v + lax.ppermute(v, "plane", [(i, i ^ bit) for i in range(planes)])
            bit *= 2
        return v

    def over_parts(v):
        def turn(k):
            return lax.ppermute(v, "tensor", [(i, i ^ k) for i in range(parts)])

        one, two, three = turn(1), turn(2), turn(3)
        return (v + one) + (two + three)

    def fence(*values):
        return lax.optimization_barrier(values) if quick else values

    def column_of(shard):
        return lax.all_gather(shard, "tensor", axis=0)

    def planes_of(column):
        every = lax.all_gather(column, "plane", axis=0)
        rows, cols = column.shape[1:]
        every = every.reshape(PLANE_BLOCKS, planes // PLANE_BLOCKS, parts, rows, cols)
        every = every.transpose(0, 2, 1, 3, 4).reshape(PLANE_BLOCKS, parts, -1, cols)
        return every[0], every[1], every[2], every[3, :2], every[3, 2:]

    def near(column):
        return step_x(column), step_y(column)

    def far(pair):
        return step_y(pair[0][:2]), step_x(pair[1][2:])

    def share(total):
        n = total.shape[0] // 2
        keep = lax.dynamic_slice_in_dim(total, core * n, n, 0)
        came = other_core(lax.dynamic_slice_in_dim(total, (1 - core) * n, n, 0))
        first = jnp.where(core == 0, keep, came).astype(WIDE)
        second = jnp.where(core == 0, came, keep).astype(WIDE)
        return first, second

    def tensor_sum(total):
        return lax.psum_scatter(total, "tensor", scatter_dimension=0)

    def hop1(grads):
        return (step_x(grads[1]), step_y(grads[3])) if quick else ()

    def hop2(grads, came):
        if not quick:
            return ()
        return step_y(add(grads[4], came[0][1])), step_x(add(grads[2], came[1][1]))

    def hop3(grads, came, last):
        own, sx, kx, sy, ky = grads
        if quick:
            return tensor_sum(combine(own, came[0], came[1], last[0], last[1]))
        blocks = [
            own,
            jnp.concatenate([sx[0], kx]),
            jnp.concatenate([ky, sy[0]]),
            jnp.concatenate([sx[1], sy[1]]),
        ]
        every = jnp.stack(blocks)
        rows = width // planes
        cols = own.shape[-1]
        every = every.reshape(PLANE_BLOCKS, parts, planes // PLANE_BLOCKS, rows, cols)
        every = every.transpose(0, 2, 1, 3, 4).reshape(planes, parts, rows, cols)
        return tensor_sum(lax.psum_scatter(every, "plane", scatter_dimension=0))

    def add(a, b):
        return (a.astype(WIDE) + b.astype(WIDE)).astype(NARROW)

    def rejoin(halves, start, cols, groups):
        pieces = [h[:, start : start + cols].reshape(h.shape[0], groups, -1) for h in halves]
        joined = jnp.concatenate(pieces, axis=2)
        return joined[:, 0] if groups == 1 else joined

    def spot(c, t):
        return c * parts + t

    def route(turn):
        pairs = []
        for c in range(2):
            for t in range(parts):
                mb = (turn + t) % 2
                pairs.append((spot(c, t), spot(t // 2, 2 * mb + c)))
        return pairs

    def bring(v):
        blocks = []
        for turn in range(2):
            mb = lax.rem(turn + part, 2)
            block = lax.dynamic_index_in_dim(v[:, 0], mb, 0, False)
            blocks.append(lax.ppermute(block, ("pair", "tensor"), route(turn)))
        return blocks

    def settle(blocks):
        swap = part // 2 == 1
        mine = jnp.concatenate(
            [jnp.where(swap, blocks[1], blocks[0]), jnp.where(swap, blocks[0], blocks[1])], axis=0
        )
        theirs = other_core(mine)
        return jnp.concatenate(
            [jnp.where(core == 0, mine, theirs), jnp.where(core == 0, theirs, mine)], axis=0
        )

    def send_home(v):
        half = v.shape[0] // 2
        mine = lax.dynamic_slice_in_dim(v, core * half, half, 0)
        first, second = mine[: half // 2], mine[half // 2 :]
        swap = part // 2 == 1
        blocks = [jnp.where(swap, second, first), jnp.where(swap, first, second)]
        came = []
        for turn in range(2):
            back = [(b, a) for a, b in route(turn)]
            came.append(lax.ppermute(blocks[turn], ("pair", "tensor"), back))
        odd = lax.rem(part, 2) == 1
        return jnp.stack([jnp.where(odd, came[1], came[0]), jnp.where(odd, came[0], came[1])])[:, None]

    (w_e1, w_r1, w_proj, w_merge, w_fe, w_fr, w_e2, w_r2) = shards
    core1 = core.astype(jnp.int32).reshape(1)
    ffc = w_e1.shape[1] // 2
    qc = w_proj.shape[2] // 2
    cc = w_fe.shape[2] // 2
    groups = [
        [w_e1],
        [w_r1],
        [w_proj[:, 0], w_proj[:, 1], w_proj[:, 2], w_merge],
        [w_fe[:, 0], w_fe[:, 1], w_fr, w_e2],
        [w_r2],
    ]
    keeps, sends = halve(groups, core1)
    pieces = fence(*[join(k, other_core(v), core1) for k, v in zip(keeps, sends)])

    gains = norm_gains.astype(WIDE)
    bias = biases.astype(WIDE)
    gain_row = lambda i: gains[i : i + 1]
    bias_row = lambda i: bias[i : i + 1]
    stride = w_e1.shape[1] * parts // width

    def pick(v):
        lead = v.shape[0]
        v = v.reshape(lead, parts, 2, -1)
        return lax.dynamic_index_in_dim(v, core, 2, False).reshape(lead, -1)

    hidden1 = pick(bias[11 : 11 + stride].reshape(1, -1))
    hidden2 = pick(bias[11 + stride : 11 + 2 * stride].reshape(1, -1))
    qb = pick(bias_row(6)).reshape(parts, 1, -1)
    vb = pick(bias_row(7)).reshape(parts, 1, -1)
    qkv_bias = jnp.concatenate([qb, jnp.zeros_like(qb), vb], axis=1).reshape(1, -1)
    taps_count = kernel.shape[0]
    taps = jnp.pad(pick(kernel.astype(WIDE)), ((0, PAD - taps_count), (0, 0)))
    depth_gain = pick(gain_row(3))
    depth_bias = pick(bias_row(3))
    buckets = distance_table.shape[0]
    table = jnp.pad(distance_table, ((0, NEAR - buckets), (0, 0)))

    pair_lengths = jnp.stack([lengths[:, 0], other_core(lengths[:, 0])])
    from_pair = jnp.bitwise_xor(lax.rem(part, 2), core)
    length = pair_lengths[from_pair, part // 2]
    rows_all = parts * inputs.shape[2]
    live = (jnp.arange(rows_all) < length).astype(WIDE)[:, None]

    col_e1 = column_of(pieces[0])
    r1c = column_of(pieces[1])
    attc = column_of(pieces[2])
    col_c = column_of(pieces[3])
    if quick:
        sd = pieces[4]
        sx, sy = step_x(sd), step_y(sd)
        sz = step_y(sx)
        col_e1, sx, sy, sz, source = fence(col_e1, sx, sy, sz, inputs)
        r2 = (column_of(jnp.stack([sd, sx, sy, sz])),) * PLANE_BLOCKS
        e1n, blocks = near(col_e1), bring(source)
        e1n, r1c, blocks = fence(e1n, r1c, blocks)
        e1f, r1n, x0 = far(e1n), near(r1c), settle(blocks)
        e1f, e1n, r1n, attc, x0 = fence(e1f, e1n, r1n, attc, x0)
        e1 = (col_e1, *e1n, *e1f)
        r1f, attn = far(r1n), near(attc)
    else:
        rows, cols = pieces[4].shape
        every = lax.all_gather(pieces[4], "plane", axis=0).reshape(PLANE_BLOCKS, -1, cols)
        r2 = (column_of(every),) * PLANE_BLOCKS
        x0 = settle(bring(inputs))
        e1 = planes_of(col_e1)
        r1 = planes_of(r1c)
        att = planes_of(attc)
        fil = planes_of(col_c[:, :, : 3 * cc])
        e2 = planes_of(col_c[:, :, 3 * cc :])
    x0 = x0.astype(WIDE)
    a1, u1, s1 = norm_expand("ff", x0, None, 0.5, gain_row(0), bias_row(0), e1, ffc, 0, p, hidden1)
    if quick:
        r1f, r1n, attn, s1 = fence(r1f, r1n, attn, s1)
        r1, attf = (r1c, *r1n, *r1f), far(attn)
    f1 = reduce_mm(s1, r1, ffc, 0, p, width)
    if quick:
        attf, attn, f1, col_c = fence(attf, attn, f1, col_c)
        att = (attc, *attn, *attf)
    f1o = other_core(f1)
    x1, bn, qkv = norm_expand(
        "qkv", x0, (f1, f1o, bias_row(9)), 0.5, gain_row(1), bias_row(1), att, 3 * qc, 0, p, qkv_bias
    )
    if quick:
        qkv, col_c = fence(qkv, col_c)
        filc, e2c = col_c[:, :, : 3 * cc], col_c[:, :, 3 * cc :]
        filn = near(filc)
    o, chances = attend(qkv, table, length.reshape(1))
    if quick:
        filn, o, e2c = fence(filn, o, e2c)
        filf, e2n = far(filn), near(e2c)
    f2 = reduce_mm(o, att, qc, 3, p, width)
    if quick:
        filf, filn, f2 = fence(filf, filn, f2)
        fil = (filc, *filn, *filf)
    f2o = other_core(f2)
    x2, cn, gate, z = norm_expand(
        "conv", x1, (f2, f2o, bias_row(8)), 1.0, gain_row(2), bias_row(2), fil, 2 * cc, 0, p, None
    )
    y, y_sums = causal_mix(z, taps, taps_count)
    if quick:
        e2n, y_sums, cot_source = fence(e2n, y_sums, cotangent)
        e2f = far(e2n)
        cot = bring(cot_source)
    y_sums = (y_sums, other_core(y_sums))
    f3, w = filter_out(y, y_sums, depth_gain, depth_bias, fil, cc, 2, p, width)
    if quick:
        e2f, cot, f3 = fence(e2f, cot, f3)
        cot = settle(cot)
        e2 = (e2c, *e2n, *e2f)
    else:
        cot = settle(bring(cotangent))
    f3o = other_core(f3)
    x3, a2, u2, s2 = norm_expand(
        "ff", x2, (f3, f3o, jnp.zeros((1, width), WIDE)), 1.0, gain_row(4), bias_row(4),
        e2, ffc, 0, p, hidden2,
    )
    f4 = reduce_mm(s2, r2, ffc, 0, p, width)
    out_rows, gx4, gf2, sums_final = final_norm(
        x3, f4, other_core(f4), bias_row(10), cot, live, gain_row(5), bias_row(5)
    )

    g_r2 = wgrad_flat(gf2, s2, p)
    g_r2, gf2 = fence(g_r2, gf2)
    z_r2 = tensor_sum(g_r2)
    gu2, gc2 = back_expand("ff", gf2, r2, ffc, 0, p, u2)
    g_e2 = wgrad([a2], [gu2], p)
    g_e2, gu2 = fence(g_e2, gu2)
    e2h1 = hop1(g_e2)
    b4 = reduce_mm(gu2, e2, ffc, 0, p, width)
    gx3, gw, sums3 = norm_back(1.0, x3, gx4, b4, other_core(b4), gain_row(4))
    gyn, depth_cols, depth_rows = filter_in(
        gw, y, y_sums, depth_gain, depth_bias, fil, cc, 2, p
    )
    depth_rows = (depth_rows, other_core(depth_rows))
    gg, taps_grad = mix_back(
        gyn, y, y_sums, depth_rows, depth_gain, z, gate, taps, taps_count, width
    )
    e2h1, gg = fence(e2h1, gg)
    e2h2 = hop2(g_e2, e2h1)
    g_fil = wgrad([cn, gw], [gg, w], p)
    filh1 = hop1(g_fil)
    b3 = reduce_mm(gg, fil, 2 * cc, 0, p, width)
    e2h2, b3, g_fil = fence(e2h2, b3, g_fil)
    z_e2 = hop3(g_e2, e2h1, e2h2)
    outputs = send_home(out_rows)
    gx2, gm, sums2 = norm_back(1.0, x2, gx3, b3, other_core(b3), gain_row(2))
    go = back_expand("low", gm, att, qc, 3, p)
    gqkv, gqkv_sums, table_grad = attend_back(qkv, go, chances, table)
    filh1, gqkv, outputs = fence(filh1, gqkv, outputs)
    filh2 = hop2(g_fil, filh1)
    g_att = wgrad([bn, gm], [gqkv, o], p)
    g_att, gqkv = fence(g_att, gqkv)
    atth1 = hop1(g_att)
    b2 = reduce_mm(gqkv, att, 3 * qc, 0, p, width)
    gx1, gf1, sums1 = norm_back(0.5, x1, gx2, b2, other_core(b2), gain_row(1))
    g_r1 = wgrad([gf1], [s1], p)

    table_rows = -(-buckets // 8)
    tail = jnp.transpose(table_grad[:HD])[1 : buckets - 1]
    ends = table_grad[HD : HD + 2, :HD]
    tail = jnp.concatenate([ends[:1], tail, ends[1:]], axis=0)
    tail = jnp.pad(tail, ((0, 8 * table_rows - buckets), (0, 0)))
    tail = tail.reshape(table_rows, 8, HD).transpose(1, 0, 2).reshape(8, table_rows * HD)
    tail = jnp.pad(tail, ((0, 0), (0, width - table_rows * HD)))
    early = pack(
        64, width, core1,
        [
            (sums_final, [("once", 0, 5), ("once", 1, 11), ("once", 2, 16)]),
            (sums3, [("once", 0, 4), ("once", 1, 10)]),
            (sums2, [("once", 0, 2), ("once", 1, 8), ("once", 2, 14)]),
            (sums1, [("once", 0, 1), ("once", 1, 7), ("once", 2, 15)]),
            (gqkv_sums, [("row", (0, 0, 3 * qc, qc), 12), ("row", (0, 2 * qc, 3 * qc, qc), 13)]),
            (depth_cols, [("row", (0, 0, cc, cc), 3), ("row", (1, 0, cc, cc), 9)]),
            (gc2, [("hidden", 0, 21)]),
            (taps_grad, [("taps", taps_count, 25)]),
            (tail, [("all", 0, 56)]),
        ],
    )
    filh2, g_r1, gf1, z_r2, early = fence(filh2, g_r1, gf1, z_r2, early)
    r1h1 = hop1(g_r1)
    z_fil = hop3(g_fil, filh1, filh2)
    half = early.shape[0] // 2
    mine = lax.dynamic_slice_in_dim(early, core * half, half, 0)
    theirs = lax.dynamic_slice_in_dim(early, (1 - core) * half, half, 0)
    gu1, gc1 = back_expand("ff", gf1, r1, ffc, 0, p, u1)
    g_e1 = wgrad([a1], [gu1], p)
    atth1, g_e1, gu1, z_e2, mine = fence(atth1, g_e1, gu1, z_e2, mine)
    atth2 = hop2(g_att, atth1)
    e1h1 = hop1(g_e1)
    early = mine + other_core(theirs)
    b1 = reduce_mm(gu1, e1, ffc, 0, p, width)
    r1h1, atth2, b1 = fence(r1h1, atth2, b1)
    r1h2 = hop2(g_r1, r1h1)
    z_att = hop3(g_att, atth1, atth2)
    gx0, _, sums0 = norm_back(1.0, x0, gx1, b1, other_core(b1), gain_row(0))
    late = pack(
        8, width, core1,
        [(sums0, [("once", 0, 0), ("once", 1, 1)]), (gc1, [("hidden", 0, 2)])],
    )
    e1h1, gx0, late, z_fil = fence(e1h1, gx0, late, z_fil)
    e1h2 = hop2(g_e1, e1h1)
    homeward = send_home(gx0.astype(NARROW))
    late = late + other_core(late)
    early = over_planes(early)
    r1h2, early, late = fence(r1h2, early, late)
    z_r1 = hop3(g_r1, r1h1, r1h2)
    late = over_planes(late)
    e1h2, late, early = fence(e1h2, late, early)
    z_e1 = hop3(g_e1, e1h1, e1h2)
    early, late = over_parts(early), over_parts(late)
    early_other = other_core(early)
    early = jnp.concatenate(
        [jnp.where(core == 0, early, early_other), jnp.where(core == 0, early_other, early)], axis=0
    )
    input_grad = homeward.astype(WIDE)
    if quick:
        rx = step_x(z_r2[1::2])
        ry = step_y(add(z_r2[2], rx[1]))
        z_r2 = (z_r2[0].astype(WIDE) + rx[0].astype(WIDE) + ry.astype(WIDE)).astype(NARROW)
    else:
        z_r2 = lax.psum_scatter(
            z_r2.reshape(planes, -1, z_r2.shape[-1]), "plane", scatter_dimension=0
        )
    e1_grad, r1_grad, att_grad, fil_grad, e2_grad, r2_grad = [
        share(v) for v in (z_e1, z_r1, z_att, z_fil, z_e2, z_r2)
    ]

    gains_grad = jnp.concatenate([late[0:1], early[1:6]], axis=0)
    bias_grad = jnp.concatenate([late[1:2], early[7:17], late[2:6], early[21:25]], axis=0)
    taps_t = early[25 : 25 + taps_count]
    table_t = early[56:64, : table_rows * HD].reshape(8, table_rows, HD).transpose(1, 0, 2)
    table_t = table_t.reshape(8 * table_rows, HD)[:buckets]
    return (
        outputs,
        input_grad,
        rejoin(e1_grad, 0, ffc, 1),
        rejoin(r1_grad, 0, ffc, 1),
        rejoin(att_grad, 0, 3 * qc, 3),
        rejoin(att_grad, 3 * qc, qc, 1),
        rejoin(fil_grad, 0, 2 * cc, 2),
        rejoin(fil_grad, 2 * cc, cc, 1),
        rejoin(e2_grad, 0, ffc, 1),
        rejoin(r2_grad, 0, ffc, 1),
        gains_grad,
        bias_grad,
        taps_t,
        table_t,
    )


def solution(mesh):
    dp = mesh.shape["dp"]
    tensor = mesh.shape["tensor"]
    split = Mesh(mesh.devices.reshape(dp // 2, 2, tensor), ("plane", "pair", "tensor"))
    both = ("plane", "pair")
    rows = P(None, both, "tensor", None)
    flat = P(both, "tensor")
    deep = P(both, None, "tensor")
    weights = (flat, flat, deep, flat, deep, flat, flat, flat)
    small = (P(), P(), P(), P())
    return jax.shard_map(
        functools.partial(on_device, dp // 2),
        mesh=split,
        in_specs=(rows, P(None, both), rows, *weights, *small),
        out_specs=(rows, rows, *weights, *small),
        check_vma=False,
    )
```

time: 1920 us -> 714 us (0.37)
  waiting for transfers between devices: 1280 us -> 198 us
  Pallas kernels: 0 us -> 243 us
  matrix products: 173 us -> 0 us
  local copies, waits for them, and re-layouts: 244 us -> 95.7 us
  starting transfers between devices: 3.47 us -> 101 us
  blocking collectives: 84 us -> 0 us
  other arithmetic: 110 us -> 52.7 us
    reduce_scatter x24 -> x6, waiting for transfers between devices: 611 us -> 4.3 us  [tensor_sum(): return lax.psum_scatter(total, 'tensor', scatter_dimension=0)]
    all_gather x22 -> x5, waiting for transfers between devices: 532 us -> 59.1 us  [column_of(): return lax.all_gather(shard, 'tensor', axis=0)]
    pallas_call x0 -> x44, Pallas kernels: none -> 243 us  [the longest x7 38 us: reduce_mm(): pl.pallas_call(functools.partial(reduce_body, len(w)), grid_spec=pltpu.Pr...]
    dot_general x66 -> x0, matrix products: 173 us -> none  [the longest x12 36.3 us: contract_rows(): lax.dot_general(left_side, right_side, (((0,), (0,)), ((), ())), preferre...]
    ppermute x0 -> x92, waiting for transfers between devices: none -> 133 us  [the longest x24 48.6 us: step_x(): return lax.ppermute(v, 'plane', [(i, i ^ 1) for i in range(planes)])]
    psum x1 -> x0, waiting for transfers between devices: 130 us -> none  [on_device(): lax.psum((gain_total, bias_total, kernel_full, distance_total), ('dp', 't...]
    ppermute x0 -> x92, starting transfers between devices: none -> 100 us  [the longest x25 27.8 us: step_y(): return lax.ppermute(v, 'plane', [(i, i ^ 2) for i in range(planes)])]
    psum x3 -> x0, blocking collectives: 62.5 us -> none  [the longest x1 40.3 us: on_device(): lax.psum((gain_total, bias_total, kernel_full, distance_total), ('dp', 't...]
  transfers between devices with their start and end apart: 47 -> 103, of which waited for: 42 -> 38; matrix products, arithmetic and copies ran while one was open for 16% -> 12% of each run, Pallas kernels for 0% -> 32%
where the time goes in v1:
time: 714 us; the launch traced here: 707 us
  Pallas kernels  243 us (34%)
  waiting for transfers between devices  198 us (28%)
  starting transfers between devices  101 us (14%)
  local copies, waits for them, and re-layouts  95.7 us (13%)
  other arithmetic  52.7 us (7%)
  between operations  15.9 us (2%)
    unnamed x344, local copies, waits for them, and re-layouts  64.6 us
    all_gather x5, waiting for transfers between devices, column_of(): return lax.all_gather(shard, 'tensor', axis=0)  59.1 us
    ppermute x24, waiting for transfers between devices, step_x(): return lax.ppermute(v, 'plane', [(i, i ^ 1) for i in range(planes)])  48.6 us
    pallas_call x7, Pallas kernels, reduce_mm(): pl.pallas_call(functools.partial(reduce_body, len(w)), grid_spec=pltpu.Pr...  38 us
    ppermute x25, waiting for transfers between devices, step_y(): return lax.ppermute(v, 'plane', [(i, i ^ 2) for i in range(planes)])  36.5 us
    pallas_call x4, Pallas kernels, norm_expand(): pl.pallas_call(functools.partial(expand_body, kind, merged, scale, len(w)...  35.4 us
    pallas_call x5, Pallas kernels, wgrad(): pl.pallas_call(functools.partial(wgrad_body, len(xs)), grid_spec=pltpu.Pr...  30.3 us
    ppermute x25, starting transfers between devices, step_y(): return lax.ppermute(v, 'plane', [(i, i ^ 2) for i in range(planes)])  27.8 us
  transfers between devices with their start and end apart: 103, of which 38 were waited for; matrix products, arithmetic and copies ran while one was open for 12% of the time, Pallas kernels for 32%

profile of v1, /device:TPU:0, one launch (start us, length us, event | category | flops | bytes accessed | tf_op | source)
XLA Modules:
  0.0 706.5 jit_solution(12597273843157202749)
XLA Ops:
  38.9 11.7 %all-gather.11.cloned.1.call-done = bf16[1024,512]{1,0:T(8,128)(2,1)} async-done(((bf16[256,512]{1,0:T(8,128)(2,1)}), bf16[1024,512]{1,0:T(8,128)(2,1)}) %all-gather.11.cloned.1.call-update) | async-done | bytes 1048592 | tf_op jit(solution)/shard_map/all_gather | solution.py:1056
  57.3 28.6 %all-gather.13.cloned.1.call-done = bf16[1024,512]{1,0:T(8,128)(2,1)} async-done(((bf16[256,512]{1,0:T(8,128)(2,1)}), bf16[1024,512]{1,0:T(8,128)(2,1)}) %all-gather.13.cloned.1.call-update) | async-done | bytes 1048592 | tf_op jit(solution)/shard_map/all_gather | solution.py:1056
  96.9 18.8 %all-gather.15.cloned.1.call-done = bf16[1024,512]{1,0:T(8,128)(2,1)} async-done(((bf16[256,512]{1,0:T(8,128)(2,1)}), bf16[1024,512]{1,0:T(8,128)(2,1)}) %all-gather.15.cloned.1.call-update) | async-done | bytes 1048592 | tf_op jit(solution)/shard_map/all_gather | solution.py:1056
  115.7 7.9 %collective-permute-done.13.refs_7_.refs_4_ = bf16[2,256,512]{2,1,0:T(8,128)(2,1)} collective-permute-done((bf16[2,256,512]{2,1,0:T(8,128)(2,1)}, bf16[2,256,512]{2,1,0:T(8,128)(2,1)}, u32[]{:S(2)}, u32[]{:S(2)}) %collective-permute-start.13) | collective-permute-done | bytes 524320 | tf_op jit(solution)/shard_map/ppermute | solution.py:1031
  138.0 8.6 %norm_expand_ff.2 = (bf16[512,1024]{1,0:T(8,128)(2,1)S(1)}, f32[512,2048]{1,0:T(8,128)}, bf16[512,2048]{1,0:T(8,128)(2,1)}) custom-call(s32[1]{0:T(128)} %bitcast.p_ref, f32[512,1024]{1,0:T(8,128)} %convert_element_type.210.refs_0_.x_ref, f32[1,1024]{1,0:T(1,128)S(1)} %get-tuple-element.523.refs_1_.g_ref, f32[1,1024]{1,0:T(1,128)S(1)} %get-tuple-element.513.refs_2_, ...), custom_call_target="tpu_custom_call" | custom-call | flops 1073741 | bytes 5242 | tf_op jit(solution)/shard_map/norm_expand_ff/pallas_call | solution.py:166
  146.7 15.4 %collective-permute-done.18.refs_4_ = bf16[2,256,512]{2,1,0:T(8,128)(2,1)S(1)} collective-permute-done((bf16[2,256,512]{2,1,0:T(8,128)(2,1)S(1)}, bf16[2,256,512]{2,1,0:T(8,128)(2,1)S(1)}, u32[]{:S(2)}, u32[]{:S(2)}) %collective-permute-start.18) | collective-permute-done | bytes 524320 | tf_op jit(solution)/shard_map/ppermute | solution.py:1031
  180.3 8.7 %norm_expand_qkv.1 = (f32[512,1024]{1,0:T(8,128)}, bf16[512,1024]{1,0:T(8,128)(2,1)S(1)}, bf16[512,1536]{1,0:T(8,128)(2,1)}) custom-call(s32[1]{0:T(128)} %bitcast.p_ref, f32[512,1024]{1,0:T(8,128)} %convert_element_type.210.refs_0_.x_ref, bf16[512,1024]{1,0:T(8,128)(2,1)S(1)} %copy-done.38, bf16[512,1024]{1,0:T(8,128)(2,1)S(1)} %collective-permute-done.23.refs_2_, ...), custom_call_target="tpu_custom_call" | custom-call | flops 805306 | bytes 4718 | tf_op jit(solution)/shard_map/norm_expand_qkv/pallas_call | solution.py:166
  194.6 17.8 %attend.1 = (bf16[512,512]{1,0:T(8,128)(2,1)S(1)}, bf16[8,512,512]{2,1,0:T(8,128)(2,1)}) custom-call(s32[1]{0:T(128)} %bitcast.21.len_ref, bf16[512,1536]{1,0:T(8,128)(2,1)S(1)} %copy-done.20, bf16[128,64]{1,0:T(8,128)(2,1)S(1)} %pad.16.table_ref), custom_call_target="tpu_custom_call" | custom-call | flops 268435 | bytes 2621 | tf_op jit(solution)/shard_map/attend/pallas_call | solution.py:560
  234.5 8.0 %norm_expand_conv.1 = (f32[512,1024]{1,0:T(8,128)}, bf16[512,1024]{1,0:T(8,128)(2,1)S(1)}, f32[512,512]{1,0:T(8,128)S(1)}, f32[512,512]{1,0:T(8,128)}) custom-call(s32[1]{0:T(128)} %bitcast.p_ref, f32[512,1024]{1,0:T(8,128)} %get-tuple-element.260.refs_0_.x_ref, bf16[512,1024]{1,0:T(8,128)(2,1)} %reduce_mm.8.refs_1_, ...), custom_call_target="tpu_custom_call" | custom-call | flops 536870 | bytes 4194 | tf_op jit(solution)/shard_map/norm_expand_conv/pallas_call | solution.py:166
  249.8 6.6 collective-permute-done.31.refs_8_.refs_2_
  286.1 10.1 %norm_expand_ff.3 = (f32[512,1024]{1,0:T(8,128)}, bf16[512,1024]{1,0:T(8,128)(2,1)S(1)}, f32[512,2048]{1,0:T(8,128)}, bf16[512,2048]{1,0:T(8,128)(2,1)}) custom-call(s32[1]{0:T(128)} %bitcast.p_ref, f32[512,1024]{1,0:T(8,128)} %get-tuple-element.275.refs_0_.x_ref, bf16[512,1024]{1,0:T(8,128)(2,1)} %get-tuple-element.285.refs_1_, ...), custom_call_target="tpu_custom_call" | custom-call | flops 1073741 | bytes 5242 | tf_op jit(solution)/shard_map/norm_expand_ff/pallas_call | solution.py:166
  308.3 7.4 %final_norm.1 = (bf16[512,1024]{1,0:T(8,128)(2,1)S(1)}, f32[512,1024]{1,0:T(8,128)}, bf16[512,1024]{1,0:T(8,128)(2,1)S(1)}, f32[8,1024]{1,0:T(8,128)S(1)}) custom-call(f32[512,1024]{1,0:T(8,128)} %get-tuple-element.288.x_ref, bf16[512,1024]{1,0:T(8,128)(2,1)S(1)} %reduce_mm.9.pa_ref, bf16[512,1024]{1,0:T(8,128)(2,1)S(1)} %collective-permute-done.38.pb_ref, ...), custom_call_target="tpu_custom_call" | custom-call | flops 6291 | bytes 4718 | tf_op jit(solution)/shard_map/final_norm/pallas_call | solution.py:489
  323.9 6.7 back_expand_ff.2
  361.0 8.8 %mix_back.1 = (bf16[512,1024]{1,0:T(8,128)(2,1)S(1)}, f32[32,512]{1,0:T(8,128)S(1)}) custom-call(f32[512,512]{1,0:T(8,128)S(1)} %get-tuple-element.310.gyn_ref, f32[512,512]{1,0:T(8,128)S(1)} %copy-done.8, f32[512,128]{1,0:T(8,128)S(1)} %get-tuple-element.283.sa_ref, f32[512,128]{1,0:T(8,128)S(1)} %copy-done.44, f32[512,128]{1,0:T(8,128)S(1)} %get-tuple-element.311.ra_ref, ...), custom_call_target="tpu_custom_call" | custom-call | flops 16252 | bytes 2621 | tf_op jit(solution)/shard_map/mix_back/pallas_call | solution.py:890
  395.1 7.2 %collective-permute-done.49 = bf16[128,1024]{1,0:T(8,128)(2,1)} collective-permute-done((bf16[128,1024]{1,0:T(8,128)(2,1)}, bf16[128,1024]{1,0:T(8,128)(2,1)}, u32[]{:S(2)}, u32[]{:S(2)}) %collective-permute-start.49) | collective-permute-done | bytes 262176 | tf_op jit(solution)/shard_map/ppermute | solution.py:1153
  404.2 6.5 norm_back.5
  416.4 25.2 %attend_back.1 = (bf16[512,1536]{1,0:T(8,128)(2,1)S(1)}, f32[1,1536]{1,0:T(1,128)S(1)}, f32[72,128]{1,0:T(8,128)S(1)}) custom-call(bf16[512,1536]{1,0:T(8,128)(2,1)S(1)} %copy-done.21, bf16[512,512]{1,0:T(8,128)(2,1)S(1)} %back_expand_low.1.go_ref, bf16[8,512,512]{2,1,0:T(8,128)(2,1)} %get-tuple-element.328.p_ref, bf16[128,64]{1,0:T(8,128)(2,1)S(1)} %copy-done.104), custom_call_target="tpu_custom_call" | custom-call | flops 671088 | bytes 2621 | tf_op jit(solution)/shard_map/attend_back/pallas_call | solution.py:666
  442.8 7.1 %wgrad.7 = (bf16[4,256,512]{2,1,0:T(8,128)(2,1)S(1)}, bf16[2,2,256,512]{3,2,1,0:T(8,128)(2,1)S(1)}, bf16[2,256,512]{2,1,0:T(8,128)(2,1)S(1)}, bf16[2,2,256,512]{...) custom-call(s32[1]{0:T(128)} %bitcast.p_ref, bf16[512,1024]{1,0:T(8,128)(2,1)S(1)} %copy-done.66, bf16[512,1024]{1,0:T(8,128)(2,1)} %copy-done.31, ...), custom_call_target="tpu_custom_call" | custom-call | flops 1073741 | bytes 3145 | tf_op jit(solution)/shard_map/wgrad/pallas_call | solution.py:333
  491.6 8.4 %collective-permute-done.53.fx_ref = bf16[2,256,384]{2,1,0:T(8,128)(2,1)} collective-permute-done((bf16[2,256,384]{2,1,0:T(8,128)(2,1)}, bf16[2,256,384]{2,1,0:T(8,128)(2,1)}, u32[]{:S(2)}, u32[]{:S(2)}) %collective-permute-start.53) | collective-permute-done | bytes 393248 | tf_op jit(solution)/shard_map/ppermute | solution.py:1034
  511.3 6.7 back_expand_ff.3
  560.2 21.8 %collective-permute-done.72 = f32[32,1024]{1,0:T(8,128)} collective-permute-done((f32[32,1024]{1,0:T(8,128)S(1)}, f32[32,1024]{1,0:T(8,128)}, u32[]{:S(2)}, u32[]{:S(2)}) %collective-permute-start.72) | collective-permute-done | bytes 131104 | tf_op jit(solution)/shard_map/ppermute | solution.py:1038
  594.8 7.0 norm_back.7
  611.4 6.6 collective-permute-done.67.fx_ref
  644.4 6.7 collective-permute-done.66.fy_ref
  (711 shorter events, 422.5 us)
Async XLA Ops:
  7.2 43.5 %all-gather.11.cloned.1.call-start = ((), (), s32[]{:S(2)}) async-start(), calls=%async_computation.12 | async-start | bytes 1310720 | tf_op jit(solution)/shard_map/all_gather | solution.py:1056
  20.0 65.9 %all-gather.13.cloned.1.call-start = ((), (), s32[]{:S(2)}) async-start(), calls=%async_computation.13 | async-start | bytes 1310720 | tf_op jit(solution)/shard_map/all_gather | solution.py:1056
  20.7 95.0 %all-gather.15.cloned.1.call-start = ((), (), s32[]{:S(2)}) async-start(), calls=%async_computation.14 | async-start | bytes 1310720 | tf_op jit(solution)/shard_map/all_gather | solution.py:1056
  21.5 150.8 %all-gather.17.cloned.1.call-start = ((), (), s32[]{:S(2)}) async-start(), calls=%async_computation.15 | async-start | bytes 2293760 | tf_op jit(solution)/shard_map/all_gather | solution.py:1056
  32.8 264.3 %all-gather.19.cloned.1.call-start = ((), (), s32[]{:S(2)}) async-start(), calls=%async_computation.16 | async-start | bytes 5242880 | tf_op jit(solution)/shard_map/all_gather | solution.py:1056
  50.6 35.3 %collective-permute-start.9 = (bf16[4,256,512]{2,1,0:T(8,128)(2,1)}, bf16[4,256,512]{2,1,0:T(8,128)(2,1)S(1)}, u32[]{:S(2)}, u32[]{:S(2)}) collective-permute-start(bf16[4,256,512]{2,1,0:T(8,128)(2,1)} %bitcast.201), channel_id=1, source_target_pairs={{0,16},{8,24},{16,0},{24,8},{1,17},{9,25},{17,1},{25,9},{2,18},{10... | collective-permute-start | bytes 3145736 | tf_op jit(solution)/shard_map/ppermute | solution.py:1034
  86.7 37.7 %collective-permute-start.15 = (bf16[4,256,512]{2,1,0:T(8,128)(2,1)}, bf16[4,256,512]{2,1,0:T(8,128)(2,1)S(1)}, u32[]{:S(2)}, u32[]{:S(2)}) collective-permute-start(bf16[4,256,512]{2,1,0:T(8,128)(2,1)} %bitcast.205), channel_id=1, source_target_pairs={{0,16},{8,24},{16,0},{24,8},{1,17},{9,25},{17,1},{25,9},{2,18},{10... | collective-permute-start | bytes 3145736 | tf_op jit(solution)/shard_map/ppermute | solution.py:1034
  87.3 37.2 %collective-permute-start.14 = (bf16[4,256,512]{2,1,0:T(8,128)(2,1)}, bf16[4,256,512]{2,1,0:T(8,128)(2,1)}, u32[]{:S(2)}, u32[]{:S(2)}) collective-permute-start(bf16[4,256,512]{2,1,0:T(8,128)(2,1)} %bitcast.206), channel_id=1, source_target_pairs={{0,8},{8,0},{16,24},{24,16},{1,9},{9,1},{17,25},{25,17},{2,10},{10... | collective-permute-start | bytes 3145736 | tf_op jit(solution)/shard_map/ppermute | solution.py:1031
  125.5 36.6 %collective-permute-start.20 = (bf16[4,256,512]{2,1,0:T(8,128)(2,1)}, bf16[4,256,512]{2,1,0:T(8,128)(2,1)S(1)}, u32[]{:S(2)}, u32[]{:S(2)}) collective-permute-start(bf16[4,256,512]{2,1,0:T(8,128)(2,1)} %bitcast.195), channel_id=1, source_target_pairs={{0,16},{8,24},{16,0},{24,8},{1,17},{9,25},{17,1},{25,9},{2,18},{10... | collective-permute-start | bytes 3145736 | tf_op jit(solution)/shard_map/ppermute | solution.py:1034
  126.9 35.1 %collective-permute-start.19 = (bf16[4,256,512]{2,1,0:T(8,128)(2,1)}, bf16[4,256,512]{2,1,0:T(8,128)(2,1)S(1)}, u32[]{:S(2)}, u32[]{:S(2)}) collective-permute-start(bf16[4,256,512]{2,1,0:T(8,128)(2,1)} %bitcast.196), channel_id=1, source_target_pairs={{0,8},{8,0},{16,24},{24,16},{1,9},{9,1},{17,25},{25,17},{2,10},{10... | collective-permute-start | bytes 3145736 | tf_op jit(solution)/shard_map/ppermute | solution.py:1031
  129.7 370.3 %reduce-scatter.7.cloned.1.call-start = ((), (), s32[]{:S(2)}) async-start(), calls=%async_computation.6 | async-start | bytes 5242880 | tf_op jit(solution)/shard_map/reduce_scatter | solution.py:1080
  322.6 204.2 %reduce-scatter.9.cloned.1.call-start = ((), (), s32[]{:S(2)}) async-start(), calls=%async_computation.7 | async-start | bytes 1310720 | tf_op jit(solution)/shard_map/reduce_scatter | solution.py:1080
  390.5 217.9 %reduce-scatter.11.cloned.1.call-start = ((), (), s32[]{:S(2)}) async-start(), calls=%async_computation.8 | async-start | bytes 983040 | tf_op jit(solution)/shard_map/reduce_scatter | solution.py:1080
  390.5 52.3 %collective-permute-start.44 = (bf16[2,2,256,384]{3,2,1,0:T(8,128)(2,1)}, bf16[2,2,256,384]{3,2,1,0:T(8,128)(2,1)S(1)}, u32[]{:S(2)}, u32[]{:S(2)}) collective-permute-start(bf16[2,2,256,384]{3,2,1,0:T(8,128)(2,1)} %copy-done.140), channel_id=1, source_target_pairs={{0,8},{8,0},{16,24},{24,16},{1,9},{9,1},{17,25},{25,17},{2,10},{10... | collective-permute-start | bytes 2359304 | tf_op jit(solution)/shard_map/ppermute | solution.py:1031
  391.1 51.7 %collective-permute-start.45 = (bf16[2,2,256,384]{3,2,1,0:T(8,128)(2,1)}, bf16[2,2,256,384]{3,2,1,0:T(8,128)(2,1)}, u32[]{:S(2)}, u32[]{:S(2)}) collective-permute-start(bf16[2,2,256,384]{3,2,1,0:T(8,128)(2,1)} %copy-done.139), channel_id=1, source_target_pairs={{0,16},{8,24},{16,0},{24,8},{1,17},{9,25},{17,1},{25,9},{2,18},{10... | collective-permute-start | bytes 2359304 | tf_op jit(solution)/shard_map/ppermute | solution.py:1034
  466.3 60.5 %collective-permute-start.51 = (bf16[2,2,256,512]{3,2,1,0:T(8,128)(2,1)}, bf16[2,2,256,512]{3,2,1,0:T(8,128)(2,1)}, u32[]{:S(2)}, u32[]{:S(2)}) collective-permute-start(bf16[2,2,256,512]{3,2,1,0:T(8,128)(2,1)} %copy-done.136), channel_id=1, source_target_pairs={{0,8},{8,0},{16,24},{24,16},{1,9},{9,1},{17,25},{25,17},{2,10},{10... | collective-permute-start | bytes 3145736 | tf_op jit(solution)/shard_map/ppermute | solution.py:1031
  466.7 60.1 %collective-permute-start.52 = (bf16[2,2,256,512]{3,2,1,0:T(8,128)(2,1)}, bf16[2,2,256,512]{3,2,1,0:T(8,128)(2,1)}, u32[]{:S(2)}, u32[]{:S(2)}) collective-permute-start(bf16[2,2,256,512]{3,2,1,0:T(8,128)(2,1)} %copy-done.135), channel_id=1, source_target_pairs={{0,16},{8,24},{16,0},{24,8},{1,17},{9,25},{17,1},{25,9},{2,18},{10... | collective-permute-start | bytes 3145736 | tf_op jit(solution)/shard_map/ppermute | solution.py:1034
  506.2 177.0 %reduce-scatter.17.cloned.1.call-start = ((), (), s32[]{:S(2)}) async-start(), calls=%async_computation.11 | async-start | bytes 1310720 | tf_op jit(solution)/shard_map/reduce_scatter | solution.py:1080
  507.2 41.9 %collective-permute-start.58 = (bf16[2,2,256,512]{3,2,1,0:T(8,128)(2,1)}, bf16[2,2,256,512]{3,2,1,0:T(8,128)(2,1)}, u32[]{:S(2)}, u32[]{:S(2)}) collective-permute-start(bf16[2,2,256,512]{3,2,1,0:T(8,128)(2,1)} %copy-done.138), channel_id=1, source_target_pairs={{0,8},{8,0},{16,24},{24,16},{1,9},{9,1},{17,25},{25,17},{2,10},{10... | collective-permute-start | bytes 3145736 | tf_op jit(solution)/shard_map/ppermute | solution.py:1031
  508.8 41.6 %collective-permute-start.59 = (bf16[2,2,256,512]{3,2,1,0:T(8,128)(2,1)}, bf16[2,2,256,512]{3,2,1,0:T(8,128)(2,1)}, u32[]{:S(2)}, u32[]{:S(2)}) collective-permute-start(bf16[2,2,256,512]{3,2,1,0:T(8,128)(2,1)} %copy-done.137), channel_id=1, source_target_pairs={{0,16},{8,24},{16,0},{24,8},{1,17},{9,25},{17,1},{25,9},{2,18},{10... | collective-permute-start | bytes 3145736 | tf_op jit(solution)/shard_map/ppermute | solution.py:1034
  545.7 57.4 %collective-permute-start.56 = (bf16[2,2,256,512]{3,2,1,0:T(8,128)(2,1)}, bf16[2,2,256,512]{3,2,1,0:T(8,128)(2,1)}, u32[]{:S(2)}, u32[]{:S(2)}) collective-permute-start(bf16[2,2,256,512]{3,2,1,0:T(8,128)(2,1)} %get-tuple-element.376), channel_id=1, source_target_pairs={{0,8},{8,0},{16,24},{24,16},{1,9},{9,1},{17,25},{25,17},{2,10},{10... | collective-permute-start | bytes 3145736 | tf_op jit(solution)/shard_map/ppermute | solution.py:1031
  547.3 34.7 %collective-permute-start.72 = (f32[32,1024]{1,0:T(8,128)S(1)}, f32[32,1024]{1,0:T(8,128)}, u32[]{:S(2)}, u32[]{:S(2)}) collective-permute-start(f32[32,1024]{1,0:T(8,128)S(1)} %add.182), channel_id=1, source_target_pairs={{0,24},{8,16},{16,8},{24,0},{1,25},{9,17},{17,9},{25,1},{2,26},{10... | collective-permute-start | bytes 393224 | tf_op jit(solution)/shard_map/ppermute | solution.py:1038
  554.7 133.2 %reduce-scatter.15.cloned.1.call-start = ((), (), s32[]{:S(2)}) async-start(), calls=%async_computation.10 | async-start | bytes 1310720 | tf_op jit(solution)/shard_map/reduce_scatter | solution.py:1080
  624.6 70.5 %reduce-scatter.13.cloned.1.call-start = ((), (), s32[]{:S(2)}) async-start(), calls=%async_computation.9 | async-start | bytes 1310720 | tf_op jit(solution)/shard_map/reduce_scatter | solution.py:1080
  (248 other events, 2260.7 us)
Sparse Core Ops, SparseCore 0:
  20.1 30.4 all-gather.10
  52.8 33.0 all-gather.12
  88.1 27.6 all-gather.14
  117.7 40.8 all-gather.16
  160.1 79.6 all-gather.18
  322.7 75.3 reduce-scatter.6
  400.6 29.9 reduce-scatter.8
  506.3 24.6 reduce-scatter.10
  554.8 27.8 reduce-scatter.16
  624.7 31.7 reduce-scatter.14
  670.1 24.9 reduce-scatter.12

commit v2 on v1

--- a/solution.py
+++ b/solution.py
@@ -358,35 +358,42 @@
     )(p, *xs, *ss)
 
 
-def wgrad_flat_body(p_ref, x_ref, s_ref, out_ref):
+def wgrad_flat_body(count, p_ref, *refs):
     p = p_ref[0]
-    width = x_ref.shape[1] // PLANE_BLOCKS
+    out_ref = refs[-1]
     for r in range(PLANE_BLOCKS):
-        out_ref[0, r] = lax.dot_general(
-            x_ref[:, rel_cols(p, r, width)],
-            s_ref[...],
-            (((0,), (0,)), ((), ())),
-            preferred_element_type=WIDE,
-        ).astype(NARROW)
-
-
-def wgrad_flat(x, s, p):
-    rows, width = x.shape
+        start = 0
+        for x_ref, s_ref in zip(refs[:count], refs[count : 2 * count]):
+            width = x_ref.shape[1] // PLANE_BLOCKS
+            cols = s_ref.shape[1]
+            out_ref[0, r, :, start : start + cols] = lax.dot_general(
+                x_ref[:, rel_cols(p, r, width)],
+                s_ref[...],
+                (((0,), (0,)), ((), ())),
+                preferred_element_type=WIDE,
+            ).astype(NARROW)
+            start += cols
+
+
+def wgrad_flat(xs, ss, p):
+    rows, width = xs[0].shape
     wrows = width // PLANE_BLOCKS
-    cols = s.shape[1] // 4
-    return pl.pallas_call(
-        wgrad_flat_body,
+    widths = [s.shape[1] // 4 for s in ss]
+    cols = sum(widths)
+    return pl.pallas_call(
+        functools.partial(wgrad_flat_body, len(xs)),
         grid_spec=pltpu.PrefetchScalarGridSpec(
             num_scalar_prefetch=1,
             grid=(4,),
-            in_specs=[whole((rows, width)), pl.BlockSpec((rows, cols), lambda t, p: (0, t))],
+            in_specs=[whole((rows, width)) for _ in xs]
+            + [pl.BlockSpec((rows, c), lambda t, p: (0, t)) for c in widths],
             out_specs=pl.BlockSpec((1, PLANE_BLOCKS, wrows, cols), lambda t, p: (t, 0, 0, 0)),
         ),
         out_shape=sds((4, PLANE_BLOCKS, wrows, cols), NARROW),
         compiler_params=params(),
         cost_estimate=cost(2 * rows * width * 4 * cols, 8 * width * cols + 4 * rows * width),
         name="wgrad_flat",
-    )(p, x, s)
+    )(p, *xs, *ss)
 
 
 def combine_body(own_ref, rx_ref, ry_ref, fx_ref, fy_ref, out_ref):
@@ -1079,6 +1086,19 @@
     def tensor_sum(total):
         return lax.psum_scatter(total, "tensor", scatter_dimension=0)
 
+    def across_x(every):
+        return step_x(every[1::2]) if quick else ()
+
+    def across_y(every, rx):
+        return step_y(add(every[2], rx[1])) if quick else ()
+
+    def across_end(every, rx, ry):
+        if quick:
+            return (every[0].astype(WIDE) + rx[0].astype(WIDE) + ry.astype(WIDE)).astype(NARROW)
+        return lax.psum_scatter(
+            every.reshape(planes, -1, every.shape[-1]), "plane", scatter_dimension=0
+        )
+
     def hop1(grads):
         return (step_x(grads[1]), step_y(grads[3])) if quick else ()
 
@@ -1088,9 +1108,12 @@
         return step_y(add(grads[4], came[0][1])), step_x(add(grads[2], came[1][1]))
 
     def hop3(grads, came, last):
+        return tensor_sum(gathered(grads, came, last))
+
+    def gathered(grads, came, last):
         own, sx, kx, sy, ky = grads
         if quick:
-            return tensor_sum(combine(own, came[0], came[1], last[0], last[1]))
+            return combine(own, came[0], came[1], last[0], last[1])
         blocks = [
             own,
             jnp.concatenate([sx[0], kx]),
@@ -1102,7 +1125,7 @@
         cols = own.shape[-1]
         every = every.reshape(PLANE_BLOCKS, parts, planes // PLANE_BLOCKS, rows, cols)
         every = every.transpose(0, 2, 1, 3, 4).reshape(planes, parts, rows, cols)
-        return tensor_sum(lax.psum_scatter(every, "plane", scatter_dimension=0))
+        return lax.psum_scatter(every, "plane", scatter_dimension=0)
 
     def add(a, b):
         return (a.astype(WIDE) + b.astype(WIDE)).astype(NARROW)
@@ -1151,6 +1174,9 @@
         for turn in range(2):
             back = [(b, a) for a, b in route(turn)]
             came.append(lax.ppermute(blocks[turn], ("pair", "tensor"), back))
+        return came
+
+    def home(came):
         odd = lax.rem(part, 2) == 1
         return jnp.stack([jnp.where(odd, came[1], came[0]), jnp.where(odd, came[0], came[1])])[:, None]
 
@@ -1209,9 +1235,10 @@
         col_e1, sx, sy, sz, source = fence(col_e1, sx, sy, sz, inputs)
         r2 = (column_of(jnp.stack([sd, sx, sy, sz])),) * PLANE_BLOCKS
         e1n, blocks = near(col_e1), bring(source)
-        e1n, r1c, blocks = fence(e1n, r1c, blocks)
+        e1n, r1c, blocks, source = fence(e1n, r1c, blocks, cotangent)
         e1f, r1n, x0 = far(e1n), near(r1c), settle(blocks)
-        e1f, e1n, r1n, attc, x0 = fence(e1f, e1n, r1n, attc, x0)
+        cot = bring(source)
+        e1f, e1n, r1n, attc, x0, cot = fence(e1f, e1n, r1n, attc, x0, cot)
         e1 = (col_e1, *e1n, *e1f)
         r1f, attn = far(r1n), near(attc)
     else:
@@ -1227,7 +1254,8 @@
     x0 = x0.astype(WIDE)
     a1, u1, s1 = norm_expand("ff", x0, None, 0.5, gain_row(0), bias_row(0), e1, ffc, 0, p, hidden1)
     if quick:
-        r1f, r1n, attn, s1 = fence(r1f, r1n, attn, s1)
+        cot = settle(cot)
+        r1f, r1n, attn, s1, cot = fence(r1f, r1n, attn, s1, cot)
         r1, attf = (r1c, *r1n, *r1f), far(attn)
     f1 = reduce_mm(s1, r1, ffc, 0, p, width)
     if quick:
@@ -1255,14 +1283,12 @@
     )
     y, y_sums = causal_mix(z, taps, taps_count)
     if quick:
-        e2n, y_sums, cot_source = fence(e2n, y_sums, cotangent)
+        e2n, y_sums = fence(e2n, y_sums)
         e2f = far(e2n)
-        cot = bring(cot_source)
     y_sums = (y_sums, other_core(y_sums))
     f3, w = filter_out(y, y_sums, depth_gain, depth_bias, fil, cc, 2, p, width)
     if quick:
-        e2f, cot, f3 = fence(e2f, cot, f3)
-        cot = settle(cot)
+        e2f, f3 = fence(e2f, f3)
         e2 = (e2c, *e2n, *e2f)
     else:
         cot = settle(bring(cotangent))
@@ -1276,7 +1302,7 @@
         x3, f4, other_core(f4), bias_row(10), cot, live, gain_row(5), bias_row(5)
     )
 
-    g_r2 = wgrad_flat(gf2, s2, p)
+    g_r2 = wgrad_flat([gf2], [s2], p)
     g_r2, gf2 = fence(g_r2, gf2)
     z_r2 = tensor_sum(g_r2)
     gu2, gc2 = back_expand("ff", gf2, r2, ffc, 0, p, u2)
@@ -1294,23 +1320,34 @@
     )
     e2h1, gg = fence(e2h1, gg)
     e2h2 = hop2(g_e2, e2h1)
-    g_fil = wgrad([cn, gw], [gg, w], p)
-    filh1 = hop1(g_fil)
+    g_fil = wgrad_flat([cn, gw], [gg, w], p)
+    z_fil = tensor_sum(g_fil)
     b3 = reduce_mm(gg, fil, 2 * cc, 0, p, width)
     e2h2, b3, g_fil = fence(e2h2, b3, g_fil)
     z_e2 = hop3(g_e2, e2h1, e2h2)
-    outputs = send_home(out_rows)
     gx2, gm, sums2 = norm_back(1.0, x2, gx3, b3, other_core(b3), gain_row(2))
     go = back_expand("low", gm, att, qc, 3, p)
+    go, z_r2 = fence(go, z_r2)
+    r2x = across_x(z_r2)
     gqkv, gqkv_sums, table_grad = attend_back(qkv, go, chances, table)
-    filh1, gqkv, outputs = fence(filh1, gqkv, outputs)
-    filh2 = hop2(g_fil, filh1)
     g_att = wgrad([bn, gm], [gqkv, o], p)
-    g_att, gqkv = fence(g_att, gqkv)
+    g_att, gqkv, r2x = fence(g_att, gqkv, r2x)
     atth1 = hop1(g_att)
     b2 = reduce_mm(gqkv, att, 3 * qc, 0, p, width)
     gx1, gf1, sums1 = norm_back(0.5, x1, gx2, b2, other_core(b2), gain_row(1))
     g_r1 = wgrad([gf1], [s1], p)
+    g_r1, gf1, atth1 = fence(g_r1, gf1, atth1)
+    r1h1 = hop1(g_r1)
+    atth2 = hop2(g_att, atth1)
+    gu1, gc1 = back_expand("ff", gf1, r1, ffc, 0, p, u1)
+    g_e1 = wgrad([a1], [gu1], p)
+    outputs = send_home(out_rows)
+    atth2, r1h1, g_e1, gu1, z_fil, outputs = fence(atth2, r1h1, g_e1, gu1, z_fil, outputs)
+    e1h1 = hop1(g_e1)
+    r1h2 = hop2(g_r1, r1h1)
+    z_att = hop3(g_att, atth1, atth2)
+    b1 = reduce_mm(gu1, e1, ffc, 0, p, width)
+    gx0, _, sums0 = norm_back(1.0, x0, gx1, b1, other_core(b1), gain_row(0))
 
     table_rows = -(-buckets // 8)
     tail = jnp.transpose(table_grad[:HD])[1 : buckets - 1]
@@ -1319,73 +1356,51 @@
     tail = jnp.pad(tail, ((0, 8 * table_rows - buckets), (0, 0)))
     tail = tail.reshape(table_rows, 8, HD).transpose(1, 0, 2).reshape(8, table_rows * HD)
     tail = jnp.pad(tail, ((0, 0), (0, width - table_rows * HD)))
-    early = pack(
+    small = pack(
         64, width, core1,
         [
             (sums_final, [("once", 0, 5), ("once", 1, 11), ("once", 2, 16)]),
             (sums3, [("once", 0, 4), ("once", 1, 10)]),
             (sums2, [("once", 0, 2), ("once", 1, 8), ("once", 2, 14)]),
             (sums1, [("once", 0, 1), ("once", 1, 7), ("once", 2, 15)]),
+            (sums0, [("once", 0, 0), ("once", 1, 6)]),
             (gqkv_sums, [("row", (0, 0, 3 * qc, qc), 12), ("row", (0, 2 * qc, 3 * qc, qc), 13)]),
             (depth_cols, [("row", (0, 0, cc, cc), 3), ("row", (1, 0, cc, cc), 9)]),
+            (gc1, [("hidden", 0, 17)]),
             (gc2, [("hidden", 0, 21)]),
             (taps_grad, [("taps", taps_count, 25)]),
             (tail, [("all", 0, 56)]),
         ],
     )
-    filh2, g_r1, gf1, z_r2, early = fence(filh2, g_r1, gf1, z_r2, early)
-    r1h1 = hop1(g_r1)
-    z_fil = hop3(g_fil, filh1, filh2)
-    half = early.shape[0] // 2
-    mine = lax.dynamic_slice_in_dim(early, core * half, half, 0)
-    theirs = lax.dynamic_slice_in_dim(early, (1 - core) * half, half, 0)
-    gu1, gc1 = back_expand("ff", gf1, r1, ffc, 0, p, u1)
-    g_e1 = wgrad([a1], [gu1], p)
-    atth1, g_e1, gu1, z_e2, mine = fence(atth1, g_e1, gu1, z_e2, mine)
-    atth2 = hop2(g_att, atth1)
-    e1h1 = hop1(g_e1)
-    early = mine + other_core(theirs)
-    b1 = reduce_mm(gu1, e1, ffc, 0, p, width)
-    r1h1, atth2, b1 = fence(r1h1, atth2, b1)
-    r1h2 = hop2(g_r1, r1h1)
-    z_att = hop3(g_att, atth1, atth2)
-    gx0, _, sums0 = norm_back(1.0, x0, gx1, b1, other_core(b1), gain_row(0))
-    late = pack(
-        8, width, core1,
-        [(sums0, [("once", 0, 0), ("once", 1, 1)]), (gc1, [("hidden", 0, 2)])],
+    half = small.shape[0] // 2
+    mine = lax.dynamic_slice_in_dim(small, core * half, half, 0)
+    came = other_core(lax.dynamic_slice_in_dim(small, (1 - core) * half, half, 0))
+    r1h2, e1h1, gx0, came, z_e2 = fence(r1h2, e1h1, gx0, came, z_e2)
+    e1h2 = hop2(g_e1, e1h1)
+    z_r1 = hop3(g_r1, r1h1, r1h2)
+    planes_came = over_planes(mine + came)
+    e1h2, planes_came = fence(e1h2, planes_came)
+    t_e1, planes_came = fence(gathered(g_e1, e1h1, e1h2), planes_came)
+    z_e1 = tensor_sum(t_e1)
+    filx, r2y = across_x(z_fil), across_y(z_r2, r2x)
+    homeward = send_home(gx0.astype(NARROW))
+    mine = over_parts(planes_came)
+    filx, r2y, mine, homeward, z_att = fence(filx, r2y, mine, homeward, z_att)
+    fily = across_y(z_fil, filx)
+    e2_grad, att_grad = share(z_e2), share(z_att)
+    theirs = other_core(mine)
+    r2_grad = share(across_end(z_r2, r2x, r2y))
+    fil_grad = share(across_end(z_fil, filx, fily))
+    small = jnp.concatenate(
+        [jnp.where(core == 0, mine, theirs), jnp.where(core == 0, theirs, mine)], axis=0
     )
-    e1h1, gx0, late, z_fil = fence(e1h1, gx0, late, z_fil)
-    e1h2 = hop2(g_e1, e1h1)
-    homeward = send_home(gx0.astype(NARROW))
-    late = late + other_core(late)
-    early = over_planes(early)
-    r1h2, early, late = fence(r1h2, early, late)
-    z_r1 = hop3(g_r1, r1h1, r1h2)
-    late = over_planes(late)
-    e1h2, late, early = fence(e1h2, late, early)
-    z_e1 = hop3(g_e1, e1h1, e1h2)
-    early, late = over_parts(early), over_parts(late)
-    early_other = other_core(early)
-    early = jnp.concatenate(
-        [jnp.where(core == 0, early, early_other), jnp.where(core == 0, early_other, early)], axis=0
-    )
-    input_grad = homeward.astype(WIDE)
-    if quick:
-        rx = step_x(z_r2[1::2])
-        ry = step_y(add(z_r2[2], rx[1]))
-        z_r2 = (z_r2[0].astype(WIDE) + rx[0].astype(WIDE) + ry.astype(WIDE)).astype(NARROW)
-    else:
-        z_r2 = lax.psum_scatter(
-            z_r2.reshape(planes, -1, z_r2.shape[-1]), "plane", scatter_dimension=0
-        )
-    e1_grad, r1_grad, att_grad, fil_grad, e2_grad, r2_grad = [
-        share(v) for v in (z_e1, z_r1, z_att, z_fil, z_e2, z_r2)
-    ]
-
-    gains_grad = jnp.concatenate([late[0:1], early[1:6]], axis=0)
-    bias_grad = jnp.concatenate([late[1:2], early[7:17], late[2:6], early[21:25]], axis=0)
-    taps_t = early[25 : 25 + taps_count]
-    table_t = early[56:64, : table_rows * HD].reshape(8, table_rows, HD).transpose(1, 0, 2)
+    outputs = home(outputs)
+    input_grad = home(homeward).astype(WIDE)
+    r1_grad, e1_grad = share(z_r1), share(z_e1)
+    gains_grad = small[0:6]
+    bias_grad = small[6:25]
+    taps_t = small[25 : 25 + taps_count]
+    table_t = small[56:64, : table_rows * HD].reshape(8, table_rows, HD).transpose(1, 0, 2)
     table_t = table_t.reshape(8 * table_rows, HD)[:buckets]
     return (
         outputs,

time: 714 us -> 669 us (0.937)
  starting transfers between devices: 101 us -> 80.2 us
  waiting for transfers between devices: 198 us -> 179 us
  other arithmetic: 52.7 us -> 45 us
    ppermute x24 -> x22, waiting for transfers between devices: 48.6 us -> 77.5 us  [step_x(): return lax.ppermute(v, 'plane', [(i, i ^ 1) for i in range(planes)])]
    ppermute x2 -> x1, waiting for transfers between devices: 21.8 us -> 0.01 us  [over_planes(): lax.ppermute(v, 'plane', [(i, i ^ 3) for i in range(4)])]
    ppermute x25 -> x23, waiting for transfers between devices: 36.5 us -> 18.1 us  [step_y(): return lax.ppermute(v, 'plane', [(i, i ^ 2) for i in range(planes)])]
    all_gather x5, waiting for transfers between devices: 59.1 us -> 47.3 us  [column_of(): return lax.all_gather(shard, 'tensor', axis=0)]
    ppermute x6 -> x3, starting transfers between devices: 14.5 us -> 4.39 us  [turn(): return lax.ppermute(v, 'tensor', [(i, i ^ k) for i in range(parts)])]
    ppermute x4, waiting for transfers between devices: 0.01 us -> 8.33 us  [bring(): blocks.append(lax.ppermute(block, ('pair', 'tensor'), route(turn)))]
    pallas_call x5 -> x4, Pallas kernels: 30.3 us -> 24.5 us  [wgrad(): pl.pallas_call(functools.partial(wgrad_body, len(xs)), grid_spec=pltpu.Pr...]
    convert_element_type x11 -> x10, other arithmetic: 17.4 us -> 13.6 us  [add(): return (a.astype(WIDE) + b.astype(WIDE)).astype(NARROW)]
  transfers between devices with their start and end apart: 103 -> 94, of which waited for: 38 -> 39; matrix products, arithmetic and copies ran while one was open for 12% -> 11% of each run, Pallas kernels for 32% -> 34%
where the time goes in v2:
time: 669 us; the launch traced here: 661 us
  Pallas kernels  241 us (36%)
  waiting for transfers between devices  179 us (27%)
  local copies, waits for them, and re-layouts  100 us (15%)
  starting transfers between devices  80.2 us (12%)
  other arithmetic  45 us (7%)
  between operations  16 us (2%)
    ppermute x22, waiting for transfers between devices, step_x(): return lax.ppermute(v, 'plane', [(i, i ^ 1) for i in range(planes)])  77.5 us
    unnamed x348, local copies, waits for them, and re-layouts  67.6 us
    all_gather x5, waiting for transfers between devices, column_of(): return lax.all_gather(shard, 'tensor', axis=0)  47.3 us
    pallas_call x7, Pallas kernels, reduce_mm(): pl.pallas_call(functools.partial(reduce_body, len(w)), grid_spec=pltpu.Pr...  39.3 us
    pallas_call x4, Pallas kernels, norm_expand(): pl.pallas_call(functools.partial(expand_body, kind, merged, scale, len(w)...  35.9 us
    ppermute x23, starting transfers between devices, step_y(): return lax.ppermute(v, 'plane', [(i, i ^ 2) for i in range(planes)])  27.1 us
    pallas_call x4, Pallas kernels, norm_back(): pl.pallas_call(functools.partial(norm_back_body, scale), grid=(rows // CH...  25.6 us
    pallas_call x1, Pallas kernels, attend_back(): pl.pallas_call(attend_back_body, grid=(4,), in_specs=[pl.BlockSpec((rows,...  25.1 us
  transfers between devices with their start and end apart: 94, of which 39 were waited for; matrix products, arithmetic and copies ran while one was open for 11% of the time, Pallas kernels for 34%

profile of v2, /device:TPU:0, one launch (start us, length us, event | category | flops | bytes accessed | tf_op | source)
XLA Modules:
  0.0 660.9 jit_solution(14388120903290682148)
XLA Ops:
  39.6 11.0 %all-gather.11.cloned.1.call-done = bf16[1024,512]{1,0:T(8,128)(2,1)} async-done(((bf16[256,512]{1,0:T(8,128)(2,1)}), bf16[1024,512]{1,0:T(8,128)(2,1)}) %all-gather.11.cloned.1.call-update) | async-done | bytes 1048592 | tf_op jit(solution)/shard_map/all_gather | solution.py:1063
  56.3 28.6 %all-gather.13.cloned.1.call-done = bf16[1024,512]{1,0:T(8,128)(2,1)} async-done(((bf16[256,512]{1,0:T(8,128)(2,1)}), bf16[1024,512]{1,0:T(8,128)(2,1)}) %all-gather.13.cloned.1.call-update) | async-done | bytes 1048592 | tf_op jit(solution)/shard_map/all_gather | solution.py:1063
  97.6 8.3 %collective-permute-done.18 = bf16[128,1024]{1,0:T(8,128)(2,1)} collective-permute-done((bf16[128,1024]{1,0:T(8,128)(2,1)}, bf16[128,1024]{1,0:T(8,128)(2,1)}, u32[]{:S(2)}, u32[]{:S(2)}) %collective-permute-start.18) | collective-permute-done | bytes 262176 | tf_op jit(solution)/shard_map/ppermute | solution.py:1154
  114.0 7.7 %all-gather.15.cloned.1.call-done = bf16[1024,512]{1,0:T(8,128)(2,1)} async-done(((bf16[256,512]{1,0:T(8,128)(2,1)}), bf16[1024,512]{1,0:T(8,128)(2,1)}) %all-gather.15.cloned.1.call-update) | async-done | bytes 1048592 | tf_op jit(solution)/shard_map/all_gather | solution.py:1063
  139.9 8.8 %norm_expand_ff.2 = (bf16[512,1024]{1,0:T(8,128)(2,1)S(1)}, f32[512,2048]{1,0:T(8,128)}, bf16[512,2048]{1,0:T(8,128)(2,1)}) custom-call(s32[1]{0:T(128)} %bitcast.p_ref, f32[512,1024]{1,0:T(8,128)} %convert_element_type.214.refs_0_.x_ref, f32[1,1024]{1,0:T(1,128)S(1)} %get-tuple-element.505.refs_1_.g_ref, f32[1,1024]{1,0:T(1,128)S(1)} %get-tuple-element.497.refs_2_, ...), custom_call_target="tpu_custom_call" | custom-call | flops 1073741 | bytes 5242 | tf_op jit(solution)/shard_map/norm_expand_ff/pallas_call | solution.py:166
  151.5 11.8 %collective-permute-done.20.refs_4_ = bf16[2,256,512]{2,1,0:T(8,128)(2,1)} collective-permute-done((bf16[2,256,512]{2,1,0:T(8,128)(2,1)}, bf16[2,256,512]{2,1,0:T(8,128)(2,1)}, u32[]{:S(2)}, u32[]{:S(2)}) %collective-permute-start.20) | collective-permute-done | bytes 524320 | tf_op jit(solution)/shard_map/ppermute | solution.py:1038
  173.6 6.3 collective-permute-done.25.refs_10_.refs_4_
  185.0 8.7 %norm_expand_qkv.1 = (f32[512,1024]{1,0:T(8,128)}, bf16[512,1024]{1,0:T(8,128)(2,1)S(1)}, bf16[512,1536]{1,0:T(8,128)(2,1)}) custom-call(s32[1]{0:T(128)} %bitcast.p_ref, f32[512,1024]{1,0:T(8,128)} %convert_element_type.214.refs_0_.x_ref, bf16[512,1024]{1,0:T(8,128)(2,1)S(1)} %copy-done.40, bf16[512,1024]{1,0:T(8,128)(2,1)S(1)} %collective-permute-done.26.refs_2_, ...), custom_call_target="tpu_custom_call" | custom-call | flops 805306 | bytes 4718 | tf_op jit(solution)/shard_map/norm_expand_qkv/pallas_call | solution.py:166
  199.3 17.7 %attend.1 = (bf16[512,512]{1,0:T(8,128)(2,1)S(1)}, bf16[8,512,512]{2,1,0:T(8,128)(2,1)}) custom-call(s32[1]{0:T(128)} %bitcast.23.len_ref, bf16[512,1536]{1,0:T(8,128)(2,1)S(1)} %copy-done.21, bf16[128,64]{1,0:T(8,128)(2,1)S(1)} %pad.16.table_ref), custom_call_target="tpu_custom_call" | custom-call | flops 268435 | bytes 2621 | tf_op jit(solution)/shard_map/attend/pallas_call | solution.py:567
  238.6 8.0 %norm_expand_conv.1 = (f32[512,1024]{1,0:T(8,128)}, bf16[512,1024]{1,0:T(8,128)(2,1)S(1)}, f32[512,512]{1,0:T(8,128)S(1)}, f32[512,512]{1,0:T(8,128)}) custom-call(s32[1]{0:T(128)} %bitcast.p_ref, f32[512,1024]{1,0:T(8,128)} %get-tuple-element.257.refs_0_.x_ref, bf16[512,1024]{1,0:T(8,128)(2,1)} %reduce_mm.8.refs_1_, ...), custom_call_target="tpu_custom_call" | custom-call | flops 536870 | bytes 4194 | tf_op jit(solution)/shard_map/norm_expand_conv/pallas_call | solution.py:166
  253.9 6.6 collective-permute-done.34.refs_8_.refs_2_
  284.5 10.4 %norm_expand_ff.3 = (f32[512,1024]{1,0:T(8,128)}, bf16[512,1024]{1,0:T(8,128)(2,1)S(1)}, f32[512,2048]{1,0:T(8,128)}, bf16[512,2048]{1,0:T(8,128)(2,1)}) custom-call(s32[1]{0:T(128)} %bitcast.p_ref, f32[512,1024]{1,0:T(8,128)} %get-tuple-element.271.refs_0_.x_ref, bf16[512,1024]{1,0:T(8,128)(2,1)} %get-tuple-element.280.refs_1_, ...), custom_call_target="tpu_custom_call" | custom-call | flops 1073741 | bytes 5242 | tf_op jit(solution)/shard_map/norm_expand_ff/pallas_call | solution.py:166
  305.9 7.4 %final_norm.1 = (bf16[512,1024]{1,0:T(8,128)(2,1)S(1)}, f32[512,1024]{1,0:T(8,128)}, bf16[512,1024]{1,0:T(8,128)(2,1)S(1)}, f32[8,1024]{1,0:T(8,128)S(1)}) custom-call(f32[512,1024]{1,0:T(8,128)} %get-tuple-element.283.x_ref, bf16[512,1024]{1,0:T(8,128)(2,1)S(1)} %reduce_mm.9.pa_ref, bf16[512,1024]{1,0:T(8,128)(2,1)S(1)} %collective-permute-done.39.pb_ref, ...), custom_call_target="tpu_custom_call" | custom-call | flops 6291 | bytes 4718 | tf_op jit(solution)/shard_map/final_norm/pallas_call | solution.py:496
  359.1 8.9 %mix_back.1 = (bf16[512,1024]{1,0:T(8,128)(2,1)S(1)}, f32[32,512]{1,0:T(8,128)S(1)}) custom-call(f32[512,512]{1,0:T(8,128)S(1)} %get-tuple-element.306.gyn_ref, f32[512,512]{1,0:T(8,128)S(1)} %copy-done.8, f32[512,128]{1,0:T(8,128)S(1)} %get-tuple-element.278.sa_ref, f32[512,128]{1,0:T(8,128)S(1)} %copy-done.52, f32[512,128]{1,0:T(8,128)S(1)} %get-tuple-element.307.ra_ref, ...), custom_call_target="tpu_custom_call" | custom-call | flops 16252 | bytes 2621 | tf_op jit(solution)/shard_map/mix_back/pallas_call | solution.py:897
  411.6 25.1 %attend_back.1 = (bf16[512,1536]{1,0:T(8,128)(2,1)S(1)}, f32[1,1536]{1,0:T(1,128)S(1)}, f32[72,128]{1,0:T(8,128)S(1)}) custom-call(bf16[512,1536]{1,0:T(8,128)(2,1)S(1)} %copy-done.22, bf16[512,512]{1,0:T(8,128)(2,1)S(1)} %copy-done.56, bf16[8,512,512]{2,1,0:T(8,128)(2,1)} %get-tuple-element.320.p_ref, bf16[128,64]{1,0:T(8,128)(2,1)S(1)} %copy-done.110), custom_call_target="tpu_custom_call" | custom-call | flops 671088 | bytes 2621 | tf_op jit(solution)/shard_map/attend_back/pallas_call | solution.py:673
  438.0 7.7 %wgrad.5 = (bf16[4,256,512]{2,1,0:T(8,128)(2,1)S(1)}, bf16[2,2,256,512]{3,2,1,0:T(8,128)(2,1)}, bf16[2,256,512]{2,1,0:T(8,128)(2,1)S(1)}, bf16[2,2,256,512]{3,2,1,0:T(8,128)(2,1)}, bf16[2,256,512]{2,1,0:T(8,128)(2,1)S(1)}) custom-call(s32[1]{0:T(128)} %bitcast.p_ref, bf16[512,1024]{1,0:T(8,128)(2,1)S(1)} %copy-done.73, bf16[512,1024]{1,0:T(8,128)(2,1)} %copy-done.31, ...), custom_call_target="tpu_custom_call" | custom-call | flops 1073741 | bytes 3145 | tf_op jit(solution)/shard_map/wgrad/pallas_call | solution.py:333
  447.5 6.6 %reduce_mm.12.pa_ref = bf16[512,1024]{1,0:T(8,128)(2,1)} custom-call(s32[1]{0:T(128)} %bitcast.p_ref, bf16[512,1536]{1,0:T(8,128)(2,1)} %copy-done.23, bf16[4,256,512]{2,1,0:T(8,128)(2,1)S(1)} %bitcast.193, bf16[4,256,512]{2,1,0:T(8,128)(2,1)S(1)} %copy-done.3, bf16[4,256,512]{2,1,0:T(8,128)(2,1)S(1)} %copy-done.1, ...), custom_call_target="tpu_custom_call" | custom-call | flops 805306 | bytes 2097 | tf_op jit(solution)/shard_map/reduce_mm/pallas_call | solution.py:203
  462.1 6.3 norm_back.6
  490.3 7.1 %back_expand_ff.3 = (bf16[512,2048]{1,0:T(8,128)(2,1)}, f32[1,2048]{1,0:T(1,128)S(1)}) custom-call(s32[1]{0:T(128)} %bitcast.p_ref, bf16[512,1024]{1,0:T(8,128)(2,1)S(1)} %get-tuple-element.345.refs_0_.g_ref, bf16[4,256,512]{2,1,0:T(8,128)(2,1)S(1)} %bitcast.201, bf16[4,256,512]{2,1,0:T(8,128)(2,1)} %collective-permute-done.14.refs_1_, ...), custom_call_target="tpu_custom_call" | custom-call | flops 1073741 | bytes 3670 | tf_op jit(solution)/shard_map/back_expand_ff/pallas_call | solution.py:257
  507.2 10.8 %collective-permute-done.52.fy_ref = bf16[2,256,512]{2,1,0:T(8,128)(2,1)} collective-permute-done((bf16[2,256,512]{2,1,0:T(8,128)(2,1)}, bf16[2,256,512]{2,1,0:T(8,128)(2,1)}, u32[]{:S(2)}, u32[]{:S(2)}) %collective-permute-start.52) | collective-permute-done | bytes 524320 | tf_op jit(solution)/shard_map/ppermute | solution.py:1038
  544.6 7.3 %norm_back.7 = (f32[512,1024]{1,0:T(8,128)S(1)}, bf16[512,1024]{1,0:T(8,128)(2,1)}, f32[8,1024]{1,0:T(8,128)S(1)}) custom-call(f32[512,1024]{1,0:T(8,128)} %convert_element_type.214.refs_0_.x_ref, f32[512,1024]{1,0:T(8,128)} %copy-done.57, bf16[512,1024]{1,0:T(8,128)(2,1)} %reduce_mm.13.pa_ref, bf16[512,1024]{1,0:T(8,128)(2,1)S(1)} %collective-permute-done.63.pb_ref, ...), custom_call_target="tpu_custom_call" | custom-call | flops 5242 | bytes 4718 | tf_op jit(solution)/shard_map/norm_back/pallas_call | solution.py:453
  556.5 16.7 %collective-permute-done.60.fy_ref = bf16[2,256,512]{2,1,0:T(8,128)(2,1)} collective-permute-done((bf16[2,256,512]{2,1,0:T(8,128)(2,1)}, bf16[2,256,512]{2,1,0:T(8,128)(2,1)}, u32[]{:S(2)}, u32[]{:S(2)}) %collective-permute-start.60) | collective-permute-done | bytes 524320 | tf_op jit(solution)/shard_map/ppermute | solution.py:1038
  592.4 9.7 %collective-permute-done.66.fy_ref = bf16[2,256,512]{2,1,0:T(8,128)(2,1)S(1)} collective-permute-done((bf16[2,256,512]{2,1,0:T(8,128)(2,1)S(1)}, bf16[2,256,512]{2,1,0:T(8,128)(2,1)S(1)}, u32[]{:S(2)}, u32[]{:S(2)}) %collective-permute-start.66) | collective-permute-done | bytes 524320 | tf_op jit(solution)/shard_map/ppermute | solution.py:1038
  642.6 6.8 %reduce-scatter.15.cloned.1.call-done = bf16[1,256,512]{2,1,0:T(8,128)(2,1)} async-done(((bf16[4,256,512]{2,1,0:T(8,128)(2,1)}), bf16[1,256,512]{2,1,0:T(8,128)(2,1)}) %reduce-scatter.15.cloned.1.call-update) | async-done | bytes 262160 | tf_op jit(solution)/shard_map/reduce_scatter | solution.py:1087
  (688 shorter events, 390.8 us)
Async XLA Ops:
  7.2 43.5 %all-gather.11.cloned.1.call-start = ((), (), s32[]{:S(2)}) async-start(), calls=%async_computation.12 | async-start | bytes 1310720 | tf_op jit(solution)/shard_map/all_gather | solution.py:1063
  20.0 64.9 %all-gather.13.cloned.1.call-start = ((), (), s32[]{:S(2)}) async-start(), calls=%async_computation.13 | async-start | bytes 1310720 | tf_op jit(solution)/shard_map/all_gather | solution.py:1063
  20.7 100.9 %all-gather.15.cloned.1.call-start = ((), (), s32[]{:S(2)}) async-start(), calls=%async_computation.14 | async-start | bytes 1310720 | tf_op jit(solution)/shard_map/all_gather | solution.py:1063
  21.5 152.1 %all-gather.17.cloned.1.call-start = ((), (), s32[]{:S(2)}) async-start(), calls=%async_computation.15 | async-start | bytes 2293760 | tf_op jit(solution)/shard_map/all_gather | solution.py:1063
  22.0 273.8 %all-gather.19.cloned.1.call-start = ((), (), s32[]{:S(2)}) async-start(), calls=%async_computation.16 | async-start | bytes 5242880 | tf_op jit(solution)/shard_map/all_gather | solution.py:1063
  50.6 34.3 %collective-permute-start.9 = (bf16[4,256,512]{2,1,0:T(8,128)(2,1)}, bf16[4,256,512]{2,1,0:T(8,128)(2,1)S(1)}, u32[]{:S(2)}, u32[]{:S(2)}) collective-permute-start(bf16[4,256,512]{2,1,0:T(8,128)(2,1)} %bitcast.194), channel_id=1, source_target_pairs={{0,16},{8,24},{16,0},{24,8},{1,17},{9,25},{17,1},{25,9},{2,18},{10... | collective-permute-start | bytes 3145736 | tf_op jit(solution)/shard_map/ppermute | solution.py:1041
  52.1 32.8 %collective-permute-start.8 = (bf16[4,256,512]{2,1,0:T(8,128)(2,1)}, bf16[4,256,512]{2,1,0:T(8,128)(2,1)S(1)}, u32[]{:S(2)}, u32[]{:S(2)}) collective-permute-start(bf16[4,256,512]{2,1,0:T(8,128)(2,1)} %bitcast.195), channel_id=1, source_target_pairs={{0,8},{8,0},{16,24},{24,16},{1,9},{9,1},{17,25},{25,17},{2,10},{10... | collective-permute-start | bytes 3145736 | tf_op jit(solution)/shard_map/ppermute | solution.py:1038
  85.7 39.1 %collective-permute-start.15 = (bf16[4,256,512]{2,1,0:T(8,128)(2,1)}, bf16[4,256,512]{2,1,0:T(8,128)(2,1)S(1)}, u32[]{:S(2)}, u32[]{:S(2)}) collective-permute-start(bf16[4,256,512]{2,1,0:T(8,128)(2,1)} %bitcast.198), channel_id=1, source_target_pairs={{0,16},{8,24},{16,0},{24,8},{1,17},{9,25},{17,1},{25,9},{2,18},{10... | collective-permute-start | bytes 3145736 | tf_op jit(solution)/shard_map/ppermute | solution.py:1041
  87.0 37.9 %collective-permute-start.14 = (bf16[4,256,512]{2,1,0:T(8,128)(2,1)}, bf16[4,256,512]{2,1,0:T(8,128)(2,1)}, u32[]{:S(2)}, u32[]{:S(2)}) collective-permute-start(bf16[4,256,512]{2,1,0:T(8,128)(2,1)} %bitcast.199), channel_id=1, source_target_pairs={{0,8},{8,0},{16,24},{24,16},{1,9},{9,1},{17,25},{25,17},{2,10},{10... | collective-permute-start | bytes 3145736 | tf_op jit(solution)/shard_map/ppermute | solution.py:1038
  109.8 297.4 %reduce-scatter.7.cloned.1.call-start = ((), (), s32[]{:S(2)}) async-start(), calls=%async_computation.6 | async-start | bytes 5242880 | tf_op jit(solution)/shard_map/reduce_scatter | solution.py:1087
  125.8 37.4 %collective-permute-start.22 = (bf16[4,256,512]{2,1,0:T(8,128)(2,1)}, bf16[4,256,512]{2,1,0:T(8,128)(2,1)S(1)}, u32[]{:S(2)}, u32[]{:S(2)}) collective-permute-start(bf16[4,256,512]{2,1,0:T(8,128)(2,1)} %bitcast.188), channel_id=1, source_target_pairs={{0,16},{8,24},{16,0},{24,8},{1,17},{9,25},{17,1},{25,9},{2,18},{10... | collective-permute-start | bytes 3145736 | tf_op jit(solution)/shard_map/ppermute | solution.py:1041
  126.6 36.6 %collective-permute-start.21 = (bf16[4,256,512]{2,1,0:T(8,128)(2,1)}, bf16[4,256,512]{2,1,0:T(8,128)(2,1)S(1)}, u32[]{:S(2)}, u32[]{:S(2)}) collective-permute-start(bf16[4,256,512]{2,1,0:T(8,128)(2,1)} %bitcast.189), channel_id=1, source_target_pairs={{0,8},{8,0},{16,24},{24,16},{1,9},{9,1},{17,25},{25,17},{2,10},{10... | collective-permute-start | bytes 3145736 | tf_op jit(solution)/shard_map/ppermute | solution.py:1038
  320.3 186.9 %reduce-scatter.9.cloned.1.call-start = ((), (), s32[]{:S(2)}) async-start(), calls=%async_computation.7 | async-start | bytes 3932160 | tf_op jit(solution)/shard_map/reduce_scatter | solution.py:1087
  374.1 182.4 %reduce-scatter.11.cloned.1.call-start = ((), (), s32[]{:S(2)}) async-start(), calls=%async_computation.8 | async-start | bytes 1310720 | tf_op jit(solution)/shard_map/reduce_scatter | solution.py:1087
  408.3 39.2 %collective-permute-start.47 = (bf16[2,256,512]{2,1,0:T(8,128)(2,1)S(1)}, bf16[2,256,512]{2,1,0:T(8,128)(2,1)S(1)}, u32[]{:S(2)}, u32[]{:S(2)}) collective-permute-start(bf16[2,256,512]{2,1,0:T(8,128)(2,1)S(1)} %slice.270), channel_id=1, source_target_pairs={{0,8},{8,0},{16,24},{24,16},{1,9},{9,1},{17,25},{25,17},{2,10},{10... | collective-permute-start | bytes 1572872 | tf_op jit(solution)/shard_map/ppermute | solution.py:1038
  460.3 163.5 %reduce-scatter.13.cloned.1.call-start = ((), (), s32[]{:S(2)}) async-start(), calls=%async_computation.9 | async-start | bytes 1310720 | tf_op jit(solution)/shard_map/reduce_scatter | solution.py:1087
  481.9 36.7 %collective-permute-start.53 = (bf16[2,2,256,512]{3,2,1,0:T(8,128)(2,1)}, bf16[2,2,256,512]{3,2,1,0:T(8,128)(2,1)S(1)}, u32[]{:S(2)}, u32[]{:S(2)}) collective-permute-start(bf16[2,2,256,512]{3,2,1,0:T(8,128)(2,1)} %get-tuple-element.342), channel_id=1, source_target_pairs={{0,8},{8,0},{16,24},{24,16},{1,9},{9,1},{17,25},{25,17},{2,10},{10... | collective-permute-start | bytes 3145736 | tf_op jit(solution)/shard_map/ppermute | solution.py:1038
  482.7 35.9 %collective-permute-start.54 = (bf16[2,2,256,512]{3,2,1,0:T(8,128)(2,1)}, bf16[2,2,256,512]{3,2,1,0:T(8,128)(2,1)S(1)}, u32[]{:S(2)}, u32[]{:S(2)}) collective-permute-start(bf16[2,2,256,512]{3,2,1,0:T(8,128)(2,1)} %get-tuple-element.343), channel_id=1, source_target_pairs={{0,16},{8,24},{16,0},{24,8},{1,17},{9,25},{17,1},{25,9},{2,18},{10... | collective-permute-start | bytes 3145736 | tf_op jit(solution)/shard_map/ppermute | solution.py:1041
  527.5 113.2 %reduce-scatter.17.cloned.1.call-start = ((), (), s32[]{:S(2)}) async-start(), calls=%async_computation.11 | async-start | bytes 1310720 | tf_op jit(solution)/shard_map/reduce_scatter | solution.py:1087
  536.1 37.9 %collective-permute-start.61 = (bf16[2,2,256,512]{3,2,1,0:T(8,128)(2,1)}, bf16[2,2,256,512]{3,2,1,0:T(8,128)(2,1)S(1)}, u32[]{:S(2)}, u32[]{:S(2)}) collective-permute-start(bf16[2,2,256,512]{3,2,1,0:T(8,128)(2,1)} %copy-done.140), channel_id=1, source_target_pairs={{0,8},{8,0},{16,24},{24,16},{1,9},{9,1},{17,25},{25,17},{2,10},{10... | collective-permute-start | bytes 3145736 | tf_op jit(solution)/shard_map/ppermute | solution.py:1038
  537.2 36.8 %collective-permute-start.62 = (bf16[2,2,256,512]{3,2,1,0:T(8,128)(2,1)}, bf16[2,2,256,512]{3,2,1,0:T(8,128)(2,1)}, u32[]{:S(2)}, u32[]{:S(2)}) collective-permute-start(bf16[2,2,256,512]{3,2,1,0:T(8,128)(2,1)} %copy-done.139), channel_id=1, source_target_pairs={{0,16},{8,24},{16,0},{24,8},{1,17},{9,25},{17,1},{25,9},{2,18},{10... | collective-permute-start | bytes 3145736 | tf_op jit(solution)/shard_map/ppermute | solution.py:1041
  540.4 32.8 %collective-permute-start.60 = (bf16[2,256,512]{2,1,0:T(8,128)(2,1)}, bf16[2,256,512]{2,1,0:T(8,128)(2,1)}, u32[]{:S(2)}, u32[]{:S(2)}) collective-permute-start(bf16[2,256,512]{2,1,0:T(8,128)(2,1)} %fusion.2), channel_id=1, source_target_pairs={{0,8},{8,0},{16,24},{24,16},{1,9},{9,1},{17,25},{25,17},{2,10},{10... | collective-permute-start | bytes 1572872 | tf_op jit(solution)/shard_map/ppermute | solution.py:1038
  578.9 70.4 %reduce-scatter.15.cloned.1.call-start = ((), (), s32[]{:S(2)}) async-start(), calls=%async_computation.10 | async-start | bytes 1310720 | tf_op jit(solution)/shard_map/reduce_scatter | solution.py:1087
  590.2 32.7 %collective-permute-start.58 = (bf16[256,512]{1,0:T(8,128)(2,1)S(1)}, bf16[256,512]{1,0:T(8,128)(2,1)S(1)}, u32[]{:S(2)}, u32[]{:S(2)}) collective-permute-start(bf16[256,512]{1,0:T(8,128)(2,1)S(1)} %copy-done.152), channel_id=1, source_target_pairs={{0,16},{8,24},{16,0},{24,8},{1,17},{9,25},{17,1},{25,9},{2,18},{10... | collective-permute-start | bytes 786440 | tf_op jit(solution)/shard_map/ppermute | solution.py:1041
  (241 other events, 2104.1 us)
Sparse Core Ops, SparseCore 0:
  20.1 30.4 all-gather.10
  52.8 32.0 all-gather.12
  87.1 34.5 all-gather.14
  123.1 40.7 all-gather.16
  165.3 79.6 all-gather.18
  320.4 73.9 reduce-scatter.6
  396.8 60.7 reduce-scatter.8
  460.4 28.9 reduce-scatter.10
  527.6 24.5 reduce-scatter.12
  579.0 24.3 reduce-scatter.16
  622.0 27.2 reduce-scatter.14

commit v3 on v2

--- a/solution.py
+++ b/solution.py
@@ -15,8 +15,10 @@
 MASKED = -1e30
 WIDE = jnp.float32
 NARROW = jnp.bfloat16
-CHUNK = 64
-QROWS = 128
+CHUNK = 256
+MIX_CHUNK = 64
+QROWS = 256
+BROWS = 512
 NEAR = 128
 VMEM_BYTES = 48 * 1024 * 1024
 PLANE_BLOCKS = 4
@@ -219,183 +221,6 @@
     )(p, s, *w)
 
 
-def back_body(kind, nw, p_ref, g_ref, *refs):
-    w_refs = refs[:nw]
-    rest = refs[nw:]
-    t = pl.program_id(0)
-    p = p_ref[0]
-    width = g_ref.shape[1] // PLANE_BLOCKS
-    acc = None
-    for r, w in enumerate(weight_blocks(w_refs, t)):
-        term = jnp.dot(g_ref[:, rel_cols(p, r, width)], w, preferred_element_type=WIDE)
-        acc = term if acc is None else acc + term
-    if kind == "ff":
-        u_ref, gu_ref, gc_ref = rest
-        u = u_ref[...]
-        logistic = sigmoid(u)
-        gu = acc * (logistic * (1.0 + u * (1.0 - logistic)))
-        gu_ref[...] = gu.astype(NARROW)
-        gc_ref[...] = jnp.sum(gu, axis=0, keepdims=True)
-    else:
-        (out_ref,) = rest
-        out_ref[...] = acc.astype(out_ref.dtype)
-
-
-def back_expand(kind, g, w, cols, col_block, p, u=None):
-    rows, width = g.shape
-    ins = [g, *w]
-    block = pl.BlockSpec((rows, cols), lambda t, p: (0, t))
-    specs = [whole((rows, width)), *weight_specs(w, cols, col_block)]
-    if kind == "ff":
-        ins.append(u)
-        specs.append(block)
-        shapes = [sds((rows, 4 * cols), NARROW), sds((1, 4 * cols), WIDE)]
-        out_specs = [block, pl.BlockSpec((1, cols), lambda t, p: (0, t))]
-    else:
-        shapes = sds((rows, 4 * cols), NARROW if kind == "low" else WIDE)
-        out_specs = block
-    return pl.pallas_call(
-        functools.partial(back_body, kind, len(w)),
-        grid_spec=pltpu.PrefetchScalarGridSpec(
-            num_scalar_prefetch=1, grid=(4,), in_specs=specs, out_specs=out_specs
-        ),
-        out_shape=shapes,
-        compiler_params=params(),
-        cost_estimate=cost(2 * rows * width * 4 * cols, 8 * width * cols + 12 * rows * cols),
-        name="back_expand_" + kind,
-    )(p, *ins)
-
-
-def wgrad_body(count, p_ref, *refs):
-    x_refs = refs[:count]
-    s_refs = refs[count : 2 * count]
-    own_ref, sx_ref, kx_ref, sy_ref, ky_ref = refs[2 * count :]
-    t = pl.program_id(0)
-    p = p_ref[0]
-
-    def grad(r, put):
-        start = 0
-        for x_ref, s_ref in zip(x_refs, s_refs):
-            width = x_ref.shape[1] // PLANE_BLOCKS
-            cols = s_ref.shape[1]
-            term = lax.dot_general(
-                x_ref[:, rel_cols(p, r, width)],
-                s_ref[...],
-                (((0,), (0,)), ((), ())),
-                preferred_element_type=WIDE,
-            ).astype(NARROW)
-            put(start, cols, term)
-            start += cols
-
-    def put_own(start, cols, term):
-        own_ref[0, :, start : start + cols] = term
-
-    grad(0, put_own)
-
-    @pl.when(t < 2)
-    def _():
-        def put_x(start, cols, term):
-            sx_ref[0, 0, :, start : start + cols] = term
-
-        def put_d(start, cols, term):
-            sx_ref[1, 0, :, start : start + cols] = term
-
-        def put_y(start, cols, term):
-            ky_ref[0, :, start : start + cols] = term
-
-        grad(1, put_x)
-        grad(3, put_d)
-        grad(2, put_y)
-
-    @pl.when(t >= 2)
-    def _():
-        def put_y(start, cols, term):
-            sy_ref[0, 0, :, start : start + cols] = term
-
-        def put_d(start, cols, term):
-            sy_ref[1, 0, :, start : start + cols] = term
-
-        def put_x(start, cols, term):
-            kx_ref[0, :, start : start + cols] = term
-
-        grad(2, put_y)
-        grad(3, put_d)
-        grad(1, put_x)
-
-
-def wgrad(xs, ss, p):
-    rows, width = xs[0].shape
-    wrows = width // PLANE_BLOCKS
-    widths = [s.shape[1] // 4 for s in ss]
-    cols = sum(widths)
-    first = lambda t: jnp.minimum(t, 1)
-    last = lambda t: jnp.maximum(t - 2, 0)
-    return pl.pallas_call(
-        functools.partial(wgrad_body, len(xs)),
-        grid_spec=pltpu.PrefetchScalarGridSpec(
-            num_scalar_prefetch=1,
-            grid=(4,),
-            in_specs=[whole((rows, width)) for _ in xs]
-            + [pl.BlockSpec((rows, c), lambda t, p: (0, t)) for c in widths],
-            out_specs=[
-                pl.BlockSpec((1, wrows, cols), lambda t, p: (t, 0, 0)),
-                pl.BlockSpec((2, 1, wrows, cols), lambda t, p: (0, first(t), 0, 0)),
-                pl.BlockSpec((1, wrows, cols), lambda t, p: (last(t), 0, 0)),
-                pl.BlockSpec((2, 1, wrows, cols), lambda t, p: (0, last(t), 0, 0)),
-                pl.BlockSpec((1, wrows, cols), lambda t, p: (first(t), 0, 0)),
-            ],
-        ),
-        out_shape=[
-            sds((4, wrows, cols), NARROW),
-            sds((2, 2, wrows, cols), NARROW),
-            sds((2, wrows, cols), NARROW),
-            sds((2, 2, wrows, cols), NARROW),
-            sds((2, wrows, cols), NARROW),
-        ],
-        compiler_params=params(),
-        cost_estimate=cost(2 * rows * width * 4 * cols, 8 * width * cols + 4 * rows * width),
-        name="wgrad",
-    )(p, *xs, *ss)
-
-
-def wgrad_flat_body(count, p_ref, *refs):
-    p = p_ref[0]
-    out_ref = refs[-1]
-    for r in range(PLANE_BLOCKS):
-        start = 0
-        for x_ref, s_ref in zip(refs[:count], refs[count : 2 * count]):
-            width = x_ref.shape[1] // PLANE_BLOCKS
-            cols = s_ref.shape[1]
-            out_ref[0, r, :, start : start + cols] = lax.dot_general(
-                x_ref[:, rel_cols(p, r, width)],
-                s_ref[...],
-                (((0,), (0,)), ((), ())),
-                preferred_element_type=WIDE,
-            ).astype(NARROW)
-            start += cols
-
-
-def wgrad_flat(xs, ss, p):
-    rows, width = xs[0].shape
-    wrows = width // PLANE_BLOCKS
-    widths = [s.shape[1] // 4 for s in ss]
-    cols = sum(widths)
-    return pl.pallas_call(
-        functools.partial(wgrad_flat_body, len(xs)),
-        grid_spec=pltpu.PrefetchScalarGridSpec(
-            num_scalar_prefetch=1,
-            grid=(4,),
-            in_specs=[whole((rows, width)) for _ in xs]
-            + [pl.BlockSpec((rows, c), lambda t, p: (0, t)) for c in widths],
-            out_specs=pl.BlockSpec((1, PLANE_BLOCKS, wrows, cols), lambda t, p: (t, 0, 0, 0)),
-        ),
-        out_shape=sds((4, PLANE_BLOCKS, wrows, cols), NARROW),
-        compiler_params=params(),
-        cost_estimate=cost(2 * rows * width * 4 * cols, 8 * width * cols + 4 * rows * width),
-        name="wgrad_flat",
-    )(p, *xs, *ss)
-
-
 def combine_body(own_ref, rx_ref, ry_ref, fx_ref, fy_ref, out_ref):
     t = pl.program_id(0)
     near = jnp.where(t < 2, rx_ref[0, 0], ry_ref[0, 0])
@@ -424,6 +249,149 @@
         cost_estimate=cost(8 * rows * cols, 32 * rows * cols),
         name="combine",
     )(own, rx, ry, fx, fy)
+
+
+def write_grads(t, p, pairs, refs):
+    def grad(r, put):
+        start = 0
+        for x_ref, value in pairs:
+            width = x_ref.shape[1] // PLANE_BLOCKS
+            cols = value.shape[1]
+            term = lax.dot_general(
+                x_ref[:, rel_cols(p, r, width)],
+                value,
+                (((0,), (0,)), ((), ())),
+                preferred_element_type=WIDE,
+            ).astype(NARROW)
+            put(slice(start, start + cols), term)
+            start += cols
+
+    def into(ref, *place):
+        def put(cols, term):
+            ref[(*place, slice(None), cols)] = term
+
+        return put
+
+    if len(refs) == 1:
+        for r in range(PLANE_BLOCKS):
+            grad(r, into(refs[0], 0, r))
+        return
+    own_ref, sx_ref, kx_ref, sy_ref, ky_ref = refs
+    grad(0, into(own_ref, 0))
+
+    @pl.when(t < 2)
+    def _():
+        grad(1, into(sx_ref, 0, 0))
+        grad(3, into(sx_ref, 1, 0))
+        grad(2, into(ky_ref, 0))
+
+    @pl.when(t >= 2)
+    def _():
+        grad(2, into(sy_ref, 0, 0))
+        grad(3, into(sy_ref, 1, 0))
+        grad(1, into(kx_ref, 0))
+
+
+def grad_outs(wrows, cols, flat):
+    if flat:
+        shape = (4, PLANE_BLOCKS, wrows, cols)
+        spec = pl.BlockSpec((1, PLANE_BLOCKS, wrows, cols), lambda t, p: (t, 0, 0, 0))
+        return [spec], [sds(shape, NARROW)]
+    first = lambda t: jnp.minimum(t, 1)
+    last = lambda t: jnp.maximum(t - 2, 0)
+    specs = [
+        pl.BlockSpec((1, wrows, cols), lambda t, p: (t, 0, 0)),
+        pl.BlockSpec((2, 1, wrows, cols), lambda t, p: (0, first(t), 0, 0)),
+        pl.BlockSpec((1, wrows, cols), lambda t, p: (last(t), 0, 0)),
+        pl.BlockSpec((2, 1, wrows, cols), lambda t, p: (0, last(t), 0, 0)),
+        pl.BlockSpec((1, wrows, cols), lambda t, p: (first(t), 0, 0)),
+    ]
+    shapes = [
+        sds((4, wrows, cols), NARROW),
+        sds((2, 2, wrows, cols), NARROW),
+        sds((2, wrows, cols), NARROW),
+        sds((2, 2, wrows, cols), NARROW),
+        sds((2, wrows, cols), NARROW),
+    ]
+    return specs, shapes
+
+
+def expand_from(g_ref, w_refs, t, p):
+    width = g_ref.shape[1] // PLANE_BLOCKS
+    acc = None
+    for r, w in enumerate(weight_blocks(w_refs, t)):
+        term = jnp.dot(g_ref[:, rel_cols(p, r, width)], w, preferred_element_type=WIDE)
+        acc = term if acc is None else acc + term
+    return acc
+
+
+def reduce_into(acc_ref, value, w_refs, t, p):
+    width = acc_ref.shape[1] // PLANE_BLOCKS
+
+    @pl.when(t == 0)
+    def _():
+        acc_ref[...] = jnp.zeros_like(acc_ref)
+
+    for r, w in enumerate(weight_blocks(w_refs, t)):
+        acc_ref[:, rel_cols(p, r, width)] += lax.dot_general(
+            value, w, (((1,), (1,)), ((), ())), preferred_element_type=WIDE
+        )
+
+
+def ff_back_body(nr, ne, fr, p_ref, g_ref, a_ref, u_ref, *refs):
+    r_refs, e_refs = refs[:nr], refs[nr : nr + ne]
+    b_ref, gc_ref = refs[nr + ne : nr + ne + 2]
+    outs, acc_ref = refs[nr + ne + 2 : -1], refs[-1]
+    t = pl.program_id(0)
+    p = p_ref[0]
+    grad = expand_from(g_ref, r_refs, t, p)
+    u = u_ref[...]
+    logistic = sigmoid(u)
+    gu = grad * (logistic * (1.0 + u * (1.0 - logistic)))
+    gc_ref[...] = jnp.sum(gu, axis=0, keepdims=True)
+    low = gu.astype(NARROW)
+    reduce_into(acc_ref, low, e_refs, t, p)
+    write_grads(t, p, [(g_ref, (u * logistic).astype(NARROW))], outs[:fr])
+    write_grads(t, p, [(a_ref, low)], outs[fr:])
+
+    @pl.when(t == 3)
+    def _():
+        b_ref[...] = acc_ref[...].astype(NARROW)
+
+
+def ff_back(g, a, u, wr, we, p, flat):
+    rows, width = g.shape
+    cols = u.shape[1] // 4
+    wrows = width // PLANE_BLOCKS
+    r_specs, r_shapes = grad_outs(wrows, cols, flat)
+    e_specs, e_shapes = grad_outs(wrows, cols, False)
+    out = pl.pallas_call(
+        functools.partial(ff_back_body, len(wr), len(we), len(r_specs)),
+        grid_spec=pltpu.PrefetchScalarGridSpec(
+            num_scalar_prefetch=1,
+            grid=(4,),
+            in_specs=[
+                whole((rows, width)),
+                whole((rows, width)),
+                pl.BlockSpec((rows, cols), lambda t, p: (0, t)),
+                *weight_specs(wr, cols, 0),
+                *weight_specs(we, cols, 0),
+            ],
+            out_specs=[
+                whole((rows, width)),
+                pl.BlockSpec((1, cols), lambda t, p: (0, t)),
+                *r_specs,
+                *e_specs,
+            ],
+            scratch_shapes=[pltpu.VMEM((rows, width), WIDE)],
+        ),
+        out_shape=[sds((rows, width), NARROW), sds((1, 4 * cols), WIDE), *r_shapes, *e_shapes],
+        compiler_params=params(),
+        cost_estimate=cost(32 * rows * width * cols, 32 * width * cols),
+        name="ff_back",
+    )(p, g, a, u, *wr, *we)
+    g_r = out[2 : 2 + len(r_specs)]
+    return out[0], out[1], (g_r[0] if flat else g_r), out[2 + len(r_specs) :]
 
 
 def norm_back_body(scale, x_ref, gx_ref, pa_ref, pb_ref, g_ref, out_ref, low_ref, sums_ref):
@@ -513,33 +481,45 @@
     )(x, pa, pb, ob, cot, live, gain, bias)
 
 
-def distances(i0, keys):
-    rows = lax.broadcasted_iota(jnp.int32, (QROWS, keys), 0) + i0
-    cols = lax.broadcasted_iota(jnp.int32, (QROWS, keys), 1)
+def distances(i0, keys, rows_here):
+    rows = lax.broadcasted_iota(jnp.int32, (rows_here, keys), 0) + i0
+    cols = lax.broadcasted_iota(jnp.int32, (rows_here, keys), 1)
     return cols - rows, cols
+
+
+def head_lanes(rows, width, e):
+    lane = lax.broadcasted_iota(jnp.int32, (rows, width), 1)
+    return (lane >= e * HD) & (lane < (e + 1) * HD)
+
+
+def doubled(table, heads):
+    return jnp.concatenate([table] * heads, axis=1)
 
 
 def attend_body(len_ref, qkv_ref, table_ref, o_ref, p_out_ref):
     keys = qkv_ref.shape[0]
     width = qkv_ref.shape[1] // 3
+    heads = width // HD
     length = len_ref[0]
-    table = table_ref[...]
-
+    table_turned = jnp.transpose(doubled(table_ref[...], heads))
+    k_turned = jnp.transpose(qkv_ref[:, width : 2 * width])
+    v = qkv_ref[:, 2 * width :]
     key_live = lax.broadcasted_iota(jnp.int32, (QROWS, keys), 1) < length
+    masks = [head_lanes(QROWS, width, e) for e in range(heads)]
     for n in range(keys // QROWS):
         i0 = n * QROWS
         rows = slice(i0, i0 + QROWS)
-        begin = max(0, i0 - QROWS)
-        end = min(keys, i0 + 2 * QROWS)
+        begin = max(0, i0 - NEAR)
+        end = min(keys, i0 + QROWS + NEAR)
         span = end - begin
-        apart = distances(i0 - begin, span)[0]
+        apart = distances(i0 - begin, span, QROWS)[0]
         far_left = apart <= -LEFT
         far_right = apart >= RIGHT
-        for e in range(width // HD):
-            q = qkv_ref[rows, e * HD : (e + 1) * HD]
-            k = qkv_ref[:, width + e * HD : width + (e + 1) * HD]
-            v = qkv_ref[:, 2 * width + e * HD : 2 * width + (e + 1) * HD]
-            near = lax.dot_general(q, table, (((1,), (1,)), ((), ())), preferred_element_type=WIDE)
+        q_all = qkv_ref[rows, :width]
+        merged = None
+        for e in range(heads):
+            q = jnp.where(masks[e], q_all, jnp.zeros_like(q_all))
+            near = jnp.dot(q, table_turned, preferred_element_type=WIDE)
             left, right = near[:, 0:1], near[:, LEFT + RIGHT : LEFT + RIGHT + 1]
             band = jnp.concatenate([near, jnp.zeros((QROWS, span - NEAR), WIDE)], axis=1)
             band = pltpu.roll(band, (i0 - begin + span - LEFT) % span, 1, stride=1, stride_axis=0)
@@ -549,15 +529,15 @@
             if end < keys:
                 pieces.append(jnp.broadcast_to(right, (QROWS, keys - end)))
             rel = jnp.concatenate(pieces, axis=1) if len(pieces) > 1 else pieces[0]
-            s = lax.dot_general(q, k, (((1,), (1,)), ((), ())), preferred_element_type=WIDE)
+            s = jnp.dot(q, k_turned, preferred_element_type=WIDE)
             s = jnp.where(key_live, (s + rel) * HD ** (-0.5), MASKED)
             top = jnp.max(s, axis=-1, keepdims=True)
             ex = jnp.exp(s - top)
             chance = (ex * (1.0 / row_sum(ex))).astype(NARROW)
             p_out_ref[e, rows, :] = chance
-            o_ref[rows, e * HD : (e + 1) * HD] = jnp.dot(
-                chance, v, preferred_element_type=WIDE
-            ).astype(NARROW)
+            part = jnp.dot(chance, v, preferred_element_type=WIDE)
+            merged = part if merged is None else jnp.where(masks[e], part, merged)
+        o_ref[rows, :] = merged.astype(NARROW)
 
 
 def attend(qkv, table, length):
@@ -585,20 +565,21 @@
     )(length, qkv, table)
 
 
-def attend_back_body(qkv_ref, go_ref, p_ref, table_ref, out_ref, sums_ref, dist_ref, gk_ref, gv_ref):
+def attend_back_parts(qkv_ref, go_ref, p_ref, table_ref, out_ref, sums_ref, dist_ref, gk_ref, gv_ref):
     keys = qkv_ref.shape[0]
     width = qkv_ref.shape[1] // 3
-    table = table_ref[...]
+    heads = width // HD
+    table = doubled(table_ref[...], heads)
     scale = HD ** (-0.5)
-    nt = (((1,), (1,)), ((), ()))
     flip = (
-        lax.broadcasted_iota(jnp.int32, (QROWS, QROWS), 0)
-        + lax.broadcasted_iota(jnp.int32, (QROWS, QROWS), 1)
-        == QROWS - 1
+        lax.broadcasted_iota(jnp.int32, (BROWS, BROWS), 0)
+        + lax.broadcasted_iota(jnp.int32, (BROWS, BROWS), 1)
+        == BROWS - 1
     ).astype(NARROW)
-    bucket = lax.broadcasted_iota(jnp.int32, (QROWS, NEAR), 1)
+    bucket = lax.broadcasted_iota(jnp.int32, (BROWS, NEAR), 1)
     first_row = table[0:1, :].astype(WIDE)
     last_row = table[LEFT + RIGHT : LEFT + RIGHT + 1, :].astype(WIDE)
+    masks = [head_lanes(BROWS, width, e) for e in range(heads)]
 
     @pl.when(pl.program_id(0) == 0)
     def _():
@@ -606,32 +587,34 @@
 
     q_turned = jnp.transpose(qkv_ref[:, :width])
     go_turned = jnp.transpose(go_ref[...])
-    for n in range(keys // QROWS):
-        i0 = n * QROWS
-        rows = slice(i0, i0 + QROWS)
-        begin = max(0, i0 - QROWS)
-        end = min(keys, i0 + 2 * QROWS)
+    v_turned = jnp.transpose(qkv_ref[:, 2 * width :])
+    k = qkv_ref[:, width : 2 * width]
+    for n in range(keys // BROWS):
+        i0 = n * BROWS
+        rows = slice(i0, i0 + BROWS)
+        begin = max(0, i0 - NEAR)
+        end = min(keys, i0 + BROWS + NEAR)
         span = end - begin
-        apart = distances(i0 - begin, span)[0]
+        apart = distances(i0 - begin, span, BROWS)[0]
         far_left = apart <= -LEFT
         far_right = apart >= RIGHT
-        key_of = lax.broadcasted_iota(jnp.int32, (QROWS, NEAR), 0) + bucket + (i0 - LEFT)
+        key_of = lax.broadcasted_iota(jnp.int32, (BROWS, NEAR), 0) + bucket + (i0 - LEFT)
         inside = (bucket > 0) & (bucket < LEFT + RIGHT) & (key_of >= 0) & (key_of < keys)
-        for e in range(width // HD):
-            lanes = slice(e * HD, (e + 1) * HD)
-            q = qkv_ref[rows, lanes]
-            k = qkv_ref[:, width + e * HD : width + (e + 1) * HD]
-            v = qkv_ref[:, 2 * width + e * HD : 2 * width + (e + 1) * HD]
-            go = go_ref[rows, lanes]
+        q_wide = qkv_ref[rows, :width].astype(WIDE)
+        go_all = go_ref[rows, :]
+        merged = None
+        for e in range(heads):
+            some = slice(e * HD, (e + 1) * HD)
+            go = jnp.where(masks[e], go_all, jnp.zeros_like(go_all))
             chance = p_ref[e, rows, :]
             wide = chance.astype(WIDE)
-            gp = lax.dot_general(go, v, nt, preferred_element_type=WIDE)
-            gs = (wide * (gp - jnp.sum(gp * wide, axis=-1, keepdims=True))).astype(NARROW)
+            gp = jnp.dot(go, v_turned, preferred_element_type=WIDE)
+            gs = (wide * (gp - row_sum(gp * wide))).astype(NARROW)
             gsw = gs.astype(WIDE)
             window = gsw[:, begin:end]
             turned = jnp.dot(flip, gs[:, begin:end], preferred_element_type=WIDE)
             turned = pltpu.roll(
-                turned, (LEFT + 1 - QROWS - (i0 - begin)) % span, 1, stride=1, stride_axis=0
+                turned, (LEFT + 1 - BROWS - (i0 - begin)) % span, 1, stride=1, stride_axis=0
             )[:, :NEAR]
             back = jnp.dot(flip, turned.astype(NARROW), preferred_element_type=WIDE)
             left_sum = row_sum(jnp.where(far_left, window, 0.0))
@@ -646,54 +629,95 @@
             gq = jnp.dot(gs, k, preferred_element_type=WIDE) * scale
             gq += jnp.dot(near, table, preferred_element_type=WIDE)
             gq += left_sum * first_row + right_sum * last_row
-            out_ref[rows, lanes] = gq.astype(NARROW)
-            q_part = q_turned[lanes, rows]
-            qw = q.astype(WIDE)
+            merged = gq if merged is None else jnp.where(masks[e], gq, merged)
+            q_part = q_turned[some, rows]
             dist_ref[:HD, :] += jnp.dot(q_part, near, preferred_element_type=WIDE)
-            dist_ref[HD : HD + 1, :HD] += jnp.sum(left_sum * qw, axis=0, keepdims=True)
-            dist_ref[HD + 1 : HD + 2, :HD] += jnp.sum(right_sum * qw, axis=0, keepdims=True)
+            ends = HD + 2 * e
+            dist_ref[ends : ends + 1, :] += jnp.sum(left_sum * q_wide, axis=0, keepdims=True)
+            dist_ref[ends + 1 : ends + 2, :] += jnp.sum(right_sum * q_wide, axis=0, keepdims=True)
             gk = jnp.dot(q_part, gs, preferred_element_type=WIDE)
-            gv = jnp.dot(go_turned[lanes, rows], chance, preferred_element_type=WIDE)
+            gv = jnp.dot(go_turned[some, rows], chance, preferred_element_type=WIDE)
             if n == 0:
-                gk_ref[lanes, :] = gk
-                gv_ref[lanes, :] = gv
+                gk_ref[some, :] = gk
+                gv_ref[some, :] = gv
             else:
-                gk_ref[lanes, :] += gk
-                gv_ref[lanes, :] += gv
+                gk_ref[some, :] += gk
+                gv_ref[some, :] += gv
+        out_ref[rows, :width] = merged.astype(NARROW)
 
     out_ref[:, width : 2 * width] = jnp.transpose(gk_ref[...] * scale).astype(NARROW)
     out_ref[:, 2 * width :] = jnp.transpose(gv_ref[...]).astype(NARROW)
     sums_ref[...] = jnp.sum(out_ref[...].astype(WIDE), axis=0, keepdims=True)
 
 
-def attend_back(qkv, go, chances, table):
-    rows = qkv.shape[0]
-    width = qkv.shape[1] // 12
-    heads = width // HD
-    return pl.pallas_call(
-        attend_back_body,
-        grid=(4,),
-        in_specs=[
-            pl.BlockSpec((rows, 3 * width), lambda t: (0, t)),
-            pl.BlockSpec((rows, width), lambda t: (0, t)),
-            pl.BlockSpec((heads, rows, rows), lambda t: (t, 0, 0)),
-            whole(table.shape),
+def attend_back_body(
+    nw, s_ref, gm_ref, bn_ref, qkv_ref, chance_ref, o_ref, table_ref, *refs
+):
+    m_refs, w_refs = refs[:nw], refs[nw : 2 * nw]
+    b_ref, sums_ref, dist_ref = refs[2 * nw : 2 * nw + 3]
+    outs = refs[2 * nw + 3 : -5]
+    acc_ref, go_ref, out_ref, gk_ref, gv_ref = refs[-5:]
+    t = pl.program_id(0)
+    p = s_ref[0]
+    go_ref[...] = expand_from(gm_ref, m_refs, t, p).astype(NARROW)
+    attend_back_parts(
+        qkv_ref, go_ref, chance_ref, table_ref, out_ref, sums_ref, dist_ref, gk_ref, gv_ref
+    )
+    grad = out_ref[...]
+    reduce_into(acc_ref, grad, w_refs, t, p)
+    write_grads(t, p, [(bn_ref, grad), (gm_ref, o_ref[...])], outs)
+
+    @pl.when(t == 3)
+    def _():
+        b_ref[...] = acc_ref[...].astype(NARROW)
+
+
+def attend_back(gm, bn, qkv, chances, o, table, w, p):
+    rows, width = gm.shape
+    wrows = width // PLANE_BLOCKS
+    cols = qkv.shape[1] // 12
+    heads = cols // HD
+    g_specs, g_shapes = grad_outs(wrows, 4 * cols, False)
+    out = pl.pallas_call(
+        functools.partial(attend_back_body, len(w)),
+        grid_spec=pltpu.PrefetchScalarGridSpec(
+            num_scalar_prefetch=1,
+            grid=(4,),
+            in_specs=[
+                whole((rows, width)),
+                whole((rows, width)),
+                pl.BlockSpec((rows, 3 * cols), lambda t, p: (0, t)),
+                pl.BlockSpec((heads, rows, rows), lambda t, p: (t, 0, 0)),
+                pl.BlockSpec((rows, cols), lambda t, p: (0, t)),
+                whole(table.shape),
+                *weight_specs(w, cols, 3),
+                *weight_specs(w, 3 * cols, 0),
+            ],
+            out_specs=[
+                whole((rows, width)),
+                pl.BlockSpec((1, 3 * cols), lambda t, p: (0, t)),
+                whole((HD + 8, NEAR)),
+                *g_specs,
+            ],
+            scratch_shapes=[
+                pltpu.VMEM((rows, width), WIDE),
+                pltpu.VMEM((rows, cols), NARROW),
+                pltpu.VMEM((rows, 3 * cols), NARROW),
+                pltpu.VMEM((cols, rows), WIDE),
+                pltpu.VMEM((cols, rows), WIDE),
+            ],
+        ),
+        out_shape=[
+            sds((rows, width), NARROW),
+            sds((1, 12 * cols), WIDE),
+            sds((HD + 8, NEAR), WIDE),
+            *g_shapes,
         ],
-        out_specs=[
-            pl.BlockSpec((rows, 3 * width), lambda t: (0, t)),
-            pl.BlockSpec((1, 3 * width), lambda t: (0, t)),
-            whole((HD + 8, NEAR)),
-        ],
-        out_shape=[
-            sds((rows, 12 * width), NARROW),
-            sds((1, 12 * width), WIDE),
-            sds((HD + 8, NEAR), WIDE),
-        ],
-        scratch_shapes=[pltpu.VMEM((width, rows), WIDE), pltpu.VMEM((width, rows), WIDE)],
         compiler_params=params(),
         cost_estimate=cost(40 * heads * rows * rows * HD, 10 * heads * rows * rows),
         name="attend_back",
-    )(qkv, go, chances, table)
+    )(p, gm, bn, qkv, chances, o, table, *w, *w)
+    return out[0], out[1], out[2], out[3:]
 
 
 def lane_pair(first, second, rows):
@@ -714,15 +738,15 @@
 
     pad_ref[0:PAD, :] = jnp.zeros((PAD, pad_ref.shape[1]), WIDE)
     pad_ref[PAD:, :] = z_ref[...]
-    for start in range(0, rows, CHUNK):
+    for start in range(0, rows, MIX_CHUNK):
         total = None
         for i in range(taps_count):
             begin = start + PAD - taps_count + 1 + i
-            term = taps_ref[i : i + 1, :] * pad_ref[begin : begin + CHUNK, :]
+            term = taps_ref[i : i + 1, :] * pad_ref[begin : begin + MIX_CHUNK, :]
             total = term if total is None else total + term
-        here = slice(start, start + CHUNK)
+        here = slice(start, start + MIX_CHUNK)
         y_ref[here, :] = total
-        sums_ref[here, :] += lane_pair(row_sum(total), row_sum(total * total), CHUNK)
+        sums_ref[here, :] += lane_pair(row_sum(total), row_sum(total * total), MIX_CHUNK)
 
 
 def causal_mix(z, taps, taps_count):
@@ -853,7 +877,7 @@
     )(p, grad, y, *sums, gain, bias, *w)
 
 
-def mix_back_body(
+def mix_back_parts(
     taps_count, width, gyn_ref, y_ref, sa_ref, sb_ref, ra_ref, rb_ref, g_ref, z_ref, gate_ref,
     taps_ref, out_ref, grad_ref, gpad_ref, zpad_ref,
 ):
@@ -866,18 +890,18 @@
     unit = (y_ref[...] - mean) * std
     gpad_ref[0:rows, :] = std * (gyn_ref[...] * g_ref[...] - pair[:, 0:1] - unit * pair[:, 1:2])
     sums = [None] * taps_count
-    for start in range(0, rows, CHUNK):
-        here = slice(start, start + CHUNK)
+    for start in range(0, rows, MIX_CHUNK):
+        here = slice(start, start + MIX_CHUNK)
         gy = gpad_ref[here, :]
         total = None
         for i in range(taps_count):
             begin = start + taps_count - 1 - i
-            term = taps_ref[i : i + 1, :] * gpad_ref[begin : begin + CHUNK, :]
+            term = taps_ref[i : i + 1, :] * gpad_ref[begin : begin + MIX_CHUNK, :]
             total = term if total is None else total + term
         for i in range(taps_count):
             begin = start + PAD - taps_count + 1 + i
-            part = zpad_ref[begin : begin + CHUNK, :] * gy
-            part = jnp.sum(part.reshape(CHUNK // 8, 8, cols), axis=0)
+            part = zpad_ref[begin : begin + MIX_CHUNK, :] * gy
+            part = jnp.sum(part.reshape(MIX_CHUNK // 8, 8, cols), axis=0)
             sums[i] = part if sums[i] is None else sums[i] + part
         gate = gate_ref[here, :]
         first = total * gate
@@ -887,24 +911,59 @@
         grad_ref[i : i + 1, :] = jnp.sum(sums[i], axis=0, keepdims=True)
 
 
-def mix_back(gyn, y, sums, pairs, gain, z, gate, taps, taps_count, width):
+def mix_back_body(taps_count, width, nw, s_ref, *refs):
+    parts, gate_taps = refs[:8], refs[8:10]
+    cn_ref, gw_ref, wact_ref = refs[10:13]
+    w_refs = refs[13 : 13 + nw]
+    b_ref, grad_ref, flat_ref = refs[13 + nw : 16 + nw]
+    acc_ref, out_ref, gpad_ref, zpad_ref = refs[16 + nw :]
+    t = pl.program_id(0)
+    p = s_ref[0]
+    mix_back_parts(
+        taps_count, width, *parts, *gate_taps, out_ref, grad_ref, gpad_ref, zpad_ref
+    )
+    grad = out_ref[...]
+    reduce_into(acc_ref, grad, w_refs, t, p)
+    write_grads(t, p, [(cn_ref, grad), (gw_ref, wact_ref[...])], [flat_ref])
+
+    @pl.when(t == 3)
+    def _():
+        b_ref[...] = acc_ref[...].astype(NARROW)
+
+
+def mix_back(gyn, y, sums, pairs, gain, z, gate, taps, taps_count, cn, gw, act, w, p):
     rows, cols = z.shape
+    width = cn.shape[1]
+    wrows = width // PLANE_BLOCKS
     n = cols // 4
-    block = pl.BlockSpec((rows, n), lambda t: (0, t))
-    row = pl.BlockSpec((1, n), lambda t: (0, t))
+    block = pl.BlockSpec((rows, n), lambda t, p: (0, t))
+    row = pl.BlockSpec((1, n), lambda t, p: (0, t))
     lanes = whole((rows, LANES))
-    tap_block = pl.BlockSpec((taps.shape[0], n), lambda t: (0, t))
+    tap_block = pl.BlockSpec((taps.shape[0], n), lambda t, p: (0, t))
+    g_specs, g_shapes = grad_outs(wrows, 3 * n, True)
     return pl.pallas_call(
-        functools.partial(mix_back_body, taps_count, width),
-        grid=(4,),
-        in_specs=[block, block, lanes, lanes, lanes, lanes, row, block, block, tap_block],
-        out_specs=[pl.BlockSpec((rows, 2 * n), lambda t: (0, t)), tap_block],
-        out_shape=[sds((rows, 2 * cols), NARROW), sds(taps.shape, WIDE)],
-        scratch_shapes=[pltpu.VMEM((rows + PAD, n), WIDE), pltpu.VMEM((rows + PAD, n), WIDE)],
+        functools.partial(mix_back_body, taps_count, width, len(w)),
+        grid_spec=pltpu.PrefetchScalarGridSpec(
+            num_scalar_prefetch=1,
+            grid=(4,),
+            in_specs=[
+                block, block, lanes, lanes, lanes, lanes, row, block, block, tap_block,
+                whole((rows, width)), whole((rows, width)), block,
+                *weight_specs(w, 2 * n, 0),
+            ],
+            out_specs=[whole((rows, width)), tap_block, *g_specs],
+            scratch_shapes=[
+                pltpu.VMEM((rows, width), WIDE),
+                pltpu.VMEM((rows, 2 * n), NARROW),
+                pltpu.VMEM((rows + PAD, n), WIDE),
+                pltpu.VMEM((rows + PAD, n), WIDE),
+            ],
+        ),
+        out_shape=[sds((rows, width), NARROW), sds(taps.shape, WIDE), *g_shapes],
         compiler_params=params(),
         cost_estimate=cost(4 * taps_count * rows * cols, 20 * rows * cols),
         name="mix_back",
-    )(gyn, y, *sums, *pairs, gain, z, gate, taps)
+    )(p, gyn, y, *sums, *pairs, gain, z, gate, taps, cn, gw, act, *w)
 
 
 def halve_body(groups, core_ref, *refs):
@@ -1302,56 +1361,44 @@
         x3, f4, other_core(f4), bias_row(10), cot, live, gain_row(5), bias_row(5)
     )
 
-    g_r2 = wgrad_flat([gf2], [s2], p)
-    g_r2, gf2 = fence(g_r2, gf2)
+    b4, gc2, g_r2, g_e2 = ff_back(gf2, a2, u2, r2, e2, p, True)
+    g_r2, g_e2, b4 = fence(g_r2, g_e2, b4)
     z_r2 = tensor_sum(g_r2)
-    gu2, gc2 = back_expand("ff", gf2, r2, ffc, 0, p, u2)
-    g_e2 = wgrad([a2], [gu2], p)
-    g_e2, gu2 = fence(g_e2, gu2)
     e2h1 = hop1(g_e2)
-    b4 = reduce_mm(gu2, e2, ffc, 0, p, width)
     gx3, gw, sums3 = norm_back(1.0, x3, gx4, b4, other_core(b4), gain_row(4))
     gyn, depth_cols, depth_rows = filter_in(
         gw, y, y_sums, depth_gain, depth_bias, fil, cc, 2, p
     )
     depth_rows = (depth_rows, other_core(depth_rows))
-    gg, taps_grad = mix_back(
-        gyn, y, y_sums, depth_rows, depth_gain, z, gate, taps, taps_count, width
-    )
-    e2h1, gg = fence(e2h1, gg)
+    b3, taps_grad, g_fil = mix_back(
+        gyn, y, y_sums, depth_rows, depth_gain, z, gate, taps, taps_count, cn, gw, w, fil, p
+    )
+    e2h1, b3, g_fil = fence(e2h1, b3, g_fil)
     e2h2 = hop2(g_e2, e2h1)
-    g_fil = wgrad_flat([cn, gw], [gg, w], p)
     z_fil = tensor_sum(g_fil)
-    b3 = reduce_mm(gg, fil, 2 * cc, 0, p, width)
-    e2h2, b3, g_fil = fence(e2h2, b3, g_fil)
+    gx2, gm, sums2 = norm_back(1.0, x2, gx3, b3, other_core(b3), gain_row(2))
+    e2h2, gm = fence(e2h2, gm)
     z_e2 = hop3(g_e2, e2h1, e2h2)
-    gx2, gm, sums2 = norm_back(1.0, x2, gx3, b3, other_core(b3), gain_row(2))
-    go = back_expand("low", gm, att, qc, 3, p)
-    go, z_r2 = fence(go, z_r2)
-    r2x = across_x(z_r2)
-    gqkv, gqkv_sums, table_grad = attend_back(qkv, go, chances, table)
-    g_att = wgrad([bn, gm], [gqkv, o], p)
-    g_att, gqkv, r2x = fence(g_att, gqkv, r2x)
+    b2, gqkv_sums, table_grad, g_att = attend_back(gm, bn, qkv, chances, o, table, att, p)
+    g_att, b2, z_r2 = fence(g_att, b2, z_r2)
     atth1 = hop1(g_att)
-    b2 = reduce_mm(gqkv, att, 3 * qc, 0, p, width)
     gx1, gf1, sums1 = norm_back(0.5, x1, gx2, b2, other_core(b2), gain_row(1))
-    g_r1 = wgrad([gf1], [s1], p)
-    g_r1, gf1, atth1 = fence(g_r1, gf1, atth1)
+    outputs = send_home(out_rows)
+    b1, gc1, g_r1, g_e1 = ff_back(gf1, a1, u1, r1, e1, p, False)
+    g_r1, g_e1, b1, atth1, outputs = fence(g_r1, g_e1, b1, atth1, outputs)
     r1h1 = hop1(g_r1)
     atth2 = hop2(g_att, atth1)
-    gu1, gc1 = back_expand("ff", gf1, r1, ffc, 0, p, u1)
-    g_e1 = wgrad([a1], [gu1], p)
-    outputs = send_home(out_rows)
-    atth2, r1h1, g_e1, gu1, z_fil, outputs = fence(atth2, r1h1, g_e1, gu1, z_fil, outputs)
+    gx0, _, sums0 = norm_back(1.0, x0, gx1, b1, other_core(b1), gain_row(0))
+    atth2, r1h1, gx0, z_fil = fence(atth2, r1h1, gx0, z_fil)
     e1h1 = hop1(g_e1)
     r1h2 = hop2(g_r1, r1h1)
     z_att = hop3(g_att, atth1, atth2)
-    b1 = reduce_mm(gu1, e1, ffc, 0, p, width)
-    gx0, _, sums0 = norm_back(1.0, x0, gx1, b1, other_core(b1), gain_row(0))
 
     table_rows = -(-buckets // 8)
     tail = jnp.transpose(table_grad[:HD])[1 : buckets - 1]
     ends = table_grad[HD : HD + 2, :HD]
+    for e in range(1, qc // HD):
+        ends = ends + table_grad[HD + 2 * e : HD + 2 * e + 2, e * HD : (e + 1) * HD]
     tail = jnp.concatenate([ends[:1], tail, ends[1:]], axis=0)
     tail = jnp.pad(tail, ((0, 8 * table_rows - buckets), (0, 0)))
     tail = tail.reshape(table_rows, 8, HD).transpose(1, 0, 2).reshape(8, table_rows * HD)
@@ -1382,11 +1429,11 @@
     e1h2, planes_came = fence(e1h2, planes_came)
     t_e1, planes_came = fence(gathered(g_e1, e1h1, e1h2), planes_came)
     z_e1 = tensor_sum(t_e1)
-    filx, r2y = across_x(z_fil), across_y(z_r2, r2x)
+    filx, r2x = across_x(z_fil), across_x(z_r2)
     homeward = send_home(gx0.astype(NARROW))
     mine = over_parts(planes_came)
-    filx, r2y, mine, homeward, z_att = fence(filx, r2y, mine, homeward, z_att)
-    fily = across_y(z_fil, filx)
+    filx, r2x, mine, homeward, z_att = fence(filx, r2x, mine, homeward, z_att)
+    fily, r2y = across_y(z_fil, filx), across_y(z_r2, r2x)
     e2_grad, att_grad = share(z_e2), share(z_att)
     theirs = other_core(mine)
     r2_grad = share(across_end(z_r2, r2x, r2y))

time: 669 us -> 641 us (0.958)
  Pallas kernels: 241 us -> 189 us
  waiting for transfers between devices: 179 us -> 200 us
  starting transfers between devices: 80.2 us -> 95.8 us
  local copies, waits for them, and re-layouts: 100 us -> 90.8 us
    pallas_call x7 -> x3, Pallas kernels: 39.3 us -> 15.2 us  [reduce_mm(): pl.pallas_call(functools.partial(reduce_body, len(w)), grid_spec=pltpu.Pr...]
    ppermute x4, starting transfers between devices: 6.29 us -> 27.4 us  [bring(): blocks.append(lax.ppermute(block, ('pair', 'tensor'), route(turn)))]
    ppermute x4, waiting for transfers between devices: 0.85 us -> 19.7 us  [send_home(): came.append(lax.ppermute(blocks[turn], ('pair', 'tensor'), back))]
    ppermute x23, waiting for transfers between devices: 18.1 us -> 34.9 us  [step_y(): return lax.ppermute(v, 'plane', [(i, i ^ 2) for i in range(planes)])]
    pallas_call x4, Pallas kernels: 25.6 us -> 15.8 us  [norm_back(): pl.pallas_call(functools.partial(norm_back_body, scale), grid=(rows // CH...]
    all_gather x5, waiting for transfers between devices: 47.3 us -> 39.3 us  [column_of(): return lax.all_gather(shard, 'tensor', axis=0)]
    reduce_scatter x6, waiting for transfers between devices: 6.8 us -> 0.03 us  [tensor_sum(): return lax.psum_scatter(total, 'tensor', scatter_dimension=0)]
    unnamed x348 -> x252, local copies, waits for them, and re-layouts: 67.6 us -> 61 us
  transfers between devices with their start and end apart: 94 -> 94, of which waited for: 39 -> 42; matrix products, arithmetic and copies ran while one was open for 11% -> 11% of each run, Pallas kernels for 34% -> 25%
where the time goes in v3:
time: 641 us; the launch traced here: 634 us
  waiting for transfers between devices  200 us (31%)
  Pallas kernels  189 us (29%)
  starting transfers between devices  95.8 us (15%)
  local copies, waits for them, and re-layouts  90.8 us (14%)
  other arithmetic  42.9 us (7%)
  between operations  15.7 us (2%)
    ppermute x22, waiting for transfers between devices, step_x(): return lax.ppermute(v, 'plane', [(i, i ^ 1) for i in range(planes)])  80.7 us
    unnamed x252, local copies, waits for them, and re-layouts  61 us
    all_gather x5, waiting for transfers between devices, column_of(): return lax.all_gather(shard, 'tensor', axis=0)  39.3 us
    pallas_call x2, Pallas kernels, ff_back(): pl.pallas_call(functools.partial(ff_back_body, len(wr), len(we), len(r_sp...  36.4 us
    ppermute x23, waiting for transfers between devices, step_y(): return lax.ppermute(v, 'plane', [(i, i ^ 2) for i in range(planes)])  34.9 us
    pallas_call x4, Pallas kernels, norm_expand(): pl.pallas_call(functools.partial(expand_body, kind, merged, scale, len(w)...  32.4 us
    pallas_call x1, Pallas kernels, attend_back(): pl.pallas_call(functools.partial(attend_back_body, len(w)), grid_spec=plt...  27.7 us
    ppermute x23, starting transfers between devices, step_y(): return lax.ppermute(v, 'plane', [(i, i ^ 2) for i in range(planes)])  27.6 us
  transfers between devices with their start and end apart: 94, of which 42 were waited for; matrix products, arithmetic and copies ran while one was open for 11% of the time, Pallas kernels for 25%

profile of v3, /device:TPU:0, one launch (start us, length us, event | category | flops | bytes accessed | tf_op | source)
XLA Modules:
  0.0 634.5 jit_solution(5547712958540885786)
XLA Ops:
  33.5 6.2 collective-permute-done.7
  39.7 11.0 %all-gather.11.cloned.1.call-done = bf16[1024,512]{1,0:T(8,128)(2,1)} async-done(((bf16[256,512]{1,0:T(8,128)(2,1)}), bf16[1024,512]{1,0:T(8,128)(2,1)}) %all-gather.11.cloned.1.call-update) | async-done | bytes 1048592 | tf_op jit(solution)/shard_map/all_gather | solution.py:1122
  57.7 28.3 %all-gather.13.cloned.1.call-done = bf16[1024,512]{1,0:T(8,128)(2,1)} async-done(((bf16[256,512]{1,0:T(8,128)(2,1)}), bf16[1024,512]{1,0:T(8,128)(2,1)}) %all-gather.13.cloned.1.call-update) | async-done | bytes 1048592 | tf_op jit(solution)/shard_map/all_gather | solution.py:1122
  102.8 19.9 %collective-permute-start.18 = (bf16[128,1024]{1,0:T(8,128)(2,1)}, bf16[128,1024]{1,0:T(8,128)(2,1)S(1)}, u32[]{:S(2)}, u32[]{:S(2)}) collective-permute-start(bf16[128,1024]{1,0:T(8,128)(2,1)} %get-tuple-element.462), channel_id=1, source_target_pairs={{0,2},{1,0},{2,6},{3,4},{4,3},{5,1},{6,7},{7,5},{8,10},{9,8},{10,1... | collective-permute-start | bytes 786440 | tf_op jit(solution)/shard_map/ppermute | solution.py:1213
  144.4 8.0 %norm_expand_ff.2 = (bf16[512,1024]{1,0:T(8,128)(2,1)S(1)}, f32[512,2048]{1,0:T(8,128)}, bf16[512,2048]{1,0:T(8,128)(2,1)}) custom-call(s32[1]{0:T(128)} %bitcast.p_ref.s_ref, f32[512,1024]{1,0:T(8,128)} %convert_element_type.214.refs_0_.x_ref, f32[1,1024]{1,0:T(1,128)S(1)} %get-tuple-element.507.refs_1_.g_ref, f32[1,1024]{1,0:T(1,128)S(1)} %get-tuple-element.497.refs_2_, ...), custom_call_target="tpu_custom_call" | custom-call | flops 1073741 | bytes 5242 | tf_op jit(solution)/shard_map/norm_expand_ff/pallas_call | solution.py:168
  155.2 12.3 %collective-permute-done.19.refs_3_ = bf16[2,256,512]{2,1,0:T(8,128)(2,1)} collective-permute-done((bf16[2,256,512]{2,1,0:T(8,128)(2,1)}, bf16[2,256,512]{2,1,0:T(8,128)(2,1)}, u32[]{:S(2)}, u32[]{:S(2)}) %collective-permute-start.19) | collective-permute-done | bytes 524320 | tf_op jit(solution)/shard_map/ppermute | solution.py:1100
  173.5 5.7 reduce_mm.3.refs_1_
  190.2 7.9 %norm_expand_qkv.1 = (f32[512,1024]{1,0:T(8,128)}, bf16[512,1024]{1,0:T(8,128)(2,1)S(1)}, bf16[512,1536]{1,0:T(8,128)(2,1)}) custom-call(s32[1]{0:T(128)} %bitcast.p_ref.s_ref, f32[512,1024]{1,0:T(8,128)} %convert_element_type.214.refs_0_.x_ref, bf16[512,1024]{1,0:T(8,128)(2,1)S(1)} %copy-done.23, bf16[512,1024]{1,0:T(8,128)(2,1)S(1)} %collective-permute-done.26.refs_2_, ...), custom_call_target="tpu_custom_call" | custom-call | flops 805306 | bytes 4718 | tf_op jit(solution)/shard_map/norm_expand_qkv/pallas_call | solution.py:168
  203.5 12.0 %attend.1 = (bf16[512,512]{1,0:T(8,128)(2,1)S(1)}, bf16[8,512,512]{2,1,0:T(8,128)(2,1)}) custom-call(s32[1]{0:T(128)} %bitcast.23.len_ref, bf16[512,1536]{1,0:T(8,128)(2,1)S(1)} %copy-done.13, bf16[128,64]{1,0:T(8,128)(2,1)S(1)} %pad.16.table_ref), custom_call_target="tpu_custom_call" | custom-call | flops 268435 | bytes 2621 | tf_op jit(solution)/shard_map/attend/pallas_call | solution.py:547
  237.7 7.1 %norm_expand_conv.1 = (f32[512,1024]{1,0:T(8,128)}, bf16[512,1024]{1,0:T(8,128)(2,1)S(1)}, f32[512,512]{1,0:T(8,128)S(1)}, f32[512,512]{1,0:T(8,128)}) custom-call(s32[1]{0:T(128)} %bitcast.p_ref.s_ref, f32[512,1024]{1,0:T(8,128)} %get-tuple-element.256.refs_0_.x_ref, bf16[512,1024]{1,0:T(8,128)(2,1)} %copy-done.24, ...), custom_call_target="tpu_custom_call" | custom-call | flops 536870 | bytes 4194 | tf_op jit(solution)/shard_map/norm_expand_conv/pallas_call | solution.py:168
  252.1 7.7 %collective-permute-done.33.refs_7_.refs_5_ = bf16[4,256,512]{2,1,0:T(8,128)(2,1)} collective-permute-done((bf16[4,256,512]{2,1,0:T(8,128)(2,1)}, bf16[4,256,512]{2,1,0:T(8,128)(2,1)}, u32[]{:S(2)}, u32[]{:S(2)}) %collective-permute-start.33) | collective-permute-done | bytes 1048608 | tf_op jit(solution)/shard_map/ppermute | solution.py:1097
  266.8 5.8 filter_out.1
  279.8 9.4 %norm_expand_ff.3 = (f32[512,1024]{1,0:T(8,128)}, bf16[512,1024]{1,0:T(8,128)(2,1)S(1)}, f32[512,2048]{1,0:T(8,128)}, bf16[512,2048]{1,0:T(8,128)(2,1)}) custom-call(s32[1]{0:T(128)} %bitcast.p_ref.s_ref, f32[512,1024]{1,0:T(8,128)} %get-tuple-element.270.refs_0_.x_ref, bf16[512,1024]{1,0:T(8,128)(2,1)} %get-tuple-element.279.refs_1_, ...), custom_call_target="tpu_custom_call" | custom-call | flops 1073741 | bytes 5242 | tf_op jit(solution)/shard_map/norm_expand_ff/pallas_call | solution.py:168
  306.9 17.4 %ff_back.2 = (bf16[512,1024]{1,0:T(8,128)(2,1)}, f32[1,2048]{1,0:T(1,128)S(1)}, bf16[4,4,256,512]{3,2,1,0:T(8,128)(2,1)}, bf16[4,256,512]{2,1,0:T(8,128)(2,1)S(1...) custom-call(s32[1]{0:T(128)} %bitcast.p_ref.s_ref, ...), custom_call_target="tpu_custom_call" | custom-call | flops 4294967 | bytes 8388 | tf_op jit(solution)/shard_map/ff_back/pallas_call | solution.py:368
  343.7 15.9 %mix_back.1 = (bf16[512,1024]{1,0:T(8,128)(2,1)S(1)}, f32[32,512]{1,0:T(8,128)S(1)}, bf16[4,4,256,384]{3,2,1,0:T(8,128)(2,1)}) custom-call(s32[1]{0:T(128)} %bitcast.p_ref.s_ref, f32[512,512]{1,0:T(8,128)} %copy-done.51, f32[512,512]{1,0:T(8,128)} %copy-done.6, f32[512,128]{1,0:T(8,128)S(1)} %get-tuple-element.277.sa_ref.refs_2_, ...), custom_call_target="tpu_custom_call" | custom-call | flops 16252 | bytes 2621 | tf_op jit(solution)/shard_map/mix_back/pallas_call | solution.py:944
  371.6 5.9 collective-permute-done.46.fy_ref
  378.7 27.7 %attend_back.1 = (bf16[512,1024]{1,0:T(8,128)(2,1)}, f32[1,1536]{1,0:T(1,128)S(1)}, f32[72,128]{1,0:T(8,128)S(1)}, bf16[4,256,512]{2,1,0:T(8,128)(2,1)S(1)}, bf1...) custom-call(s32[1]{0:T(128)} %bitcast.p_ref.s_ref, ...), custom_call_target="tpu_custom_call" | custom-call | flops 671088 | bytes 2621 | tf_op jit(solution)/shard_map/attend_back/pallas_call | solution.py:681
  430.4 19.0 %ff_back.3 = (bf16[512,1024]{1,0:T(8,128)(2,1)S(1)}, f32[1,2048]{1,0:T(1,128)S(1)}, bf16[4,256,512]{2,1,0:T(8,128)(2,1)}, bf16[2,2,256,512]{3,2,1,0:T(8,128)(2,1...) custom-call(s32[1]{0:T(128)} %bitcast.p_ref.s_ref, ...), custom_call_target="tpu_custom_call" | custom-call | flops 4294967 | bytes 8388 | tf_op jit(solution)/shard_map/ff_back/pallas_call | solution.py:368
  452.7 12.4 %collective-permute-done.51 = bf16[128,1024]{1,0:T(8,128)(2,1)S(1)} collective-permute-done((bf16[128,1024]{1,0:T(8,128)(2,1)S(1)}, bf16[128,1024]{1,0:T(8,128)(2,1)S(1)}, u32[]{:S(2)}, u32[]{:S(2)}) %collective-permute-start.51) | collective-permute-done | bytes 262176 | tf_op jit(solution)/shard_map/ppermute | solution.py:1235
  478.7 24.6 %collective-permute-done.53.fy_ref = bf16[2,256,512]{2,1,0:T(8,128)(2,1)} collective-permute-done((bf16[2,256,512]{2,1,0:T(8,128)(2,1)}, bf16[2,256,512]{2,1,0:T(8,128)(2,1)}, u32[]{:S(2)}, u32[]{:S(2)}) %collective-permute-start.53) | collective-permute-done | bytes 524320 | tf_op jit(solution)/shard_map/ppermute | solution.py:1097
  525.8 10.8 %collective-permute-done.61.rx_ref = bf16[2,2,256,512]{3,2,1,0:T(8,128)(2,1)S(1)} collective-permute-done((bf16[2,2,256,512]{3,2,1,0:T(8,128)(2,1)}, bf16[2,2,256,512]{3,2,1,0:T(8,128)(2,1)S(1)}, u32[]{:S(2)}, u32[]{:S(2)}) %collective-permute-start.61) | collective-permute-done | bytes 1048608 | tf_op jit(solution)/shard_map/ppermute | solution.py:1097
  538.1 8.4 %collective-permute-done.60.fy_ref = bf16[2,256,512]{2,1,0:T(8,128)(2,1)} collective-permute-done((bf16[2,256,512]{2,1,0:T(8,128)(2,1)}, bf16[2,256,512]{2,1,0:T(8,128)(2,1)}, u32[]{:S(2)}, u32[]{:S(2)}) %collective-permute-start.60) | collective-permute-done | bytes 524320 | tf_op jit(solution)/shard_map/ppermute | solution.py:1097
  567.6 9.3 %collective-permute-done.65.fy_ref = bf16[2,256,512]{2,1,0:T(8,128)(2,1)S(1)} collective-permute-done((bf16[2,256,512]{2,1,0:T(8,128)(2,1)S(1)}, bf16[2,256,512]{2,1,0:T(8,128)(2,1)S(1)}, u32[]{:S(2)}, u32[]{:S(2)}) %collective-permute-start.65) | collective-permute-done | bytes 524320 | tf_op jit(solution)/shard_map/ppermute | solution.py:1097
  594.5 7.3 %collective-permute-done.73 = bf16[128,1024]{1,0:T(8,128)(2,1)S(1)} collective-permute-done((bf16[128,1024]{1,0:T(8,128)(2,1)}, bf16[128,1024]{1,0:T(8,128)(2,1)S(1)}, u32[]{:S(2)}, u32[]{:S(2)}) %collective-permute-start.73) | collective-permute-done | bytes 262176 | tf_op jit(solution)/shard_map/ppermute | solution.py:1235
  (580 shorter events, 318.8 us)
Async XLA Ops:
  7.2 43.6 %all-gather.11.cloned.1.call-start = ((), (), s32[]{:S(2)}) async-start(), calls=%async_computation.12 | async-start | bytes 1310720 | tf_op jit(solution)/shard_map/all_gather | solution.py:1122
  20.1 65.9 %all-gather.13.cloned.1.call-start = ((), (), s32[]{:S(2)}) async-start(), calls=%async_computation.13 | async-start | bytes 1310720 | tf_op jit(solution)/shard_map/all_gather | solution.py:1122
  20.8 104.3 %all-gather.15.cloned.1.call-start = ((), (), s32[]{:S(2)}) async-start(), calls=%async_computation.14 | async-start | bytes 1310720 | tf_op jit(solution)/shard_map/all_gather | solution.py:1122
  21.6 158.6 %all-gather.17.cloned.1.call-start = ((), (), s32[]{:S(2)}) async-start(), calls=%async_computation.15 | async-start | bytes 2293760 | tf_op jit(solution)/shard_map/all_gather | solution.py:1122
  22.2 268.1 %all-gather.19.cloned.1.call-start = ((), (), s32[]{:S(2)}) async-start(), calls=%async_computation.16 | async-start | bytes 5242880 | tf_op jit(solution)/shard_map/all_gather | solution.py:1122
  50.8 35.2 %collective-permute-start.8 = (bf16[4,256,512]{2,1,0:T(8,128)(2,1)}, bf16[4,256,512]{2,1,0:T(8,128)(2,1)S(1)}, u32[]{:S(2)}, u32[]{:S(2)}) collective-permute-start(bf16[4,256,512]{2,1,0:T(8,128)(2,1)} %bitcast.194), channel_id=1, source_target_pairs={{0,8},{8,0},{16,24},{24,16},{1,9},{9,1},{17,25},{25,17},{2,10},{10... | collective-permute-start | bytes 3145736 | tf_op jit(solution)/shard_map/ppermute | solution.py:1097
  52.2 33.8 %collective-permute-start.9 = (bf16[4,256,512]{2,1,0:T(8,128)(2,1)}, bf16[4,256,512]{2,1,0:T(8,128)(2,1)S(1)}, u32[]{:S(2)}, u32[]{:S(2)}) collective-permute-start(bf16[4,256,512]{2,1,0:T(8,128)(2,1)} %bitcast.195), channel_id=1, source_target_pairs={{0,16},{8,24},{16,0},{24,8},{1,17},{9,25},{17,1},{25,9},{2,18},{10... | collective-permute-start | bytes 3145736 | tf_op jit(solution)/shard_map/ppermute | solution.py:1100
  86.8 43.2 %collective-permute-start.14 = (bf16[4,256,512]{2,1,0:T(8,128)(2,1)}, bf16[4,256,512]{2,1,0:T(8,128)(2,1)S(1)}, u32[]{:S(2)}, u32[]{:S(2)}) collective-permute-start(bf16[4,256,512]{2,1,0:T(8,128)(2,1)} %bitcast.198), channel_id=1, source_target_pairs={{0,8},{8,0},{16,24},{24,16},{1,9},{9,1},{17,25},{25,17},{2,10},{10... | collective-permute-start | bytes 3145736 | tf_op jit(solution)/shard_map/ppermute | solution.py:1097
  87.7 42.3 %collective-permute-start.15 = (bf16[4,256,512]{2,1,0:T(8,128)(2,1)}, bf16[4,256,512]{2,1,0:T(8,128)(2,1)}, u32[]{:S(2)}, u32[]{:S(2)}) collective-permute-start(bf16[4,256,512]{2,1,0:T(8,128)(2,1)} %bitcast.199), channel_id=1, source_target_pairs={{0,16},{8,24},{16,0},{24,8},{1,17},{9,25},{17,1},{25,9},{2,18},{10... | collective-permute-start | bytes 3145736 | tf_op jit(solution)/shard_map/ppermute | solution.py:1100
  102.7 307.4 %reduce-scatter.7.cloned.1.call-start = ((), (), s32[]{:S(2)}) async-start(), calls=%async_computation.6 | async-start | bytes 5242880 | tf_op jit(solution)/shard_map/reduce_scatter | solution.py:1146
  131.0 36.5 %collective-permute-start.21 = (bf16[4,256,512]{2,1,0:T(8,128)(2,1)}, bf16[4,256,512]{2,1,0:T(8,128)(2,1)S(1)}, u32[]{:S(2)}, u32[]{:S(2)}) collective-permute-start(bf16[4,256,512]{2,1,0:T(8,128)(2,1)} %bitcast.188), channel_id=1, source_target_pairs={{0,8},{8,0},{16,24},{24,16},{1,9},{9,1},{17,25},{25,17},{2,10},{10... | collective-permute-start | bytes 3145736 | tf_op jit(solution)/shard_map/ppermute | solution.py:1097
  131.2 36.4 %collective-permute-start.22 = (bf16[4,256,512]{2,1,0:T(8,128)(2,1)}, bf16[4,256,512]{2,1,0:T(8,128)(2,1)S(1)}, u32[]{:S(2)}, u32[]{:S(2)}) collective-permute-start(bf16[4,256,512]{2,1,0:T(8,128)(2,1)} %bitcast.189), channel_id=1, source_target_pairs={{0,16},{8,24},{16,0},{24,8},{1,17},{9,25},{17,1},{25,9},{2,18},{10... | collective-permute-start | bytes 3145736 | tf_op jit(solution)/shard_map/ppermute | solution.py:1100
  328.4 150.2 %reduce-scatter.9.cloned.1.call-start = ((), (), s32[]{:S(2)}) async-start(), calls=%async_computation.7 | async-start | bytes 3932160 | tf_op jit(solution)/shard_map/reduce_scatter | solution.py:1146
  360.5 165.3 %reduce-scatter.11.cloned.1.call-start = ((), (), s32[]{:S(2)}) async-start(), calls=%async_computation.8 | async-start | bytes 1310720 | tf_op jit(solution)/shard_map/reduce_scatter | solution.py:1146
  410.1 55.0 %collective-permute-start.48 = (bf16[2,2,256,512]{3,2,1,0:T(8,128)(2,1)}, bf16[2,2,256,512]{3,2,1,0:T(8,128)(2,1)S(1)}, u32[]{:S(2)}, u32[]{:S(2)}) collective-permute-start(bf16[2,2,256,512]{3,2,1,0:T(8,128)(2,1)} %copy-done.95), channel_id=1, source_target_pairs={{0,8},{8,0},{16,24},{24,16},{1,9},{9,1},{17,25},{25,17},{2,10},{10... | collective-permute-start | bytes 3145736 | tf_op jit(solution)/shard_map/ppermute | solution.py:1097
  410.8 54.2 %collective-permute-start.49 = (bf16[2,2,256,512]{3,2,1,0:T(8,128)(2,1)}, bf16[2,2,256,512]{3,2,1,0:T(8,128)(2,1)S(1)}, u32[]{:S(2)}, u32[]{:S(2)}) collective-permute-start(bf16[2,2,256,512]{3,2,1,0:T(8,128)(2,1)} %get-tuple-element.344), channel_id=1, source_target_pairs={{0,16},{8,24},{16,0},{24,8},{1,17},{9,25},{17,1},{25,9},{2,18},{10... | collective-permute-start | bytes 3145736 | tf_op jit(solution)/shard_map/ppermute | solution.py:1100
  418.6 183.2 %reduce-scatter.13.cloned.1.call-start = ((), (), s32[]{:S(2)}) async-start(), calls=%async_computation.9 | async-start | bytes 1310720 | tf_op jit(solution)/shard_map/reduce_scatter | solution.py:1146
  419.8 32.8 %collective-permute-start.50 = (bf16[128,1024]{1,0:T(8,128)(2,1)S(1)}, bf16[128,1024]{1,0:T(8,128)(2,1)S(1)}, u32[]{:S(2)}, u32[]{:S(2)}) collective-permute-start(bf16[128,1024]{1,0:T(8,128)(2,1)S(1)} %get-tuple-element.449), channel_id=1, source_target_pairs={{0,0},{2,1},{4,2},{6,3},{1,4},{3,5},{5,6},{7,7},{8,8},{10,9},{12,1... | collective-permute-start | bytes 786440 | tf_op jit(solution)/shard_map/ppermute | solution.py:1235
  420.5 44.5 %collective-permute-start.51 = (bf16[128,1024]{1,0:T(8,128)(2,1)S(1)}, bf16[128,1024]{1,0:T(8,128)(2,1)S(1)}, u32[]{:S(2)}, u32[]{:S(2)}) collective-permute-start(bf16[128,1024]{1,0:T(8,128)(2,1)S(1)} %get-tuple-element.448), channel_id=1, source_target_pairs={{2,0},{0,1},{6,2},{4,3},{3,4},{1,5},{7,6},{5,7},{10,8},{8,9},{14,1... | collective-permute-start | bytes 786440 | tf_op jit(solution)/shard_map/ppermute | solution.py:1235
  466.1 37.4 %collective-permute-start.54 = (bf16[2,2,256,512]{3,2,1,0:T(8,128)(2,1)}, bf16[2,2,256,512]{3,2,1,0:T(8,128)(2,1)S(1)}, u32[]{:S(2)}, u32[]{:S(2)}) collective-permute-start(bf16[2,2,256,512]{3,2,1,0:T(8,128)(2,1)} %get-tuple-element.352), channel_id=1, source_target_pairs={{0,8},{8,0},{16,24},{24,16},{1,9},{9,1},{17,25},{25,17},{2,10},{10... | collective-permute-start | bytes 3145736 | tf_op jit(solution)/shard_map/ppermute | solution.py:1097
  466.2 37.3 %collective-permute-start.55 = (bf16[2,2,256,512]{3,2,1,0:T(8,128)(2,1)}, bf16[2,2,256,512]{3,2,1,0:T(8,128)(2,1)S(1)}, u32[]{:S(2)}, u32[]{:S(2)}) collective-permute-start(bf16[2,2,256,512]{3,2,1,0:T(8,128)(2,1)} %get-tuple-element.353), channel_id=1, source_target_pairs={{0,16},{8,24},{16,0},{24,8},{1,17},{9,25},{17,1},{25,9},{2,18},{10... | collective-permute-start | bytes 3145736 | tf_op jit(solution)/shard_map/ppermute | solution.py:1100
  470.4 32.8 %collective-permute-start.53 = (bf16[2,256,512]{2,1,0:T(8,128)(2,1)}, bf16[2,256,512]{2,1,0:T(8,128)(2,1)}, u32[]{:S(2)}, u32[]{:S(2)}) collective-permute-start(bf16[2,256,512]{2,1,0:T(8,128)(2,1)} %fusion.4), channel_id=1, source_target_pairs={{0,8},{8,0},{16,24},{24,16},{1,9},{9,1},{17,25},{25,17},{2,10},{10... | collective-permute-start | bytes 1572872 | tf_op jit(solution)/shard_map/ppermute | solution.py:1097
  510.0 110.5 %reduce-scatter.17.cloned.1.call-start = ((), (), s32[]{:S(2)}) async-start(), calls=%async_computation.11 | async-start | bytes 1310720 | tf_op jit(solution)/shard_map/reduce_scatter | solution.py:1146
  553.6 68.8 %reduce-scatter.15.cloned.1.call-start = ((), (), s32[]{:S(2)}) async-start(), calls=%async_computation.10 | async-start | bytes 1310720 | tf_op jit(solution)/shard_map/reduce_scatter | solution.py:1146
  (193 other events, 1825.4 us)
Sparse Core Ops, SparseCore 0:
  20.2 30.4 all-gather.10
  52.9 33.0 all-gather.12
  88.1 33.7 all-gather.14
  124.0 40.2 all-gather.16
  165.7 79.6 all-gather.18
  328.6 74.2 reduce-scatter.6
  405.3 68.9 reduce-scatter.8
  476.7 28.6 reduce-scatter.10
  510.1 25.1 reduce-scatter.12
  553.7 24.9 reduce-scatter.16
  593.3 27.2 reduce-scatter.14

commit v4 on v3

--- a/solution.py
+++ b/solution.py
@@ -1205,13 +1205,13 @@
                 pairs.append((spot(c, t), spot(t // 2, 2 * mb + c)))
         return pairs
 
+    def bring_one(v, turn):
+        mb = lax.rem(turn + part, 2)
+        block = lax.dynamic_index_in_dim(v[:, 0], mb, 0, False)
+        return lax.ppermute(block, ("pair", "tensor"), route(turn))
+
     def bring(v):
-        blocks = []
-        for turn in range(2):
-            mb = lax.rem(turn + part, 2)
-            block = lax.dynamic_index_in_dim(v[:, 0], mb, 0, False)
-            blocks.append(lax.ppermute(block, ("pair", "tensor"), route(turn)))
-        return blocks
+        return [bring_one(v, turn) for turn in range(2)]
 
     def settle(blocks):
         swap = part // 2 == 1
@@ -1293,11 +1293,11 @@
         sz = step_y(sx)
         col_e1, sx, sy, sz, source = fence(col_e1, sx, sy, sz, inputs)
         r2 = (column_of(jnp.stack([sd, sx, sy, sz])),) * PLANE_BLOCKS
-        e1n, blocks = near(col_e1), bring(source)
-        e1n, r1c, blocks, source = fence(e1n, r1c, blocks, cotangent)
-        e1f, r1n, x0 = far(e1n), near(r1c), settle(blocks)
-        cot = bring(source)
-        e1f, e1n, r1n, attc, x0, cot = fence(e1f, e1n, r1n, attc, x0, cot)
+        e1n, block0 = near(col_e1), bring_one(source, 0)
+        e1n, r1c, block0, source = fence(e1n, r1c, block0, source)
+        e1f, r1n, block1 = far(e1n), near(r1c), bring_one(source, 1)
+        e1f, e1n, r1n, attc, block1, source = fence(e1f, e1n, r1n, attc, block1, cotangent)
+        x0, cot0 = settle([block0, block1]), bring_one(source, 0)
         e1 = (col_e1, *e1n, *e1f)
         r1f, attn = far(r1n), near(attc)
     else:
@@ -1313,12 +1313,13 @@
     x0 = x0.astype(WIDE)
     a1, u1, s1 = norm_expand("ff", x0, None, 0.5, gain_row(0), bias_row(0), e1, ffc, 0, p, hidden1)
     if quick:
-        cot = settle(cot)
-        r1f, r1n, attn, s1, cot = fence(r1f, r1n, attn, s1, cot)
+        r1f, r1n, attn, s1, cot0, source = fence(r1f, r1n, attn, s1, cot0, source)
+        cot1 = bring_one(source, 1)
         r1, attf = (r1c, *r1n, *r1f), far(attn)
     f1 = reduce_mm(s1, r1, ffc, 0, p, width)
     if quick:
-        attf, attn, f1, col_c = fence(attf, attn, f1, col_c)
+        attf, attn, f1, col_c, cot1 = fence(attf, attn, f1, col_c, cot1)
+        cot = settle([cot0, cot1])
         att = (attc, *attn, *attf)
     f1o = other_core(f1)
     x1, bn, qkv = norm_expand(
@@ -1383,13 +1384,13 @@
     g_att, b2, z_r2 = fence(g_att, b2, z_r2)
     atth1 = hop1(g_att)
     gx1, gf1, sums1 = norm_back(0.5, x1, gx2, b2, other_core(b2), gain_row(1))
+    b1, gc1, g_r1, g_e1 = ff_back(gf1, a1, u1, r1, e1, p, False)
+    g_r1, g_e1, b1, atth1 = fence(g_r1, g_e1, b1, atth1)
     outputs = send_home(out_rows)
-    b1, gc1, g_r1, g_e1 = ff_back(gf1, a1, u1, r1, e1, p, False)
-    g_r1, g_e1, b1, atth1, outputs = fence(g_r1, g_e1, b1, atth1, outputs)
     r1h1 = hop1(g_r1)
     atth2 = hop2(g_att, atth1)
     gx0, _, sums0 = norm_back(1.0, x0, gx1, b1, other_core(b1), gain_row(0))
-    atth2, r1h1, gx0, z_fil = fence(atth2, r1h1, gx0, z_fil)
+    atth2, r1h1, gx0, z_fil, outputs = fence(atth2, r1h1, gx0, z_fil, outputs)
     e1h1 = hop1(g_e1)
     r1h2 = hop2(g_r1, r1h1)
     z_att = hop3(g_att, atth1, atth2)
@@ -1422,7 +1423,8 @@
     half = small.shape[0] // 2
     mine = lax.dynamic_slice_in_dim(small, core * half, half, 0)
     came = other_core(lax.dynamic_slice_in_dim(small, (1 - core) * half, half, 0))
-    r1h2, e1h1, gx0, came, z_e2 = fence(r1h2, e1h1, gx0, came, z_e2)
+    homeward = send_home(gx0.astype(NARROW))
+    r1h2, e1h1, came, z_e2, homeward = fence(r1h2, e1h1, came, z_e2, homeward)
     e1h2 = hop2(g_e1, e1h1)
     z_r1 = hop3(g_r1, r1h1, r1h2)
     planes_came = over_planes(mine + came)
@@ -1430,9 +1432,8 @@
     t_e1, planes_came = fence(gathered(g_e1, e1h1, e1h2), planes_came)
     z_e1 = tensor_sum(t_e1)
     filx, r2x = across_x(z_fil), across_x(z_r2)
-    homeward = send_home(gx0.astype(NARROW))
     mine = over_parts(planes_came)
-    filx, r2x, mine, homeward, z_att = fence(filx, r2x, mine, homeward, z_att)
+    filx, r2x, mine, z_att = fence(filx, r2x, mine, z_att)
     fily, r2y = across_y(z_fil, filx), across_y(z_r2, r2x)
     e2_grad, att_grad = share(z_e2), share(z_att)
     theirs = other_core(mine)

time: 641 us -> 612 us (0.955)
  waiting for transfers between devices: 200 us -> 178 us
    ppermute x22, waiting for transfers between devices: 80.7 us -> 54.1 us  [step_x(): return lax.ppermute(v, 'plane', [(i, i ^ 1) for i in range(planes)])]
    all_gather x5, waiting for transfers between devices: 39.3 us -> 60.1 us  [column_of(): return lax.all_gather(shard, 'tensor', axis=0)]
    ppermute x4, starting transfers between devices: 27.4 us -> 6.97 us  [bring_one(): return lax.ppermute(block, ('pair', 'tensor'), route(turn))]
    ppermute x4, starting transfers between devices: 5.5 us -> 22.7 us  [send_home(): came.append(lax.ppermute(blocks[turn], ('pair', 'tensor'), back))]
    ppermute x4, waiting for transfers between devices: 19.7 us -> 8.37 us  [send_home(): came.append(lax.ppermute(blocks[turn], ('pair', 'tensor'), back))]
    unnamed x252 -> x250, local copies, waits for them, and re-layouts: 61 us -> 56.7 us
  transfers between devices with their start and end apart: 94 -> 94, of which waited for: 42 -> 37; matrix products, arithmetic and copies ran while one was open for 11% -> 11% of each run, Pallas kernels for 25% -> 27%
where the time goes in v4:
time: 612 us; the launch traced here: 603 us
  Pallas kernels  191 us (31%)
  waiting for transfers between devices  178 us (29%)
  starting transfers between devices  92.6 us (15%)
  local copies, waits for them, and re-layouts  85.2 us (14%)
  other arithmetic  40.9 us (7%)
  between operations  15.7 us (3%)
    all_gather x5, waiting for transfers between devices, column_of(): return lax.all_gather(shard, 'tensor', axis=0)  60.1 us
    unnamed x250, local copies, waits for them, and re-layouts  56.7 us
    ppermute x22, waiting for transfers between devices, step_x(): return lax.ppermute(v, 'plane', [(i, i ^ 1) for i in range(planes)])  54.1 us
    pallas_call x2, Pallas kernels, ff_back(): pl.pallas_call(functools.partial(ff_back_body, len(wr), len(we), len(r_sp...  36.3 us
    ppermute x23, waiting for transfers between devices, step_y(): return lax.ppermute(v, 'plane', [(i, i ^ 2) for i in range(planes)])  35.2 us
    pallas_call x4, Pallas kernels, norm_expand(): pl.pallas_call(functools.partial(expand_body, kind, merged, scale, len(w)...  32.2 us
    pallas_call x1, Pallas kernels, attend_back(): pl.pallas_call(functools.partial(attend_back_body, len(w)), grid_spec=plt...  27.8 us
    ppermute x22, starting transfers between devices, step_x(): return lax.ppermute(v, 'plane', [(i, i ^ 1) for i in range(planes)])  26.9 us
  transfers between devices with their start and end apart: 94, of which 37 were waited for; matrix products, arithmetic and copies ran while one was open for 11% of the time, Pallas kernels for 27%

profile of v4, /device:TPU:0, one launch (start us, length us, event | category | flops | bytes accessed | tf_op | source)
XLA Modules:
  0.0 603.4 jit_solution(14490026833540886050)
XLA Ops:
  33.6 6.1 %collective-permute-done.7 = bf16[256,512]{1,0:T(8,128)(2,1)S(1)} collective-permute-done((bf16[256,512]{1,0:T(8,128)(2,1)S(1)}, bf16[256,512]{1,0:T(8,128)(2,1)S(1)}, u32[]{:S(2)}, u32[]{:S(2)}) %collective-permute-start.7) | collective-permute-done | bytes 262176 | tf_op jit(solution)/shard_map/ppermute | solution.py:1100
  39.7 11.1 %all-gather.11.cloned.1.call-done = bf16[1024,512]{1,0:T(8,128)(2,1)} async-done(((bf16[256,512]{1,0:T(8,128)(2,1)}), bf16[1024,512]{1,0:T(8,128)(2,1)}) %all-gather.11.cloned.1.call-update) | async-done | bytes 1048592 | tf_op jit(solution)/shard_map/all_gather | solution.py:1122
  54.5 26.7 %all-gather.13.cloned.1.call-done = bf16[1024,512]{1,0:T(8,128)(2,1)} async-done(((bf16[256,512]{1,0:T(8,128)(2,1)}), bf16[1024,512]{1,0:T(8,128)(2,1)}) %all-gather.13.cloned.1.call-update) | async-done | bytes 1048592 | tf_op jit(solution)/shard_map/all_gather | solution.py:1122
  92.9 22.0 %all-gather.15.cloned.1.call-done = bf16[1024,512]{1,0:T(8,128)(2,1)} async-done(((bf16[256,512]{1,0:T(8,128)(2,1)}), bf16[1024,512]{1,0:T(8,128)(2,1)}) %all-gather.15.cloned.1.call-update) | async-done | bytes 1048592 | tf_op jit(solution)/shard_map/all_gather | solution.py:1122
  131.9 7.7 %norm_expand_ff.2 = (bf16[512,1024]{1,0:T(8,128)(2,1)S(1)}, f32[512,2048]{1,0:T(8,128)}, bf16[512,2048]{1,0:T(8,128)(2,1)}) custom-call(s32[1]{0:T(128)} %bitcast.p_ref.s_ref, f32[512,1024]{1,0:T(8,128)} %maximum_convert_fusion.refs_0_.x_ref, f32[1,1024]{1,0:T(1,128)S(1)} %get-tuple-element.501.refs_1_.g_ref, f32[1,1024]{1,0:T(1,128)S(1)} %get-tuple-element.491.refs_2_, ...), custom_call_target="tpu_custom_call" | custom-call | flops 1073741 | bytes 5242 | tf_op jit(solution)/shard_map/norm_expand_ff/pallas_call | solution.py:168
  139.7 14.9 %collective-permute-done.17.refs_3_ = bf16[2,256,512]{2,1,0:T(8,128)(2,1)S(1)} collective-permute-done((bf16[2,256,512]{2,1,0:T(8,128)(2,1)S(1)}, bf16[2,256,512]{2,1,0:T(8,128)(2,1)S(1)}, u32[]{:S(2)}, u32[]{:S(2)}) %collective-permute-start.17) | collective-permute-done | bytes 524320 | tf_op jit(solution)/shard_map/ppermute | solution.py:1100
  162.3 5.5 reduce_mm.3.refs_1_
  175.4 8.2 %norm_expand_qkv.1 = (f32[512,1024]{1,0:T(8,128)}, bf16[512,1024]{1,0:T(8,128)(2,1)S(1)}, bf16[512,1536]{1,0:T(8,128)(2,1)}) custom-call(s32[1]{0:T(128)} %bitcast.p_ref.s_ref, f32[512,1024]{1,0:T(8,128)} %maximum_convert_fusion.refs_0_.x_ref, bf16[512,1024]{1,0:T(8,128)(2,1)S(1)} %copy-done.21, bf16[512,1024]{1,0:T(8,128)(2,1)S(1)} %collective-permute-done.25.refs_2_, ...), custom_call_target="tpu_custom_call" | custom-call | flops 805306 | bytes 4718 | tf_op jit(solution)/shard_map/norm_expand_qkv/pallas_call | solution.py:168
  188.3 11.9 %attend.1 = (bf16[512,512]{1,0:T(8,128)(2,1)S(1)}, bf16[8,512,512]{2,1,0:T(8,128)(2,1)}) custom-call(s32[1]{0:T(128)} %bitcast.23.len_ref, bf16[512,1536]{1,0:T(8,128)(2,1)S(1)} %copy-done.12, bf16[128,64]{1,0:T(8,128)(2,1)S(1)} %pad.16.table_ref), custom_call_target="tpu_custom_call" | custom-call | flops 268435 | bytes 2621 | tf_op jit(solution)/shard_map/attend/pallas_call | solution.py:547
  222.7 7.1 %norm_expand_conv.1 = (f32[512,1024]{1,0:T(8,128)}, bf16[512,1024]{1,0:T(8,128)(2,1)S(1)}, f32[512,512]{1,0:T(8,128)S(1)}, f32[512,512]{1,0:T(8,128)}) custom-call(s32[1]{0:T(128)} %bitcast.p_ref.s_ref, f32[512,1024]{1,0:T(8,128)} %get-tuple-element.254.refs_0_.x_ref, bf16[512,1024]{1,0:T(8,128)(2,1)} %reduce_mm.4.refs_1_, ...), custom_call_target="tpu_custom_call" | custom-call | flops 536870 | bytes 4194 | tf_op jit(solution)/shard_map/norm_expand_conv/pallas_call | solution.py:168
  236.5 8.0 %collective-permute-done.32.refs_7_.refs_5_ = bf16[4,256,512]{2,1,0:T(8,128)(2,1)S(1)} collective-permute-done((bf16[4,256,512]{2,1,0:T(8,128)(2,1)}, bf16[4,256,512]{2,1,0:T(8,128)(2,1)S(1)}, u32[]{:S(2)}, u32[]{:S(2)}) %collective-permute-start.32) | collective-permute-done | bytes 1048608 | tf_op jit(solution)/shard_map/ppermute | solution.py:1097
  250.9 5.8 filter_out.1
  264.3 9.2 %norm_expand_ff.3 = (f32[512,1024]{1,0:T(8,128)}, bf16[512,1024]{1,0:T(8,128)(2,1)S(1)}, f32[512,2048]{1,0:T(8,128)}, bf16[512,2048]{1,0:T(8,128)(2,1)}) custom-call(s32[1]{0:T(128)} %bitcast.p_ref.s_ref, f32[512,1024]{1,0:T(8,128)} %get-tuple-element.268.refs_0_.x_ref, bf16[512,1024]{1,0:T(8,128)(2,1)} %get-tuple-element.277.refs_1_, ...), custom_call_target="tpu_custom_call" | custom-call | flops 1073741 | bytes 5242 | tf_op jit(solution)/shard_map/norm_expand_ff/pallas_call | solution.py:168
  276.1 5.7 reduce_mm.5.pa_ref
  292.4 17.1 %ff_back.2 = (bf16[512,1024]{1,0:T(8,128)(2,1)S(1)}, f32[1,2048]{1,0:T(1,128)S(1)}, bf16[4,4,256,512]{3,2,1,0:T(8,128)(2,1)}, bf16[4,256,512]{2,1,0:T(8,128)(2,1...) custom-call(s32[1]{0:T(128)} %bitcast.p_ref.s_ref, ...), custom_call_target="tpu_custom_call" | custom-call | flops 4294967 | bytes 8388 | tf_op jit(solution)/shard_map/ff_back/pallas_call | solution.py:368
  329.8 15.9 %mix_back.1 = (bf16[512,1024]{1,0:T(8,128)(2,1)S(1)}, f32[32,512]{1,0:T(8,128)S(1)}, bf16[4,4,256,384]{3,2,1,0:T(8,128)(2,1)}) custom-call(s32[1]{0:T(128)} %bitcast.p_ref.s_ref, f32[512,512]{1,0:T(8,128)} %copy-done.54, f32[512,512]{1,0:T(8,128)} %copy-done.8, f32[512,128]{1,0:T(8,128)S(1)} %get-tuple-element.275.sa_ref.refs_2_, ...), custom_call_target="tpu_custom_call" | custom-call | flops 16252 | bytes 2621 | tf_op jit(solution)/shard_map/mix_back/pallas_call | solution.py:944
  365.2 27.8 %attend_back.1 = (bf16[512,1024]{1,0:T(8,128)(2,1)}, f32[1,1536]{1,0:T(1,128)S(1)}, f32[72,128]{1,0:T(8,128)S(1)}, bf16[4,256,512]{2,1,0:T(8,128)(2,1)S(1)}, bf1...) custom-call(s32[1]{0:T(128)} %bitcast.p_ref.s_ref, ...), custom_call_target="tpu_custom_call" | custom-call | flops 671088 | bytes 2621 | tf_op jit(solution)/shard_map/attend_back/pallas_call | solution.py:681
  410.2 19.2 %ff_back.3 = (bf16[512,1024]{1,0:T(8,128)(2,1)}, f32[1,2048]{1,0:T(1,128)S(1)}, bf16[4,256,512]{2,1,0:T(8,128)(2,1)}, bf16[2,2,256,512]{3,2,1,0:T(8,128)(2,1)}, ...) custom-call(s32[1]{0:T(128)} %bitcast.p_ref.s_ref, ...), custom_call_target="tpu_custom_call" | custom-call | flops 4294967 | bytes 8388 | tf_op jit(solution)/shard_map/ff_back/pallas_call | solution.py:368
  443.1 15.5 %collective-permute-start.56 = (bf16[128,1024]{1,0:T(8,128)(2,1)S(1)}, bf16[128,1024]{1,0:T(8,128)(2,1)}, u32[]{:S(2)}, u32[]{:S(2)}) collective-permute-start(bf16[128,1024]{1,0:T(8,128)(2,1)S(1)} %get-tuple-element.446), channel_id=1, source_target_pairs={{2,0},{0,1},{6,2},{4,3},{3,4},{1,5},{7,6},{5,7},{10,8},{8,9},{14,1... | collective-permute-start | bytes 786440 | tf_op jit(solution)/shard_map/ppermute | solution.py:1235
  464.4 6.8 %collective-permute-done.51.fy_ref = bf16[2,256,512]{2,1,0:T(8,128)(2,1)} collective-permute-done((bf16[2,256,512]{2,1,0:T(8,128)(2,1)}, bf16[2,256,512]{2,1,0:T(8,128)(2,1)}, u32[]{:S(2)}, u32[]{:S(2)}) %collective-permute-start.51) | collective-permute-done | bytes 524320 | tf_op jit(solution)/shard_map/ppermute | solution.py:1097
  492.7 11.9 %collective-permute-done.59.rx_ref = bf16[2,2,256,512]{3,2,1,0:T(8,128)(2,1)S(1)} collective-permute-done((bf16[2,2,256,512]{3,2,1,0:T(8,128)(2,1)}, bf16[2,2,256,512]{3,2,1,0:T(8,128)(2,1)S(1)}, u32[]{:S(2)}, u32[]{:S(2)}) %collective-permute-start.59) | collective-permute-done | bytes 1048608 | tf_op jit(solution)/shard_map/ppermute | solution.py:1097
  514.6 8.4 %collective-permute-done.63 = bf16[128,1024]{1,0:T(8,128)(2,1)} collective-permute-done((bf16[128,1024]{1,0:T(8,128)(2,1)}, bf16[128,1024]{1,0:T(8,128)(2,1)}, u32[]{:S(2)}, u32[]{:S(2)}) %collective-permute-start.63) | collective-permute-done | bytes 262176 | tf_op jit(solution)/shard_map/ppermute | solution.py:1235
  544.1 8.4 %collective-permute-done.65.fy_ref = bf16[2,256,512]{2,1,0:T(8,128)(2,1)S(1)} collective-permute-done((bf16[2,256,512]{2,1,0:T(8,128)(2,1)S(1)}, bf16[2,256,512]{2,1,0:T(8,128)(2,1)S(1)}, u32[]{:S(2)}, u32[]{:S(2)}) %collective-permute-start.65) | collective-permute-done | bytes 524320 | tf_op jit(solution)/shard_map/ppermute | solution.py:1097
  562.3 5.2 collective-permute-done.74
  (579 shorter events, 301.7 us)
Async XLA Ops:
  7.2 43.6 %all-gather.11.cloned.1.call-start = ((), (), s32[]{:S(2)}) async-start(), calls=%async_computation.12 | async-start | bytes 1310720 | tf_op jit(solution)/shard_map/all_gather | solution.py:1122
  20.2 61.0 %all-gather.13.cloned.1.call-start = ((), (), s32[]{:S(2)}) async-start(), calls=%async_computation.13 | async-start | bytes 1310720 | tf_op jit(solution)/shard_map/all_gather | solution.py:1122
  20.9 94.0 %all-gather.15.cloned.1.call-start = ((), (), s32[]{:S(2)}) async-start(), calls=%async_computation.14 | async-start | bytes 1310720 | tf_op jit(solution)/shard_map/all_gather | solution.py:1122
  21.6 147.6 %all-gather.17.cloned.1.call-start = ((), (), s32[]{:S(2)}) async-start(), calls=%async_computation.15 | async-start | bytes 2293760 | tf_op jit(solution)/shard_map/all_gather | solution.py:1122
  22.2 252.3 %all-gather.19.cloned.1.call-start = ((), (), s32[]{:S(2)}) async-start(), calls=%async_computation.16 | async-start | bytes 5242880 | tf_op jit(solution)/shard_map/all_gather | solution.py:1122
  81.2 37.5 %collective-permute-start.13 = (bf16[4,256,512]{2,1,0:T(8,128)(2,1)}, bf16[4,256,512]{2,1,0:T(8,128)(2,1)}, u32[]{:S(2)}, u32[]{:S(2)}) collective-permute-start(bf16[4,256,512]{2,1,0:T(8,128)(2,1)} %bitcast.198), channel_id=1, source_target_pairs={{0,8},{8,0},{16,24},{24,16},{1,9},{9,1},{17,25},{25,17},{2,10},{10... | collective-permute-start | bytes 3145736 | tf_op jit(solution)/shard_map/ppermute | solution.py:1097
  82.0 36.7 %collective-permute-start.14 = (bf16[4,256,512]{2,1,0:T(8,128)(2,1)}, bf16[4,256,512]{2,1,0:T(8,128)(2,1)}, u32[]{:S(2)}, u32[]{:S(2)}) collective-permute-start(bf16[4,256,512]{2,1,0:T(8,128)(2,1)} %bitcast.199), channel_id=1, source_target_pairs={{0,16},{8,24},{16,0},{24,8},{1,17},{9,25},{17,1},{25,9},{2,18},{10... | collective-permute-start | bytes 3145736 | tf_op jit(solution)/shard_map/ppermute | solution.py:1100
  84.3 33.6 %collective-permute-start.11 = (bf16[2,256,512]{2,1,0:T(8,128)(2,1)}, bf16[2,256,512]{2,1,0:T(8,128)(2,1)S(1)}, u32[]{:S(2)}, u32[]{:S(2)}) collective-permute-start(bf16[2,256,512]{2,1,0:T(8,128)(2,1)} %slice.240), channel_id=1, source_target_pairs={{0,16},{8,24},{16,0},{24,8},{1,17},{9,25},{17,1},{25,9},{2,18},{10... | collective-permute-start | bytes 1572872 | tf_op jit(solution)/shard_map/ppermute | solution.py:1100
  85.7 33.0 %collective-permute-start.12 = (bf16[2,256,512]{2,1,0:T(8,128)(2,1)}, bf16[2,256,512]{2,1,0:T(8,128)(2,1)}, u32[]{:S(2)}, u32[]{:S(2)}) collective-permute-start(bf16[2,256,512]{2,1,0:T(8,128)(2,1)} %slice.241), channel_id=1, source_target_pairs={{0,8},{8,0},{16,24},{24,16},{1,9},{9,1},{17,25},{25,17},{2,10},{10... | collective-permute-start | bytes 1572872 | tf_op jit(solution)/shard_map/ppermute | solution.py:1097
  92.8 303.3 %reduce-scatter.7.cloned.1.call-start = ((), (), s32[]{:S(2)}) async-start(), calls=%async_computation.6 | async-start | bytes 5242880 | tf_op jit(solution)/shard_map/reduce_scatter | solution.py:1146
  118.7 35.8 %collective-permute-start.19 = (bf16[4,256,512]{2,1,0:T(8,128)(2,1)}, bf16[4,256,512]{2,1,0:T(8,128)(2,1)S(1)}, u32[]{:S(2)}, u32[]{:S(2)}) collective-permute-start(bf16[4,256,512]{2,1,0:T(8,128)(2,1)} %bitcast.188), channel_id=1, source_target_pairs={{0,8},{8,0},{16,24},{24,16},{1,9},{9,1},{17,25},{25,17},{2,10},{10... | collective-permute-start | bytes 3145736 | tf_op jit(solution)/shard_map/ppermute | solution.py:1097
  119.9 34.7 %collective-permute-start.20 = (bf16[4,256,512]{2,1,0:T(8,128)(2,1)}, bf16[4,256,512]{2,1,0:T(8,128)(2,1)S(1)}, u32[]{:S(2)}, u32[]{:S(2)}) collective-permute-start(bf16[4,256,512]{2,1,0:T(8,128)(2,1)} %bitcast.189), channel_id=1, source_target_pairs={{0,16},{8,24},{16,0},{24,8},{1,17},{9,25},{17,1},{25,9},{2,18},{10... | collective-permute-start | bytes 3145736 | tf_op jit(solution)/shard_map/ppermute | solution.py:1100
  313.6 150.8 %reduce-scatter.9.cloned.1.call-start = ((), (), s32[]{:S(2)}) async-start(), calls=%async_computation.7 | async-start | bytes 3932160 | tf_op jit(solution)/shard_map/reduce_scatter | solution.py:1146
  345.7 168.9 %reduce-scatter.11.cloned.1.call-start = ((), (), s32[]{:S(2)}) async-start(), calls=%async_computation.8 | async-start | bytes 1310720 | tf_op jit(solution)/shard_map/reduce_scatter | solution.py:1146
  396.2 37.0 %collective-permute-start.48 = (bf16[2,2,256,512]{3,2,1,0:T(8,128)(2,1)}, bf16[2,2,256,512]{3,2,1,0:T(8,128)(2,1)S(1)}, u32[]{:S(2)}, u32[]{:S(2)}) collective-permute-start(bf16[2,2,256,512]{3,2,1,0:T(8,128)(2,1)} %get-tuple-element.343), channel_id=1, source_target_pairs={{0,8},{8,0},{16,24},{24,16},{1,9},{9,1},{17,25},{25,17},{2,10},{10... | collective-permute-start | bytes 3145736 | tf_op jit(solution)/shard_map/ppermute | solution.py:1097
  396.9 36.3 %collective-permute-start.49 = (bf16[2,2,256,512]{3,2,1,0:T(8,128)(2,1)}, bf16[2,2,256,512]{3,2,1,0:T(8,128)(2,1)S(1)}, u32[]{:S(2)}, u32[]{:S(2)}) collective-permute-start(bf16[2,2,256,512]{3,2,1,0:T(8,128)(2,1)} %get-tuple-element.344), channel_id=1, source_target_pairs={{0,16},{8,24},{16,0},{24,8},{1,17},{9,25},{17,1},{25,9},{2,18},{10... | collective-permute-start | bytes 3145736 | tf_op jit(solution)/shard_map/ppermute | solution.py:1100
  403.6 167.1 %reduce-scatter.17.cloned.1.call-start = ((), (), s32[]{:S(2)}) async-start(), calls=%async_computation.11 | async-start | bytes 1310720 | tf_op jit(solution)/shard_map/reduce_scatter | solution.py:1146
  434.8 37.3 %collective-permute-start.52 = (bf16[2,2,256,512]{3,2,1,0:T(8,128)(2,1)}, bf16[2,2,256,512]{3,2,1,0:T(8,128)(2,1)S(1)}, u32[]{:S(2)}, u32[]{:S(2)}) collective-permute-start(bf16[2,2,256,512]{3,2,1,0:T(8,128)(2,1)} %get-tuple-element.348), channel_id=1, source_target_pairs={{0,8},{8,0},{16,24},{24,16},{1,9},{9,1},{17,25},{25,17},{2,10},{10... | collective-permute-start | bytes 3145736 | tf_op jit(solution)/shard_map/ppermute | solution.py:1097
  435.8 36.3 %collective-permute-start.53 = (bf16[2,2,256,512]{3,2,1,0:T(8,128)(2,1)}, bf16[2,2,256,512]{3,2,1,0:T(8,128)(2,1)S(1)}, u32[]{:S(2)}, u32[]{:S(2)}) collective-permute-start(bf16[2,2,256,512]{3,2,1,0:T(8,128)(2,1)} %get-tuple-element.349), channel_id=1, source_target_pairs={{0,16},{8,24},{16,0},{24,8},{1,17},{9,25},{17,1},{25,9},{2,18},{10... | collective-permute-start | bytes 3145736 | tf_op jit(solution)/shard_map/ppermute | solution.py:1100
  478.3 111.1 %reduce-scatter.15.cloned.1.call-start = ((), (), s32[]{:S(2)}) async-start(), calls=%async_computation.10 | async-start | bytes 1310720 | tf_op jit(solution)/shard_map/reduce_scatter | solution.py:1146
  480.2 32.6 %collective-permute-start.60 = (bf16[2,2,256,512]{3,2,1,0:T(8,128)(2,1)}, bf16[2,2,256,512]{3,2,1,0:T(8,128)(2,1)}, u32[]{:S(2)}, u32[]{:S(2)}) collective-permute-start(bf16[2,2,256,512]{3,2,1,0:T(8,128)(2,1)} %get-tuple-element.362), channel_id=1, source_target_pairs={{0,16},{8,24},{16,0},{24,8},{1,17},{9,25},{17,1},{25,9},{2,18},{10... | collective-permute-start | bytes 3145736 | tf_op jit(solution)/shard_map/ppermute | solution.py:1100
  483.1 39.9 %collective-permute-start.58 = (bf16[2,256,512]{2,1,0:T(8,128)(2,1)}, bf16[2,256,512]{2,1,0:T(8,128)(2,1)}, u32[]{:S(2)}, u32[]{:S(2)}) collective-permute-start(bf16[2,256,512]{2,1,0:T(8,128)(2,1)} %fusion.2), channel_id=1, source_target_pairs={{0,8},{8,0},{16,24},{24,16},{1,9},{9,1},{17,25},{25,17},{2,10},{10... | collective-permute-start | bytes 1572872 | tf_op jit(solution)/shard_map/ppermute | solution.py:1097
  486.6 36.5 %collective-permute-start.57 = (bf16[2,256,512]{2,1,0:T(8,128)(2,1)}, bf16[2,256,512]{2,1,0:T(8,128)(2,1)}, u32[]{:S(2)}, u32[]{:S(2)}) collective-permute-start(bf16[2,256,512]{2,1,0:T(8,128)(2,1)} %fusion.3), channel_id=1, source_target_pairs={{0,16},{8,24},{16,0},{24,8},{1,17},{9,25},{17,1},{25,9},{2,18},{10... | collective-permute-start | bytes 1572872 | tf_op jit(solution)/shard_map/ppermute | solution.py:1100
  527.9 63.4 %reduce-scatter.13.cloned.1.call-start = ((), (), s32[]{:S(2)}) async-start(), calls=%async_computation.9 | async-start | bytes 1310720 | tf_op jit(solution)/shard_map/reduce_scatter | solution.py:1146
  (192 other events, 1783.8 us)
Sparse Core Ops, SparseCore 0:
  20.3 30.4 all-gather.10
  52.9 28.1 all-gather.12
  83.3 31.5 all-gather.14
  116.9 52.3 all-gather.16
  170.6 78.8 all-gather.18
  313.1 75.7 reduce-scatter.6
  391.4 63.4 reduce-scatter.8
  457.3 31.5 reduce-scatter.10
  491.2 31.3 reduce-scatter.16
  528.0 25.1 reduce-scatter.14
  562.4 25.0 reduce-scatter.12

commit v5 on v4

--- a/solution.py
+++ b/solution.py
@@ -21,6 +21,7 @@
 BROWS = 512
 NEAR = 128
 VMEM_BYTES = 48 * 1024 * 1024
+MOST_VMEM = 60 * 1024 * 1024
 PLANE_BLOCKS = 4
 LANES = 128
 COST_PART = 0.0005
@@ -31,10 +32,8 @@
     return jax.ShapeDtypeStruct(shape, dtype)
 
 
-def params(parallel=1):
-    return pltpu.CompilerParams(
-        dimension_semantics=("arbitrary",) * parallel, vmem_limit_bytes=VMEM_BYTES
-    )
+def params(limit=VMEM_BYTES):
+    return pltpu.CompilerParams(dimension_semantics=("arbitrary",), vmem_limit_bytes=limit)
 
 
 def cost(flops, moved, exps=0):
@@ -86,7 +85,7 @@
     return center * inv_std, inv_std
 
 
-def expand_body(kind, merged, scale, nw, p_ref, *refs):
+def expand_body(kind, merged, scale, nw, nr, p_ref, *refs):
     refs = list(refs)
     x_ref = refs.pop(0)
     if merged:
@@ -94,7 +93,8 @@
         refs = refs[3:]
     g_ref, b_ref = refs[:2]
     w_refs = refs[2 : 2 + nw]
-    refs = refs[2 + nw :]
+    r_refs = refs[2 + nw : 2 + nw + nr]
+    refs = refs[2 + nw + nr :]
     if kind != "conv":
         hb_ref = refs.pop(0)
     if merged:
@@ -127,7 +127,16 @@
     if kind == "ff":
         u = acc + hb_ref[...]
         outs[0][...] = u
-        outs[1][...] = (u * sigmoid(u)).astype(NARROW)
+        s = (u * sigmoid(u)).astype(NARROW)
+        if nr == 0:
+            outs[1][...] = s
+        else:
+            f_ref, acc_ref = outs[1:]
+            reduce_into(acc_ref, s, r_refs, t, p)
+
+            @pl.when(t == 3)
+            def _():
+                f_ref[...] = acc_ref[...].astype(NARROW)
     elif kind == "qkv":
         outs[0][...] = (acc + hb_ref[...]).astype(NARROW)
     else:
@@ -137,7 +146,7 @@
         outs[1][...] = acc[:, :half] * gate
 
 
-def norm_expand(kind, x, merge, scale, gain, bias, w, cols, col_block, p, hidden_bias):
+def norm_expand(kind, x, merge, scale, gain, bias, w, cols, col_block, p, hidden_bias, wr=()):
     rows, width = x.shape
     merged = merge is not None
     ins = [x]
@@ -145,8 +154,10 @@
     if merged:
         ins += list(merge)
         specs += [whole((rows, width)), whole((rows, width)), whole((1, width))]
-    ins += [gain, bias, *w]
+    ins += [gain, bias, *w, *wr]
     specs += [whole((1, width)), whole((1, width)), *weight_specs(w, cols, col_block)]
+    if wr:
+        specs += weight_specs(wr, cols, 0)
     if kind != "conv":
         ins.append(hidden_bias)
         specs.append(pl.BlockSpec((1, cols), lambda t, p: (0, t)))
@@ -157,7 +168,7 @@
     shapes.append(sds((rows, width), NARROW))
     out_specs.append(whole((rows, width)))
     if kind == "ff":
-        outs = [(cols, WIDE), (cols, NARROW)]
+        outs = [(cols, WIDE)] if wr else [(cols, WIDE), (cols, NARROW)]
     elif kind == "qkv":
         outs = [(cols, NARROW)]
     else:
@@ -165,10 +176,14 @@
     for out_cols, dtype in outs:
         shapes.append(sds((rows, 4 * out_cols), dtype))
         out_specs.append(pl.BlockSpec((rows, out_cols), lambda t, p: (0, t)))
+    if wr:
+        shapes.append(sds((rows, width), NARROW))
+        out_specs.append(whole((rows, width)))
     return pl.pallas_call(
-        functools.partial(expand_body, kind, merged, scale, len(w)),
+        functools.partial(expand_body, kind, merged, scale, len(w), len(wr)),
         grid_spec=pltpu.PrefetchScalarGridSpec(
-            num_scalar_prefetch=1, grid=(4,), in_specs=specs, out_specs=out_specs
+            num_scalar_prefetch=1, grid=(4,), in_specs=specs, out_specs=out_specs,
+            scratch_shapes=[pltpu.VMEM((rows, width), WIDE)] if wr else [],
         ),
         out_shape=shapes,
         compiler_params=params(),
@@ -386,7 +401,7 @@
             scratch_shapes=[pltpu.VMEM((rows, width), WIDE)],
         ),
         out_shape=[sds((rows, width), NARROW), sds((1, 4 * cols), WIDE), *r_shapes, *e_shapes],
-        compiler_params=params(),
+        compiler_params=params(MOST_VMEM),
         cost_estimate=cost(32 * rows * width * cols, 32 * width * cols),
         name="ff_back",
     )(p, g, a, u, *wr, *we)
@@ -713,7 +728,7 @@
             sds((HD + 8, NEAR), WIDE),
             *g_shapes,
         ],
-        compiler_params=params(),
+        compiler_params=params(MOST_VMEM),
         cost_estimate=cost(40 * heads * rows * rows * HD, 10 * heads * rows * rows),
         name="attend_back",
     )(p, gm, bn, qkv, chances, o, table, *w, *w)
@@ -960,7 +975,7 @@
             ],
         ),
         out_shape=[sds((rows, width), NARROW), sds(taps.shape, WIDE), *g_shapes],
-        compiler_params=params(),
+        compiler_params=params(MOST_VMEM),
         cost_estimate=cost(4 * taps_count * rows * cols, 20 * rows * cols),
         name="mix_back",
     )(p, gyn, y, *sums, *pairs, gain, z, gate, taps, cn, gw, act, *w)
@@ -1353,11 +1368,10 @@
     else:
         cot = settle(bring(cotangent))
     f3o = other_core(f3)
-    x3, a2, u2, s2 = norm_expand(
+    x3, a2, u2, f4 = norm_expand(
         "ff", x2, (f3, f3o, jnp.zeros((1, width), WIDE)), 1.0, gain_row(4), bias_row(4),
-        e2, ffc, 0, p, hidden2,
+        e2, ffc, 0, p, hidden2, r2,
     )
-    f4 = reduce_mm(s2, r2, ffc, 0, p, width)
     out_rows, gx4, gf2, sums_final = final_norm(
         x3, f4, other_core(f4), bias_row(10), cot, live, gain_row(5), bias_row(5)
     )

time: 612 us -> 601 us (0.982)
  local copies, waits for them, and re-layouts: 85.2 us -> 75.2 us
    unnamed x250 -> x240, local copies, waits for them, and re-layouts: 56.7 us -> 47.2 us
    pallas_call x3 -> x2, Pallas kernels: 16.1 us -> 10.3 us  [reduce_mm(): pl.pallas_call(functools.partial(reduce_body, len(w)), grid_spec=pltpu.Pr...]
  transfers between devices with their start and end apart: 94 -> 94, of which waited for: 37 -> 36; matrix products, arithmetic and copies ran while one was open for 11% -> 11% of each run, Pallas kernels for 27% -> 26%
where the time goes in v5:
time: 601 us; the launch traced here: 594 us
  Pallas kernels  193 us (32%)
  waiting for transfers between devices  174 us (29%)
  starting transfers between devices  94.7 us (16%)
  local copies, waits for them, and re-layouts  75.2 us (13%)
  other arithmetic  40.1 us (7%)
  between operations  15.8 us (3%)
    all_gather x5, waiting for transfers between devices, column_of(): return lax.all_gather(shard, 'tensor', axis=0)  60.1 us
    ppermute x22, waiting for transfers between devices, step_x(): return lax.ppermute(v, 'plane', [(i, i ^ 1) for i in range(planes)])  51.8 us
    unnamed x240, local copies, waits for them, and re-layouts  47.2 us
    pallas_call x2, Pallas kernels, ff_back(): pl.pallas_call(functools.partial(ff_back_body, len(wr), len(we), len(r_sp...  38.1 us
    pallas_call x4, Pallas kernels, norm_expand(): pl.pallas_call(functools.partial(expand_body, kind, merged, scale, len(w)...  36.5 us
    ppermute x23, waiting for transfers between devices, step_y(): return lax.ppermute(v, 'plane', [(i, i ^ 2) for i in range(planes)])  35 us
    pallas_call x1, Pallas kernels, attend_back(): pl.pallas_call(functools.partial(attend_back_body, len(w)), grid_spec=plt...  28.2 us
    ppermute x22, starting transfers between devices, step_x(): return lax.ppermute(v, 'plane', [(i, i ^ 1) for i in range(planes)])  27.5 us
  transfers between devices with their start and end apart: 94, of which 36 were waited for; matrix products, arithmetic and copies ran while one was open for 11% of the time, Pallas kernels for 26%

profile of v5, /device:TPU:0, one launch (start us, length us, event | category | flops | bytes accessed | tf_op | source)
XLA Modules:
  0.0 593.5 jit_solution(8345111343217612215)
XLA Ops:
  26.7 5.1 collective-permute-done.5
  33.6 6.1 %collective-permute-done.7 = bf16[256,512]{1,0:T(8,128)(2,1)S(1)} collective-permute-done((bf16[256,512]{1,0:T(8,128)(2,1)S(1)}, bf16[256,512]{1,0:T(8,128)(2,1)S(1)}, u32[]{:S(2)}, u32[]{:S(2)}) %collective-permute-start.7) | collective-permute-done | bytes 262176 | tf_op jit(solution)/shard_map/ppermute | solution.py:1115
  39.7 11.1 %all-gather.11.cloned.1.call-done = bf16[1024,512]{1,0:T(8,128)(2,1)} async-done(((bf16[256,512]{1,0:T(8,128)(2,1)}), bf16[1024,512]{1,0:T(8,128)(2,1)}) %all-gather.11.cloned.1.call-update) | async-done | bytes 1048592 | tf_op jit(solution)/shard_map/all_gather | solution.py:1137
  54.5 26.7 %all-gather.13.cloned.1.call-done = bf16[1024,512]{1,0:T(8,128)(2,1)} async-done(((bf16[256,512]{1,0:T(8,128)(2,1)}), bf16[1024,512]{1,0:T(8,128)(2,1)}) %all-gather.13.cloned.1.call-update) | async-done | bytes 1048592 | tf_op jit(solution)/shard_map/all_gather | solution.py:1137
  92.9 22.0 %all-gather.15.cloned.1.call-done = bf16[1024,512]{1,0:T(8,128)(2,1)} async-done(((bf16[256,512]{1,0:T(8,128)(2,1)}), bf16[1024,512]{1,0:T(8,128)(2,1)}) %all-gather.15.cloned.1.call-update) | async-done | bytes 1048592 | tf_op jit(solution)/shard_map/all_gather | solution.py:1137
  131.9 7.7 %norm_expand_ff.2 = (bf16[512,1024]{1,0:T(8,128)(2,1)S(1)}, f32[512,2048]{1,0:T(8,128)}, bf16[512,2048]{1,0:T(8,128)(2,1)}) custom-call(s32[1]{0:T(128)} %bitcast.p_ref.s_ref, f32[512,1024]{1,0:T(8,128)} %maximum_convert_fusion.refs_0_.x_ref, f32[1,1024]{1,0:T(1,128)S(1)} %get-tuple-element.501.refs_1_.g_ref, f32[1,1024]{1,0:T(1,128)S(1)} %get-tuple-element.491.refs_2_, ...), custom_call_target="tpu_custom_call" | custom-call | flops 1073741 | bytes 5242 | tf_op jit(solution)/shard_map/norm_expand_ff/pallas_call | solution.py:182
  139.7 14.8 %collective-permute-done.17.refs_3_ = bf16[2,256,512]{2,1,0:T(8,128)(2,1)S(1)} collective-permute-done((bf16[2,256,512]{2,1,0:T(8,128)(2,1)S(1)}, bf16[2,256,512]{2,1,0:T(8,128)(2,1)S(1)}, u32[]{:S(2)}, u32[]{:S(2)}) %collective-permute-start.17) | collective-permute-done | bytes 524320 | tf_op jit(solution)/shard_map/ppermute | solution.py:1115
  162.3 5.5 reduce_mm.2.refs_1_
  175.4 8.1 %norm_expand_qkv.1 = (f32[512,1024]{1,0:T(8,128)}, bf16[512,1024]{1,0:T(8,128)(2,1)S(1)}, bf16[512,1536]{1,0:T(8,128)(2,1)}) custom-call(s32[1]{0:T(128)} %bitcast.p_ref.s_ref, f32[512,1024]{1,0:T(8,128)} %maximum_convert_fusion.refs_0_.x_ref, bf16[512,1024]{1,0:T(8,128)(2,1)S(1)} %copy-done.23, bf16[512,1024]{1,0:T(8,128)(2,1)S(1)} %collective-permute-done.25.refs_2_, ...), custom_call_target="tpu_custom_call" | custom-call | flops 805306 | bytes 4718 | tf_op jit(solution)/shard_map/norm_expand_qkv/pallas_call | solution.py:182
  188.2 11.9 %attend.1 = (bf16[512,512]{1,0:T(8,128)(2,1)S(1)}, bf16[8,512,512]{2,1,0:T(8,128)(2,1)}) custom-call(s32[1]{0:T(128)} %bitcast.23.len_ref, bf16[512,1536]{1,0:T(8,128)(2,1)S(1)} %copy-done.13, bf16[128,64]{1,0:T(8,128)(2,1)S(1)} %pad.16.table_ref), custom_call_target="tpu_custom_call" | custom-call | flops 268435 | bytes 2621 | tf_op jit(solution)/shard_map/attend/pallas_call | solution.py:562
  209.4 4.9 reduce_mm.3.refs_1_
  222.6 7.2 %norm_expand_conv.1 = (f32[512,1024]{1,0:T(8,128)}, bf16[512,1024]{1,0:T(8,128)(2,1)S(1)}, f32[512,512]{1,0:T(8,128)S(1)}, f32[512,512]{1,0:T(8,128)}) custom-call(s32[1]{0:T(128)} %bitcast.p_ref.s_ref, f32[512,1024]{1,0:T(8,128)} %get-tuple-element.254.refs_0_.x_ref, bf16[512,1024]{1,0:T(8,128)(2,1)} %reduce_mm.3.refs_1_, ...), custom_call_target="tpu_custom_call" | custom-call | flops 536870 | bytes 4194 | tf_op jit(solution)/shard_map/norm_expand_conv/pallas_call | solution.py:182
  236.5 7.9 %collective-permute-done.32.refs_7_.refs_5_ = bf16[4,256,512]{2,1,0:T(8,128)(2,1)S(1)} collective-permute-done((bf16[4,256,512]{2,1,0:T(8,128)(2,1)}, bf16[4,256,512]{2,1,0:T(8,128)(2,1)S(1)}, u32[]{:S(2)}, u32[]{:S(2)}) %collective-permute-start.32) | collective-permute-done | bytes 1048608 | tf_op jit(solution)/shard_map/ppermute | solution.py:1112
  250.9 5.9 filter_out.1
  264.3 13.4 %norm_expand_ff.3 = (f32[512,1024]{1,0:T(8,128)}, bf16[512,1024]{1,0:T(8,128)(2,1)S(1)}, f32[512,2048]{1,0:T(8,128)}, bf16[512,1024]{1,0:T(8,128)(2,1)S(1)}) custom-call(s32[1]{0:T(128)} %bitcast.p_ref.s_ref, f32[512,1024]{1,0:T(8,128)} %get-tuple-element.268.refs_0_.x_ref, bf16[512,1024]{1,0:T(8,128)(2,1)} %get-tuple-element.277.refs_1_, ...), custom_call_target="tpu_custom_call" | custom-call | flops 1073741 | bytes 5242 | tf_op jit(solution)/shard_map/norm_expand_ff/pallas_call | solution.py:182
  288.3 18.2 %ff_back.2 = (bf16[512,1024]{1,0:T(8,128)(2,1)}, f32[1,2048]{1,0:T(1,128)}, bf16[4,4,256,512]{3,2,1,0:T(8,128)(2,1)}, bf16[4,256,512]{2,1,0:T(8,128)(2,1)}, bf16...) custom-call(s32[1]{0:T(128)} %bitcast.p_ref.s_ref, ...), custom_call_target="tpu_custom_call" | custom-call | flops 4294967 | bytes 8388 | tf_op jit(solution)/shard_map/ff_back/pallas_call | solution.py:383
  324.1 17.0 %mix_back.1 = (bf16[512,1024]{1,0:T(8,128)(2,1)}, f32[32,512]{1,0:T(8,128)}, bf16[4,4,256,384]{3,2,1,0:T(8,128)(2,1)}) custom-call(s32[1]{0:T(128)} %bitcast.p_ref.s_ref, f32[512,512]{1,0:T(8,128)} %copy-done.49, f32[512,512]{1,0:T(8,128)} %copy-done.9, f32[512,128]{1,0:T(8,128)} %copy-done.26, f32[512,128]{1,0:T(8,128)} %copy-done.27, ...), custom_call_target="tpu_custom_call" | custom-call | flops 16252 | bytes 2621 | tf_op jit(solution)/shard_map/mix_back/pallas_call | solution.py:959
  361.3 28.2 %attend_back.1 = (bf16[512,1024]{1,0:T(8,128)(2,1)}, f32[1,1536]{1,0:T(1,128)}, f32[72,128]{1,0:T(8,128)}, bf16[4,256,512]{2,1,0:T(8,128)(2,1)}, bf16[2,2,256,51...) custom-call(s32[1]{0:T(128)} %bitcast.p_ref.s_ref, ...), custom_call_target="tpu_custom_call" | custom-call | flops 671088 | bytes 2621 | tf_op jit(solution)/shard_map/attend_back/pallas_call | solution.py:696
  404.5 19.9 %ff_back.3 = (bf16[512,1024]{1,0:T(8,128)(2,1)}, f32[1,2048]{1,0:T(1,128)}, bf16[4,256,512]{2,1,0:T(8,128)(2,1)}, bf16[2,2,256,512]{3,2,1,0:T(8,128)(2,1)}, bf16...) custom-call(s32[1]{0:T(128)} %bitcast.p_ref.s_ref, ...), custom_call_target="tpu_custom_call" | custom-call | flops 4294967 | bytes 8388 | tf_op jit(solution)/shard_map/ff_back/pallas_call | solution.py:383
  433.3 18.0 %collective-permute-start.56 = (bf16[128,1024]{1,0:T(8,128)(2,1)S(1)}, bf16[128,1024]{1,0:T(8,128)(2,1)}, u32[]{:S(2)}, u32[]{:S(2)}) collective-permute-start(bf16[128,1024]{1,0:T(8,128)(2,1)S(1)} %get-tuple-element.446), channel_id=1, source_target_pairs={{2,0},{0,1},{6,2},{4,3},{3,4},{1,5},{7,6},{5,7},{10,8},{8,9},{14,1... | collective-permute-start | bytes 786440 | tf_op jit(solution)/shard_map/ppermute | solution.py:1250
  457.0 5.5 collective-permute-done.51.fy_ref
  484.3 11.9 %collective-permute-done.59.rx_ref = bf16[2,2,256,512]{3,2,1,0:T(8,128)(2,1)S(1)} collective-permute-done((bf16[2,2,256,512]{3,2,1,0:T(8,128)(2,1)}, bf16[2,2,256,512]{3,2,1,0:T(8,128)(2,1)S(1)}, u32[]{:S(2)}, u32[]{:S(2)}) %collective-permute-start.59) | collective-permute-done | bytes 1048608 | tf_op jit(solution)/shard_map/ppermute | solution.py:1112
  506.1 8.2 %collective-permute-done.63 = bf16[128,1024]{1,0:T(8,128)(2,1)} collective-permute-done((bf16[128,1024]{1,0:T(8,128)(2,1)}, bf16[128,1024]{1,0:T(8,128)(2,1)}, u32[]{:S(2)}, u32[]{:S(2)}) %collective-permute-start.63) | collective-permute-done | bytes 262176 | tf_op jit(solution)/shard_map/ppermute | solution.py:1250
  534.5 8.3 %collective-permute-done.65.fy_ref = bf16[2,256,512]{2,1,0:T(8,128)(2,1)S(1)} collective-permute-done((bf16[2,256,512]{2,1,0:T(8,128)(2,1)S(1)}, bf16[2,256,512]{2,1,0:T(8,128)(2,1)S(1)}, u32[]{:S(2)}, u32[]{:S(2)}) %collective-permute-start.65) | collective-permute-done | bytes 524320 | tf_op jit(solution)/shard_map/ppermute | solution.py:1112
  (568 shorter events, 284.1 us)
Async XLA Ops:
  7.2 43.6 %all-gather.11.cloned.1.call-start = ((), (), s32[]{:S(2)}) async-start(), calls=%async_computation.12 | async-start | bytes 1310720 | tf_op jit(solution)/shard_map/all_gather | solution.py:1137
  20.2 61.0 %all-gather.13.cloned.1.call-start = ((), (), s32[]{:S(2)}) async-start(), calls=%async_computation.13 | async-start | bytes 1310720 | tf_op jit(solution)/shard_map/all_gather | solution.py:1137
  20.9 94.0 %all-gather.15.cloned.1.call-start = ((), (), s32[]{:S(2)}) async-start(), calls=%async_computation.14 | async-start | bytes 1310720 | tf_op jit(solution)/shard_map/all_gather | solution.py:1137
  21.6 147.6 %all-gather.17.cloned.1.call-start = ((), (), s32[]{:S(2)}) async-start(), calls=%async_computation.15 | async-start | bytes 2293760 | tf_op jit(solution)/shard_map/all_gather | solution.py:1137
  22.2 241.2 %all-gather.19.cloned.1.call-start = ((), (), s32[]{:S(2)}) async-start(), calls=%async_computation.16 | async-start | bytes 5242880 | tf_op jit(solution)/shard_map/all_gather | solution.py:1137
  81.2 37.5 %collective-permute-start.13 = (bf16[4,256,512]{2,1,0:T(8,128)(2,1)}, bf16[4,256,512]{2,1,0:T(8,128)(2,1)}, u32[]{:S(2)}, u32[]{:S(2)}) collective-permute-start(bf16[4,256,512]{2,1,0:T(8,128)(2,1)} %bitcast.198), channel_id=1, source_target_pairs={{0,8},{8,0},{16,24},{24,16},{1,9},{9,1},{17,25},{25,17},{2,10},{10... | collective-permute-start | bytes 3145736 | tf_op jit(solution)/shard_map/ppermute | solution.py:1112
  82.0 36.7 %collective-permute-start.14 = (bf16[4,256,512]{2,1,0:T(8,128)(2,1)}, bf16[4,256,512]{2,1,0:T(8,128)(2,1)}, u32[]{:S(2)}, u32[]{:S(2)}) collective-permute-start(bf16[4,256,512]{2,1,0:T(8,128)(2,1)} %bitcast.199), channel_id=1, source_target_pairs={{0,16},{8,24},{16,0},{24,8},{1,17},{9,25},{17,1},{25,9},{2,18},{10... | collective-permute-start | bytes 3145736 | tf_op jit(solution)/shard_map/ppermute | solution.py:1115
  84.3 33.6 %collective-permute-start.11 = (bf16[2,256,512]{2,1,0:T(8,128)(2,1)}, bf16[2,256,512]{2,1,0:T(8,128)(2,1)S(1)}, u32[]{:S(2)}, u32[]{:S(2)}) collective-permute-start(bf16[2,256,512]{2,1,0:T(8,128)(2,1)} %slice.240), channel_id=1, source_target_pairs={{0,16},{8,24},{16,0},{24,8},{1,17},{9,25},{17,1},{25,9},{2,18},{10... | collective-permute-start | bytes 1572872 | tf_op jit(solution)/shard_map/ppermute | solution.py:1115
  85.7 33.0 %collective-permute-start.12 = (bf16[2,256,512]{2,1,0:T(8,128)(2,1)}, bf16[2,256,512]{2,1,0:T(8,128)(2,1)}, u32[]{:S(2)}, u32[]{:S(2)}) collective-permute-start(bf16[2,256,512]{2,1,0:T(8,128)(2,1)} %slice.241), channel_id=1, source_target_pairs={{0,8},{8,0},{16,24},{24,16},{1,9},{9,1},{17,25},{25,17},{2,10},{10... | collective-permute-start | bytes 1572872 | tf_op jit(solution)/shard_map/ppermute | solution.py:1112
  92.8 296.7 %reduce-scatter.7.cloned.1.call-start = ((), (), s32[]{:S(2)}) async-start(), calls=%async_computation.6 | async-start | bytes 5242880 | tf_op jit(solution)/shard_map/reduce_scatter | solution.py:1161
  118.7 35.8 %collective-permute-start.19 = (bf16[4,256,512]{2,1,0:T(8,128)(2,1)}, bf16[4,256,512]{2,1,0:T(8,128)(2,1)S(1)}, u32[]{:S(2)}, u32[]{:S(2)}) collective-permute-start(bf16[4,256,512]{2,1,0:T(8,128)(2,1)} %bitcast.188), channel_id=1, source_target_pairs={{0,8},{8,0},{16,24},{24,16},{1,9},{9,1},{17,25},{25,17},{2,10},{10... | collective-permute-start | bytes 3145736 | tf_op jit(solution)/shard_map/ppermute | solution.py:1112
  119.9 34.7 %collective-permute-start.20 = (bf16[4,256,512]{2,1,0:T(8,128)(2,1)}, bf16[4,256,512]{2,1,0:T(8,128)(2,1)S(1)}, u32[]{:S(2)}, u32[]{:S(2)}) collective-permute-start(bf16[4,256,512]{2,1,0:T(8,128)(2,1)} %bitcast.189), channel_id=1, source_target_pairs={{0,16},{8,24},{16,0},{24,8},{1,17},{9,25},{17,1},{25,9},{2,18},{10... | collective-permute-start | bytes 3145736 | tf_op jit(solution)/shard_map/ppermute | solution.py:1115
  306.5 150.5 %reduce-scatter.9.cloned.1.call-start = ((), (), s32[]{:S(2)}) async-start(), calls=%async_computation.7 | async-start | bytes 3932160 | tf_op jit(solution)/shard_map/reduce_scatter | solution.py:1161
  307.8 33.3 %collective-permute-start.40 = (bf16[2,2,256,512]{3,2,1,0:T(8,128)(2,1)}, bf16[2,2,256,512]{3,2,1,0:T(8,128)(2,1)}, u32[]{:S(2)}, u32[]{:S(2)}) collective-permute-start(bf16[2,2,256,512]{3,2,1,0:T(8,128)(2,1)} %get-tuple-element.298), channel_id=1, source_target_pairs={{0,8},{8,0},{16,24},{24,16},{1,9},{9,1},{17,25},{25,17},{2,10},{10... | collective-permute-start | bytes 3145736 | tf_op jit(solution)/shard_map/ppermute | solution.py:1112
  341.2 164.9 %reduce-scatter.11.cloned.1.call-start = ((), (), s32[]{:S(2)}) async-start(), calls=%async_computation.8 | async-start | bytes 1310720 | tf_op jit(solution)/shard_map/reduce_scatter | solution.py:1161
  389.6 34.8 %collective-permute-start.48 = (bf16[2,2,256,512]{3,2,1,0:T(8,128)(2,1)}, bf16[2,2,256,512]{3,2,1,0:T(8,128)(2,1)S(1)}, u32[]{:S(2)}, u32[]{:S(2)}) collective-permute-start(bf16[2,2,256,512]{3,2,1,0:T(8,128)(2,1)} %get-tuple-element.343), channel_id=1, source_target_pairs={{0,8},{8,0},{16,24},{24,16},{1,9},{9,1},{17,25},{25,17},{2,10},{10... | collective-permute-start | bytes 3145736 | tf_op jit(solution)/shard_map/ppermute | solution.py:1112
  390.1 34.4 %collective-permute-start.49 = (bf16[2,2,256,512]{3,2,1,0:T(8,128)(2,1)}, bf16[2,2,256,512]{3,2,1,0:T(8,128)(2,1)S(1)}, u32[]{:S(2)}, u32[]{:S(2)}) collective-permute-start(bf16[2,2,256,512]{3,2,1,0:T(8,128)(2,1)} %get-tuple-element.344), channel_id=1, source_target_pairs={{0,16},{8,24},{16,0},{24,8},{1,17},{9,25},{17,1},{25,9},{2,18},{10... | collective-permute-start | bytes 3145736 | tf_op jit(solution)/shard_map/ppermute | solution.py:1115
  397.0 163.8 %reduce-scatter.17.cloned.1.call-start = ((), (), s32[]{:S(2)}) async-start(), calls=%async_computation.11 | async-start | bytes 1310720 | tf_op jit(solution)/shard_map/reduce_scatter | solution.py:1161
  426.1 37.7 %collective-permute-start.52 = (bf16[2,2,256,512]{3,2,1,0:T(8,128)(2,1)}, bf16[2,2,256,512]{3,2,1,0:T(8,128)(2,1)S(1)}, u32[]{:S(2)}, u32[]{:S(2)}) collective-permute-start(bf16[2,2,256,512]{3,2,1,0:T(8,128)(2,1)} %get-tuple-element.348), channel_id=1, source_target_pairs={{0,8},{8,0},{16,24},{24,16},{1,9},{9,1},{17,25},{25,17},{2,10},{10... | collective-permute-start | bytes 3145736 | tf_op jit(solution)/shard_map/ppermute | solution.py:1112
  427.3 36.5 %collective-permute-start.53 = (bf16[2,2,256,512]{3,2,1,0:T(8,128)(2,1)}, bf16[2,2,256,512]{3,2,1,0:T(8,128)(2,1)S(1)}, u32[]{:S(2)}, u32[]{:S(2)}) collective-permute-start(bf16[2,2,256,512]{3,2,1,0:T(8,128)(2,1)} %get-tuple-element.349), channel_id=1, source_target_pairs={{0,16},{8,24},{16,0},{24,8},{1,17},{9,25},{17,1},{25,9},{2,18},{10... | collective-permute-start | bytes 3145736 | tf_op jit(solution)/shard_map/ppermute | solution.py:1115
  470.0 109.5 %reduce-scatter.15.cloned.1.call-start = ((), (), s32[]{:S(2)}) async-start(), calls=%async_computation.10 | async-start | bytes 1310720 | tf_op jit(solution)/shard_map/reduce_scatter | solution.py:1161
  474.2 40.2 %collective-permute-start.58 = (bf16[2,256,512]{2,1,0:T(8,128)(2,1)}, bf16[2,256,512]{2,1,0:T(8,128)(2,1)}, u32[]{:S(2)}, u32[]{:S(2)}) collective-permute-start(bf16[2,256,512]{2,1,0:T(8,128)(2,1)} %fusion.2), channel_id=1, source_target_pairs={{0,8},{8,0},{16,24},{24,16},{1,9},{9,1},{17,25},{25,17},{2,10},{10... | collective-permute-start | bytes 1572872 | tf_op jit(solution)/shard_map/ppermute | solution.py:1112
  478.1 36.2 %collective-permute-start.57 = (bf16[2,256,512]{2,1,0:T(8,128)(2,1)}, bf16[2,256,512]{2,1,0:T(8,128)(2,1)}, u32[]{:S(2)}, u32[]{:S(2)}) collective-permute-start(bf16[2,256,512]{2,1,0:T(8,128)(2,1)} %fusion.3), channel_id=1, source_target_pairs={{0,16},{8,24},{16,0},{24,8},{1,17},{9,25},{17,1},{25,9},{2,18},{10... | collective-permute-start | bytes 1572872 | tf_op jit(solution)/shard_map/ppermute | solution.py:1115
  519.3 62.2 %reduce-scatter.13.cloned.1.call-start = ((), (), s32[]{:S(2)}) async-start(), calls=%async_computation.9 | async-start | bytes 1310720 | tf_op jit(solution)/shard_map/reduce_scatter | solution.py:1161
  (187 other events, 2278.1 us)
Sparse Core Ops, SparseCore 0:
  20.3 30.4 all-gather.10
  52.9 28.1 all-gather.12
  83.3 31.5 all-gather.14
  116.9 52.3 all-gather.16
  170.6 78.8 all-gather.18
  306.6 75.8 reduce-scatter.6
  384.9 63.5 reduce-scatter.8
  450.9 31.6 reduce-scatter.10
  484.9 31.3 reduce-scatter.16
  519.4 25.2 reduce-scatter.14
  553.7 25.0 reduce-scatter.12

commit v6 on v5

--- a/solution.py
+++ b/solution.py
@@ -1249,6 +1249,14 @@
             back = [(b, a) for a, b in route(turn)]
             came.append(lax.ppermute(blocks[turn], ("pair", "tensor"), back))
         return came
+
+    def send_one(v, turn):
+        half = v.shape[0] // 2
+        mine = lax.dynamic_slice_in_dim(v, core * half, half, 0)
+        first, second = mine[: half // 2], mine[half // 2 :]
+        other = (part // 2 == 1) == (turn == 0)
+        block = jnp.where(other, second, first)
+        return lax.ppermute(block, ("pair", "tensor"), [(b, a) for a, b in route(turn)])
 
     def home(came):
         odd = lax.rem(part, 2) == 1
@@ -1398,13 +1406,15 @@
     g_att, b2, z_r2 = fence(g_att, b2, z_r2)
     atth1 = hop1(g_att)
     gx1, gf1, sums1 = norm_back(0.5, x1, gx2, b2, other_core(b2), gain_row(1))
+    home0 = send_one(out_rows, 0)
     b1, gc1, g_r1, g_e1 = ff_back(gf1, a1, u1, r1, e1, p, False)
-    g_r1, g_e1, b1, atth1 = fence(g_r1, g_e1, b1, atth1)
-    outputs = send_home(out_rows)
+    g_r1, g_e1, b1, atth1, home0, out_rows = fence(g_r1, g_e1, b1, atth1, home0, out_rows)
+    home1 = send_one(out_rows, 1)
     r1h1 = hop1(g_r1)
     atth2 = hop2(g_att, atth1)
     gx0, _, sums0 = norm_back(1.0, x0, gx1, b1, other_core(b1), gain_row(0))
-    atth2, r1h1, gx0, z_fil, outputs = fence(atth2, r1h1, gx0, z_fil, outputs)
+    atth2, r1h1, gx0, z_fil, home1 = fence(atth2, r1h1, gx0, z_fil, home1)
+    outputs = [home0, home1]
     e1h1 = hop1(g_e1)
     r1h2 = hop2(g_r1, r1h1)
     z_att = hop3(g_att, atth1, atth2)

time: 601 us -> 599 us (level)
  starting transfers between devices: 94.7 us -> 77.1 us
  waiting for transfers between devices: 174 us -> 189 us
    ppermute x4 -> x2, starting transfers between devices: 25.1 us -> 3.86 us  [send_home(): came.append(lax.ppermute(blocks[turn], ('pair', 'tensor'), back))]
    reduce_scatter x6, waiting for transfers between devices: 0.05 us -> 10.1 us  [tensor_sum(): return lax.psum_scatter(total, 'tensor', scatter_dimension=0)]
    unnamed x240 -> x236, local copies, waits for them, and re-layouts: 47.2 us -> 45.3 us
  transfers between devices with their start and end apart: 94 -> 94, of which waited for: 36 -> 39; matrix products, arithmetic and copies ran while one was open for 11% -> 12% of each run, Pallas kernels for 26% -> 26%
where the time goes in v6:
time: 599 us; the launch traced here: 592 us
  Pallas kernels  193 us (32%)
  waiting for transfers between devices  189 us (32%)
  starting transfers between devices  77.1 us (13%)
  local copies, waits for them, and re-layouts  73.3 us (12%)
  other arithmetic  42.6 us (7%)
  between operations  15.8 us (3%)
    all_gather x5, waiting for transfers between devices, column_of(): return lax.all_gather(shard, 'tensor', axis=0)  60.1 us
    ppermute x22, waiting for transfers between devices, step_x(): return lax.ppermute(v, 'plane', [(i, i ^ 1) for i in range(planes)])  55.3 us
    unnamed x236, local copies, waits for them, and re-layouts  45.3 us
    pallas_call x2, Pallas kernels, ff_back(): pl.pallas_call(functools.partial(ff_back_body, len(wr), len(we), len(r_sp...  38 us
    pallas_call x4, Pallas kernels, norm_expand(): pl.pallas_call(functools.partial(expand_body, kind, merged, scale, len(w)...  36.3 us
    ppermute x23, waiting for transfers between devices, step_y(): return lax.ppermute(v, 'plane', [(i, i ^ 2) for i in range(planes)])  34.8 us
    pallas_call x1, Pallas kernels, attend_back(): pl.pallas_call(functools.partial(attend_back_body, len(w)), grid_spec=plt...  28.2 us
    ppermute x23, starting transfers between devices, step_y(): return lax.ppermute(v, 'plane', [(i, i ^ 2) for i in range(planes)])  25.9 us
  transfers between devices with their start and end apart: 94, of which 39 were waited for; matrix products, arithmetic and copies ran while one was open for 12% of the time, Pallas kernels for 26%

profile of v6, /device:TPU:0, one launch (start us, length us, event | category | flops | bytes accessed | tf_op | source)
XLA Modules:
  0.0 591.5 jit_solution(7187895055890062931)
XLA Ops:
  26.7 5.1 collective-permute-done.5
  33.6 6.1 %collective-permute-done.7 = bf16[256,512]{1,0:T(8,128)(2,1)S(1)} collective-permute-done((bf16[256,512]{1,0:T(8,128)(2,1)S(1)}, bf16[256,512]{1,0:T(8,128)(2,1)S(1)}, u32[]{:S(2)}, u32[]{:S(2)}) %collective-permute-start.7) | collective-permute-done | bytes 262176 | tf_op jit(solution)/shard_map/ppermute | solution.py:1115
  39.7 11.1 %all-gather.11.cloned.1.call-done = bf16[1024,512]{1,0:T(8,128)(2,1)} async-done(((bf16[256,512]{1,0:T(8,128)(2,1)}), bf16[1024,512]{1,0:T(8,128)(2,1)}) %all-gather.11.cloned.1.call-update) | async-done | bytes 1048592 | tf_op jit(solution)/shard_map/all_gather | solution.py:1137
  54.5 26.7 %all-gather.13.cloned.1.call-done = bf16[1024,512]{1,0:T(8,128)(2,1)} async-done(((bf16[256,512]{1,0:T(8,128)(2,1)}), bf16[1024,512]{1,0:T(8,128)(2,1)}) %all-gather.13.cloned.1.call-update) | async-done | bytes 1048592 | tf_op jit(solution)/shard_map/all_gather | solution.py:1137
  92.9 22.0 %all-gather.15.cloned.1.call-done = bf16[1024,512]{1,0:T(8,128)(2,1)} async-done(((bf16[256,512]{1,0:T(8,128)(2,1)}), bf16[1024,512]{1,0:T(8,128)(2,1)}) %all-gather.15.cloned.1.call-update) | async-done | bytes 1048592 | tf_op jit(solution)/shard_map/all_gather | solution.py:1137
  131.9 7.7 %norm_expand_ff.2 = (bf16[512,1024]{1,0:T(8,128)(2,1)S(1)}, f32[512,2048]{1,0:T(8,128)}, bf16[512,2048]{1,0:T(8,128)(2,1)}) custom-call(s32[1]{0:T(128)} %bitcast.p_ref.s_ref, f32[512,1024]{1,0:T(8,128)} %maximum_convert_fusion.refs_0_.x_ref, f32[1,1024]{1,0:T(1,128)S(1)} %get-tuple-element.501.refs_1_.g_ref, f32[1,1024]{1,0:T(1,128)S(1)} %get-tuple-element.491.refs_2_, ...), custom_call_target="tpu_custom_call" | custom-call | flops 1073741 | bytes 5242 | tf_op jit(solution)/shard_map/norm_expand_ff/pallas_call | solution.py:182
  139.7 14.9 %collective-permute-done.17.refs_3_ = bf16[2,256,512]{2,1,0:T(8,128)(2,1)S(1)} collective-permute-done((bf16[2,256,512]{2,1,0:T(8,128)(2,1)S(1)}, bf16[2,256,512]{2,1,0:T(8,128)(2,1)S(1)}, u32[]{:S(2)}, u32[]{:S(2)}) %collective-permute-start.17) | collective-permute-done | bytes 524320 | tf_op jit(solution)/shard_map/ppermute | solution.py:1115
  162.3 5.5 reduce_mm.2.refs_1_
  175.4 8.1 %norm_expand_qkv.1 = (f32[512,1024]{1,0:T(8,128)}, bf16[512,1024]{1,0:T(8,128)(2,1)S(1)}, bf16[512,1536]{1,0:T(8,128)(2,1)}) custom-call(s32[1]{0:T(128)} %bitcast.p_ref.s_ref, f32[512,1024]{1,0:T(8,128)} %maximum_convert_fusion.refs_0_.x_ref, bf16[512,1024]{1,0:T(8,128)(2,1)S(1)} %copy-done.23, bf16[512,1024]{1,0:T(8,128)(2,1)S(1)} %collective-permute-done.25.refs_2_, ...), custom_call_target="tpu_custom_call" | custom-call | flops 805306 | bytes 4718 | tf_op jit(solution)/shard_map/norm_expand_qkv/pallas_call | solution.py:182
  188.2 11.9 %attend.1 = (bf16[512,512]{1,0:T(8,128)(2,1)S(1)}, bf16[8,512,512]{2,1,0:T(8,128)(2,1)}) custom-call(s32[1]{0:T(128)} %bitcast.23.len_ref, bf16[512,1536]{1,0:T(8,128)(2,1)S(1)} %copy-done.13, bf16[128,64]{1,0:T(8,128)(2,1)S(1)} %pad.16.table_ref), custom_call_target="tpu_custom_call" | custom-call | flops 268435 | bytes 2621 | tf_op jit(solution)/shard_map/attend/pallas_call | solution.py:562
  209.3 4.9 reduce_mm.3.refs_1_
  222.6 7.2 %norm_expand_conv.1 = (f32[512,1024]{1,0:T(8,128)}, bf16[512,1024]{1,0:T(8,128)(2,1)S(1)}, f32[512,512]{1,0:T(8,128)S(1)}, f32[512,512]{1,0:T(8,128)}) custom-call(s32[1]{0:T(128)} %bitcast.p_ref.s_ref, f32[512,1024]{1,0:T(8,128)} %get-tuple-element.255.refs_0_.x_ref, bf16[512,1024]{1,0:T(8,128)(2,1)} %reduce_mm.3.refs_1_, ...), custom_call_target="tpu_custom_call" | custom-call | flops 536870 | bytes 4194 | tf_op jit(solution)/shard_map/norm_expand_conv/pallas_call | solution.py:182
  236.4 7.9 %collective-permute-done.32.refs_7_.refs_5_ = bf16[4,256,512]{2,1,0:T(8,128)(2,1)S(1)} collective-permute-done((bf16[4,256,512]{2,1,0:T(8,128)(2,1)}, bf16[4,256,512]{2,1,0:T(8,128)(2,1)S(1)}, u32[]{:S(2)}, u32[]{:S(2)}) %collective-permute-start.32) | collective-permute-done | bytes 1048608 | tf_op jit(solution)/shard_map/ppermute | solution.py:1112
  250.9 5.9 %filter_out.1 = (bf16[512,1024]{1,0:T(8,128)(2,1)}, bf16[512,512]{1,0:T(8,128)(2,1)S(1)}) custom-call(s32[1]{0:T(128)} %bitcast.p_ref.s_ref, f32[512,512]{1,0:T(8,128)} %copy-done.9, f32[512,128]{1,0:T(8,128)S(1)} %get-tuple-element.276.sa_ref.refs_2_, f32[512,128]{1,0:T(8,128)S(1)} %collective-permute-done.36.sb_ref.refs_3_, ...), custom_call_target="tpu_custom_call" | custom-call | flops 268435 | bytes 2097 | tf_op jit(solution)/shard_map/filter_out/pallas_call | solution.py:819
  264.3 13.4 %norm_expand_ff.3 = (f32[512,1024]{1,0:T(8,128)}, bf16[512,1024]{1,0:T(8,128)(2,1)S(1)}, f32[512,2048]{1,0:T(8,128)}, bf16[512,1024]{1,0:T(8,128)(2,1)S(1)}) custom-call(s32[1]{0:T(128)} %bitcast.p_ref.s_ref, f32[512,1024]{1,0:T(8,128)} %get-tuple-element.269.refs_0_.x_ref, bf16[512,1024]{1,0:T(8,128)(2,1)} %get-tuple-element.278.refs_1_, ...), custom_call_target="tpu_custom_call" | custom-call | flops 1073741 | bytes 5242 | tf_op jit(solution)/shard_map/norm_expand_ff/pallas_call | solution.py:182
  288.2 18.2 %ff_back.2 = (bf16[512,1024]{1,0:T(8,128)(2,1)}, f32[1,2048]{1,0:T(1,128)}, bf16[4,4,256,512]{3,2,1,0:T(8,128)(2,1)}, bf16[4,256,512]{2,1,0:T(8,128)(2,1)}, bf16...) custom-call(s32[1]{0:T(128)} %bitcast.p_ref.s_ref, ...), custom_call_target="tpu_custom_call" | custom-call | flops 4294967 | bytes 8388 | tf_op jit(solution)/shard_map/ff_back/pallas_call | solution.py:383
  324.0 17.0 %mix_back.1 = (bf16[512,1024]{1,0:T(8,128)(2,1)}, f32[32,512]{1,0:T(8,128)}, bf16[4,4,256,384]{3,2,1,0:T(8,128)(2,1)}) custom-call(s32[1]{0:T(128)} %bitcast.p_ref.s_ref, f32[512,512]{1,0:T(8,128)} %copy-done.47, f32[512,512]{1,0:T(8,128)} %copy-done.9, f32[512,128]{1,0:T(8,128)} %copy-done.24, f32[512,128]{1,0:T(8,128)} %copy-done.25, ...), custom_call_target="tpu_custom_call" | custom-call | flops 16252 | bytes 2621 | tf_op jit(solution)/shard_map/mix_back/pallas_call | solution.py:959
  361.2 28.2 %attend_back.1 = (bf16[512,1024]{1,0:T(8,128)(2,1)}, f32[1,1536]{1,0:T(1,128)}, f32[72,128]{1,0:T(8,128)}, bf16[4,256,512]{2,1,0:T(8,128)(2,1)}, bf16[2,2,256,51...) custom-call(s32[1]{0:T(128)} %bitcast.p_ref.s_ref, ...), custom_call_target="tpu_custom_call" | custom-call | flops 671088 | bytes 2621 | tf_op jit(solution)/shard_map/attend_back/pallas_call | solution.py:696
  405.6 19.9 %ff_back.3 = (bf16[512,1024]{1,0:T(8,128)(2,1)}, f32[1,2048]{1,0:T(1,128)}, bf16[4,256,512]{2,1,0:T(8,128)(2,1)}, bf16[2,2,256,512]{3,2,1,0:T(8,128)(2,1)}, bf16...) custom-call(s32[1]{0:T(128)} %bitcast.p_ref.s_ref, ...), custom_call_target="tpu_custom_call" | custom-call | flops 4294967 | bytes 8388 | tf_op jit(solution)/shard_map/ff_back/pallas_call | solution.py:383
  443.9 10.0 %reduce-scatter.9.cloned.1.call-done = bf16[1,4,256,384]{3,2,1,0:T(8,128)(2,1)} async-done(((bf16[4,4,256,384]{3,2,1,0:T(8,128)(2,1)}), bf16[1,4,256,384]{3,2,1,0:T(8,128)(2,1)}) %reduce-scatter.9.cloned.1.call-update) | async-done | bytes 786448 | tf_op jit(solution)/shard_map/reduce_scatter | solution.py:1161
  456.1 8.0 %collective-permute-done.52.fy_ref = bf16[2,256,512]{2,1,0:T(8,128)(2,1)} collective-permute-done((bf16[2,256,512]{2,1,0:T(8,128)(2,1)}, bf16[2,256,512]{2,1,0:T(8,128)(2,1)}, u32[]{:S(2)}, u32[]{:S(2)}) %collective-permute-start.52) | collective-permute-done | bytes 524320 | tf_op jit(solution)/shard_map/ppermute | solution.py:1112
  484.7 12.3 %collective-permute-done.59.rx_ref = bf16[2,2,256,512]{3,2,1,0:T(8,128)(2,1)S(1)} collective-permute-done((bf16[2,2,256,512]{3,2,1,0:T(8,128)(2,1)}, bf16[2,2,256,512]{3,2,1,0:T(8,128)(2,1)S(1)}, u32[]{:S(2)}, u32[]{:S(2)}) %collective-permute-start.59) | collective-permute-done | bytes 1048608 | tf_op jit(solution)/shard_map/ppermute | solution.py:1112
  505.0 10.0 %collective-permute-done.63 = bf16[128,1024]{1,0:T(8,128)(2,1)} collective-permute-done((bf16[128,1024]{1,0:T(8,128)(2,1)}, bf16[128,1024]{1,0:T(8,128)(2,1)}, u32[]{:S(2)}, u32[]{:S(2)}) %collective-permute-start.63) | collective-permute-done | bytes 262176 | tf_op jit(solution)/shard_map/ppermute | solution.py:1250
  534.1 9.2 %collective-permute-done.65.fy_ref = bf16[2,256,512]{2,1,0:T(8,128)(2,1)S(1)} collective-permute-done((bf16[2,256,512]{2,1,0:T(8,128)(2,1)S(1)}, bf16[2,256,512]{2,1,0:T(8,128)(2,1)S(1)}, u32[]{:S(2)}, u32[]{:S(2)}) %collective-permute-start.65) | collective-permute-done | bytes 524320 | tf_op jit(solution)/shard_map/ppermute | solution.py:1112
  (565 shorter events, 284.6 us)
Async XLA Ops:
  7.2 43.6 %all-gather.11.cloned.1.call-start = ((), (), s32[]{:S(2)}) async-start(), calls=%async_computation.12 | async-start | bytes 1310720 | tf_op jit(solution)/shard_map/all_gather | solution.py:1137
  20.2 61.0 %all-gather.13.cloned.1.call-start = ((), (), s32[]{:S(2)}) async-start(), calls=%async_computation.13 | async-start | bytes 1310720 | tf_op jit(solution)/shard_map/all_gather | solution.py:1137
  20.9 94.0 %all-gather.15.cloned.1.call-start = ((), (), s32[]{:S(2)}) async-start(), calls=%async_computation.14 | async-start | bytes 1310720 | tf_op jit(solution)/shard_map/all_gather | solution.py:1137
  21.6 147.6 %all-gather.17.cloned.1.call-start = ((), (), s32[]{:S(2)}) async-start(), calls=%async_computation.15 | async-start | bytes 2293760 | tf_op jit(solution)/shard_map/all_gather | solution.py:1137
  22.2 241.2 %all-gather.19.cloned.1.call-start = ((), (), s32[]{:S(2)}) async-start(), calls=%async_computation.16 | async-start | bytes 5242880 | tf_op jit(solution)/shard_map/all_gather | solution.py:1137
  81.2 37.5 %collective-permute-start.13 = (bf16[4,256,512]{2,1,0:T(8,128)(2,1)}, bf16[4,256,512]{2,1,0:T(8,128)(2,1)}, u32[]{:S(2)}, u32[]{:S(2)}) collective-permute-start(bf16[4,256,512]{2,1,0:T(8,128)(2,1)} %bitcast.198), channel_id=1, source_target_pairs={{0,8},{8,0},{16,24},{24,16},{1,9},{9,1},{17,25},{25,17},{2,10},{10... | collective-permute-start | bytes 3145736 | tf_op jit(solution)/shard_map/ppermute | solution.py:1112
  82.0 36.7 %collective-permute-start.14 = (bf16[4,256,512]{2,1,0:T(8,128)(2,1)}, bf16[4,256,512]{2,1,0:T(8,128)(2,1)}, u32[]{:S(2)}, u32[]{:S(2)}) collective-permute-start(bf16[4,256,512]{2,1,0:T(8,128)(2,1)} %bitcast.199), channel_id=1, source_target_pairs={{0,16},{8,24},{16,0},{24,8},{1,17},{9,25},{17,1},{25,9},{2,18},{10... | collective-permute-start | bytes 3145736 | tf_op jit(solution)/shard_map/ppermute | solution.py:1115
  84.3 33.6 %collective-permute-start.11 = (bf16[2,256,512]{2,1,0:T(8,128)(2,1)}, bf16[2,256,512]{2,1,0:T(8,128)(2,1)S(1)}, u32[]{:S(2)}, u32[]{:S(2)}) collective-permute-start(bf16[2,256,512]{2,1,0:T(8,128)(2,1)} %slice.246), channel_id=1, source_target_pairs={{0,16},{8,24},{16,0},{24,8},{1,17},{9,25},{17,1},{25,9},{2,18},{10... | collective-permute-start | bytes 1572872 | tf_op jit(solution)/shard_map/ppermute | solution.py:1115
  85.7 33.0 %collective-permute-start.12 = (bf16[2,256,512]{2,1,0:T(8,128)(2,1)}, bf16[2,256,512]{2,1,0:T(8,128)(2,1)}, u32[]{:S(2)}, u32[]{:S(2)}) collective-permute-start(bf16[2,256,512]{2,1,0:T(8,128)(2,1)} %slice.247), channel_id=1, source_target_pairs={{0,8},{8,0},{16,24},{24,16},{1,9},{9,1},{17,25},{25,17},{2,10},{10... | collective-permute-start | bytes 1572872 | tf_op jit(solution)/shard_map/ppermute | solution.py:1112
  92.8 296.6 %reduce-scatter.7.cloned.1.call-start = ((), (), s32[]{:S(2)}) async-start(), calls=%async_computation.6 | async-start | bytes 5242880 | tf_op jit(solution)/shard_map/reduce_scatter | solution.py:1161
  118.7 35.8 %collective-permute-start.19 = (bf16[4,256,512]{2,1,0:T(8,128)(2,1)}, bf16[4,256,512]{2,1,0:T(8,128)(2,1)S(1)}, u32[]{:S(2)}, u32[]{:S(2)}) collective-permute-start(bf16[4,256,512]{2,1,0:T(8,128)(2,1)} %bitcast.188), channel_id=1, source_target_pairs={{0,8},{8,0},{16,24},{24,16},{1,9},{9,1},{17,25},{25,17},{2,10},{10... | collective-permute-start | bytes 3145736 | tf_op jit(solution)/shard_map/ppermute | solution.py:1112
  119.9 34.7 %collective-permute-start.20 = (bf16[4,256,512]{2,1,0:T(8,128)(2,1)}, bf16[4,256,512]{2,1,0:T(8,128)(2,1)S(1)}, u32[]{:S(2)}, u32[]{:S(2)}) collective-permute-start(bf16[4,256,512]{2,1,0:T(8,128)(2,1)} %bitcast.189), channel_id=1, source_target_pairs={{0,16},{8,24},{16,0},{24,8},{1,17},{9,25},{17,1},{25,9},{2,18},{10... | collective-permute-start | bytes 3145736 | tf_op jit(solution)/shard_map/ppermute | solution.py:1115
  306.4 147.5 %reduce-scatter.9.cloned.1.call-start = ((), (), s32[]{:S(2)}) async-start(), calls=%async_computation.7 | async-start | bytes 3932160 | tf_op jit(solution)/shard_map/reduce_scatter | solution.py:1161
  307.7 33.3 %collective-permute-start.40 = (bf16[2,2,256,512]{3,2,1,0:T(8,128)(2,1)}, bf16[2,2,256,512]{3,2,1,0:T(8,128)(2,1)}, u32[]{:S(2)}, u32[]{:S(2)}) collective-permute-start(bf16[2,2,256,512]{3,2,1,0:T(8,128)(2,1)} %get-tuple-element.299), channel_id=1, source_target_pairs={{0,8},{8,0},{16,24},{24,16},{1,9},{9,1},{17,25},{25,17},{2,10},{10... | collective-permute-start | bytes 3145736 | tf_op jit(solution)/shard_map/ppermute | solution.py:1112
  341.1 163.9 %reduce-scatter.11.cloned.1.call-start = ((), (), s32[]{:S(2)}) async-start(), calls=%async_computation.8 | async-start | bytes 1310720 | tf_op jit(solution)/shard_map/reduce_scatter | solution.py:1161
  389.5 36.0 %collective-permute-start.48 = (bf16[2,2,256,512]{3,2,1,0:T(8,128)(2,1)}, bf16[2,2,256,512]{3,2,1,0:T(8,128)(2,1)S(1)}, u32[]{:S(2)}, u32[]{:S(2)}) collective-permute-start(bf16[2,2,256,512]{3,2,1,0:T(8,128)(2,1)} %get-tuple-element.344), channel_id=1, source_target_pairs={{0,8},{8,0},{16,24},{24,16},{1,9},{9,1},{17,25},{25,17},{2,10},{10... | collective-permute-start | bytes 3145736 | tf_op jit(solution)/shard_map/ppermute | solution.py:1112
  389.9 35.5 %collective-permute-start.49 = (bf16[2,2,256,512]{3,2,1,0:T(8,128)(2,1)}, bf16[2,2,256,512]{3,2,1,0:T(8,128)(2,1)}, u32[]{:S(2)}, u32[]{:S(2)}) collective-permute-start(bf16[2,2,256,512]{3,2,1,0:T(8,128)(2,1)} %get-tuple-element.345), channel_id=1, source_target_pairs={{0,16},{8,24},{16,0},{24,8},{1,17},{9,25},{17,1},{25,9},{2,18},{10... | collective-permute-start | bytes 3145736 | tf_op jit(solution)/shard_map/ppermute | solution.py:1115
  396.9 161.8 %reduce-scatter.17.cloned.1.call-start = ((), (), s32[]{:S(2)}) async-start(), calls=%async_computation.11 | async-start | bytes 1310720 | tf_op jit(solution)/shard_map/reduce_scatter | solution.py:1161
  426.8 38.3 %collective-permute-start.53 = (bf16[2,2,256,512]{3,2,1,0:T(8,128)(2,1)}, bf16[2,2,256,512]{3,2,1,0:T(8,128)(2,1)S(1)}, u32[]{:S(2)}, u32[]{:S(2)}) collective-permute-start(bf16[2,2,256,512]{3,2,1,0:T(8,128)(2,1)} %get-tuple-element.350), channel_id=1, source_target_pairs={{0,8},{8,0},{16,24},{24,16},{1,9},{9,1},{17,25},{25,17},{2,10},{10... | collective-permute-start | bytes 3145736 | tf_op jit(solution)/shard_map/ppermute | solution.py:1112
  428.2 36.9 %collective-permute-start.54 = (bf16[2,2,256,512]{3,2,1,0:T(8,128)(2,1)}, bf16[2,2,256,512]{3,2,1,0:T(8,128)(2,1)S(1)}, u32[]{:S(2)}, u32[]{:S(2)}) collective-permute-start(bf16[2,2,256,512]{3,2,1,0:T(8,128)(2,1)} %get-tuple-element.351), channel_id=1, source_target_pairs={{0,16},{8,24},{16,0},{24,8},{1,17},{9,25},{17,1},{25,9},{2,18},{10... | collective-permute-start | bytes 3145736 | tf_op jit(solution)/shard_map/ppermute | solution.py:1115
  470.3 107.2 %reduce-scatter.15.cloned.1.call-start = ((), (), s32[]{:S(2)}) async-start(), calls=%async_computation.10 | async-start | bytes 1310720 | tf_op jit(solution)/shard_map/reduce_scatter | solution.py:1161
  475.4 39.6 %collective-permute-start.58 = (bf16[2,256,512]{2,1,0:T(8,128)(2,1)}, bf16[2,256,512]{2,1,0:T(8,128)(2,1)}, u32[]{:S(2)}, u32[]{:S(2)}) collective-permute-start(bf16[2,256,512]{2,1,0:T(8,128)(2,1)} %fusion.2), channel_id=1, source_target_pairs={{0,8},{8,0},{16,24},{24,16},{1,9},{9,1},{17,25},{25,17},{2,10},{10... | collective-permute-start | bytes 1572872 | tf_op jit(solution)/shard_map/ppermute | solution.py:1112
  478.5 36.5 %collective-permute-start.57 = (bf16[2,256,512]{2,1,0:T(8,128)(2,1)}, bf16[2,256,512]{2,1,0:T(8,128)(2,1)}, u32[]{:S(2)}, u32[]{:S(2)}) collective-permute-start(bf16[2,256,512]{2,1,0:T(8,128)(2,1)} %fusion.3), channel_id=1, source_target_pairs={{0,16},{8,24},{16,0},{24,8},{1,17},{9,25},{17,1},{25,9},{2,18},{10... | collective-permute-start | bytes 1572872 | tf_op jit(solution)/shard_map/ppermute | solution.py:1115
  519.9 59.5 %reduce-scatter.13.cloned.1.call-start = ((), (), s32[]{:S(2)}) async-start(), calls=%async_computation.9 | async-start | bytes 1310720 | tf_op jit(solution)/shard_map/reduce_scatter | solution.py:1161
  (185 other events, 2262.5 us)
Sparse Core Ops, SparseCore 0:
  20.3 30.4 all-gather.10
  52.9 28.1 all-gather.12
  83.3 31.5 all-gather.14
  116.9 52.3 all-gather.16
  170.6 78.8 all-gather.18
  306.5 75.8 reduce-scatter.6
  384.9 69.0 reduce-scatter.8
  456.3 28.6 reduce-scatter.10
  487.3 31.3 reduce-scatter.16
  521.0 25.8 reduce-scatter.14
  554.2 24.6 reduce-scatter.12
